TPU v7x, 32 devices: a whole 2x2x4 slice. The times are simulated.
32 devices in a mesh: fsdp: 2 (over core), ctx: 4 (over z), tp: 4 (over y, x).
Axes of the slice: x: 2, y: 2, z: 4, core: 2. Of those that a mesh axis runs over, the one named last changes fastest.
Arguments:
- hidden_in: bfloat16 [8, 256, 1536], P('fsdp', 'ctx'), may hold values from -6 to 6
- segment_ids: int32 [8, 256], P('fsdp', 'ctx'), may hold values from 0 to 5, as said below
- doc_starts: int32 [8, 4], P('fsdp', 'ctx'), may hold values from 0 to 129, as said below
- norm1_gain: bfloat16 [1536], P(('fsdp', 'ctx')), may hold values from 0.5 to 1.5
- w_query: bfloat16 [1536, 1536], P(('fsdp', 'ctx'), 'tp'), may hold values from -0.15625 to 0.15625
- w_key: bfloat16 [1536, 1536], P(('fsdp', 'ctx'), 'tp'), may hold values from -0.15625 to 0.15625
- w_value: bfloat16 [1536, 1536], P(('fsdp', 'ctx'), 'tp'), may hold values from -0.15625 to 0.15625
- w_house: bfloat16 [1536, 1536], P(('fsdp', 'ctx'), 'tp'), may hold values from -0.15625 to 0.15625
- w_beta: bfloat16 [1536, 12], P(('fsdp', 'ctx'), 'tp'), may hold values from -0.5 to 0.5
- w_out: bfloat16 [1536, 1536], P(('fsdp', 'ctx'), 'tp'), may hold values from -0.625 to 0.625
- norm2_gain: bfloat16 [1536], P(('fsdp', 'ctx')), may hold values from 0.5 to 1.5
- w_gate: bfloat16 [1536, 4096], P(('fsdp', 'ctx'), 'tp'), may hold values from -0.15625 to 0.15625
- w_up: bfloat16 [1536, 4096], P(('fsdp', 'ctx'), 'tp'), may hold values from -0.15625 to 0.15625
- w_down: bfloat16 [1536, 4096], P(('fsdp', 'ctx'), 'tp'), may hold values from -0.09375 to 0.09375
- output_grad: bfloat16 [8, 256, 1536], P('fsdp', 'ctx'), may hold values from -6 to 6
Outputs:
- block_out: bfloat16 [8, 256, 1536], P('fsdp', 'ctx')
- input_grad: bfloat16 [8, 256, 1536], P('fsdp', 'ctx')
- norm1_gain_grad: float32 [1536], P(('fsdp', 'ctx'))
- w_query_grad: float32 [1536, 1536], P(('fsdp', 'ctx'), 'tp')
- w_key_grad: float32 [1536, 1536], P(('fsdp', 'ctx'), 'tp')
- w_value_grad: float32 [1536, 1536], P(('fsdp', 'ctx'), 'tp')
- w_house_grad: float32 [1536, 1536], P(('fsdp', 'ctx'), 'tp')
- w_beta_grad: float32 [1536, 12], P(('fsdp', 'ctx'), 'tp')
- w_out_grad: float32 [1536, 1536], P(('fsdp', 'ctx'), 'tp')
- norm2_gain_grad: float32 [1536], P(('fsdp', 'ctx'))
- w_gate_grad: float32 [1536, 4096], P(('fsdp', 'ctx'), 'tp')
- w_up_grad: float32 [1536, 4096], P(('fsdp', 'ctx'), 'tp')
- w_down_grad: float32 [1536, 4096], P(('fsdp', 'ctx'), 'tp')
Inputs may be any that keep to these rules, and one draw needn't show every extreme that they name: `segment_ids`: ids never fall along a sequence; each sequence holds 6 documents, numbered in order from 0; the last document of each sequence begins one position after the first position of its second-to-last group and runs to the end. `doc_starts`: for group c of 64 positions, the position within the sequence where the document that holds position c * 64 begins, as given by segment_ids; it is at most c * 64.
All inputs are finite; a program needn't handle non-finite values.
Results may differ from a plain program's by a relative error of at most 0.02.
Values may be sent and summed in bfloat16 or wider, within the bound.
No kernel may reach another device: no remote copies, remote signals or barrier semaphores. Data moves between devices by JAX's collectives and lax.ppermute only.
A program may use at most 128 MiB of HBM per device.

v0:
```python
import functools
import math

import jax
import jax.numpy as jnp
from jax import lax
from jax.experimental import pallas as pl
from jax.experimental.pallas import tpu as pltpu
from jax.sharding import PartitionSpec as P

EPSILON = 1e-06
HIGHEST = lax.Precision.HIGHEST
NEGATIVE = -1e30


def passed_along(block, axis, distance):
    devices = range(lax.axis_size(axis))
    route = [(i - distance, i) for i in devices if i - distance in devices]
    return lax.ppermute(block, axis, route)


def group_algebra(queries, key_rows, house, betas):
    length = queries.shape[0]
    scaling = 1.0 / math.sqrt(queries.shape[1])
    row_index = lax.broadcasted_iota(jnp.int32, (length, length), 0)
    column_index = lax.broadcasted_iota(jnp.int32, (length, length), 1)
    strict_below = row_index > column_index
    house_gram = jnp.dot(house, house.T, precision=HIGHEST)
    system = jnp.where(strict_below, house_gram, 0.0) + jnp.diag(1.0 / betas)
    identity = jnp.eye(length, dtype=house.dtype)
    inverse = jax.scipy.linalg.solve_triangular(system, identity, lower=True)
    query_house = jnp.where(
        row_index >= column_index, jnp.dot(queries, house.T, precision=HIGHEST), 0.0
    )
    house_key = jnp.where(strict_below, jnp.dot(house, key_rows.T, precision=HIGHEST), 0.0)
    query_side = jnp.dot(query_house, inverse, precision=HIGHEST)
    key_side = jnp.dot(inverse, house_key, precision=HIGHEST)
    scores = (
        jnp.dot(queries, key_rows.T, precision=HIGHEST)
        - jnp.dot(query_side, house_key, precision=HIGHEST)
    ) * scaling
    query_bar = queries - jnp.dot(query_side, house, precision=HIGHEST)
    key_bar = key_rows - jnp.dot(key_side.T, house, precision=HIGHEST)
    inner = jnp.dot(inverse, house, precision=HIGHEST)
    factor = jnp.eye(house.shape[1], dtype=house.dtype) - jnp.dot(house.T, inner, precision=HIGHEST)
    return (scores, query_bar, key_bar, factor)


def local_map(queries, key_rows, house_raw, beta_logits):
    house = house_raw * lax.rsqrt(jnp.sum(house_raw * house_raw, axis=-1, keepdims=True) + EPSILON)
    betas = 2.0 * jax.nn.sigmoid(beta_logits)
    return jax.vmap(jax.vmap(group_algebra))(queries, key_rows, house, betas)


def doc_starts_local(segment_ids, group_first, first_position):
    length = segment_ids.shape[-1]
    previous = jnp.concatenate([segment_ids[..., :1], segment_ids[..., :-1]], axis=-1)
    offsets = lax.broadcasted_iota(jnp.int32, segment_ids.shape, segment_ids.ndim - 1)
    boundary = (offsets > 0) & (segment_ids != previous)
    marks = jnp.where(boundary, offsets + first_position, -1)
    row_index = lax.broadcasted_iota(jnp.int32, (length, length), 0)
    column_index = lax.broadcasted_iota(jnp.int32, (length, length), 1)
    seen = jnp.where(column_index <= row_index, marks[..., None, :], -1)
    return jnp.maximum(jnp.max(seen, axis=-1), group_first)


def norm_rows(values):
    factor = lax.rsqrt(jnp.mean(values * values, axis=-1, keepdims=True) + EPSILON)
    return (values * factor, factor)


def norm_back(gradient, normed, factor, norm_gain):
    scaled = gradient * norm_gain
    return factor * (scaled - normed * jnp.mean(scaled * normed, axis=-1, keepdims=True))


def split_heads(tensor, head_count):
    seq_count, length, total_width = tensor.shape
    return tensor.reshape(seq_count, length, head_count, total_width // head_count).transpose(
        0, 2, 1, 3
    )


def join_heads(tensor):
    seq_count, head_count, length, head_width = tensor.shape
    return tensor.transpose(0, 2, 1, 3).reshape(seq_count, length, head_count * head_width)


def project(inputs, weight):
    return jnp.einsum("scd,df->scf", inputs, weight, preferred_element_type=jnp.float32)


def project_back(gradient, weight):
    return jnp.einsum("scf,df->scd", gradient, weight, preferred_element_type=jnp.float32)


def weight_grad(inputs, gradient):
    return jnp.einsum("scd,scf->df", inputs, gradient, preferred_element_type=jnp.float32)


def cross_scores(query_rot, key_low, scaling):
    return (
        jnp.einsum("shqd,shkd->shqk", query_rot, key_low, preferred_element_type=jnp.float32)
        * scaling
    )


def weighted_values(weights, values_in):
    return jnp.einsum("shqk,shkd->shqd", weights, values_in, preferred_element_type=jnp.float32)


def ring_of_groups(
    hidden_in,
    segment_ids,
    doc_starts,
    norm1_gain,
    w_query,
    w_key,
    w_value,
    w_house,
    w_beta,
    w_out,
    norm2_gain,
    w_gate,
    w_up,
    w_down,
    output_grad,
):
    gathered = (
        lax.all_gather(norm1_gain, ("fsdp", "ctx"), axis=0, tiled=True),
        lax.all_gather(w_query, ("fsdp", "ctx"), axis=0, tiled=True),
        lax.all_gather(w_key, ("fsdp", "ctx"), axis=0, tiled=True),
        lax.all_gather(w_value, ("fsdp", "ctx"), axis=0, tiled=True),
        lax.all_gather(w_house, ("fsdp", "ctx"), axis=0, tiled=True),
        lax.all_gather(w_beta, ("fsdp", "ctx"), axis=0, tiled=True),
        lax.all_gather(w_out, ("fsdp", "ctx"), axis=0, tiled=True),
        lax.all_gather(norm2_gain, ("fsdp", "ctx"), axis=0, tiled=True),
        lax.all_gather(w_gate, ("fsdp", "ctx"), axis=0, tiled=True),
        lax.all_gather(w_up, ("fsdp", "ctx"), axis=0, tiled=True),
        lax.all_gather(w_down, ("fsdp", "ctx"), axis=0, tiled=True),
    )
    (
        gain_one,
        query_full,
        key_full,
        value_full,
        house_full,
        beta_full,
        out_full,
        gain_two,
        gate_full,
        up_full,
        down_full,
    ) = gathered
    gain_one_f = gain_one.astype(jnp.float32)
    gain_two_f = gain_two.astype(jnp.float32)
    head_count = beta_full.shape[1]
    length = hidden_in.shape[1]
    residual = hidden_in.astype(jnp.float32)
    normed_one, factor_one = norm_rows(residual)
    h_one = (normed_one * gain_one_f).astype(jnp.bfloat16)
    queries = split_heads(project(h_one, query_full), head_count)
    key_rows = split_heads(project(h_one, key_full), head_count)
    values_low = split_heads(project(h_one, value_full).astype(jnp.bfloat16), head_count)
    house_raw = split_heads(project(h_one, house_full), head_count)
    beta_logits = project(h_one, beta_full).transpose(0, 2, 1)
    (scores_local, query_bar, key_bar, factors), local_back = jax.vjp(
        local_map, queries, key_rows, house_raw, beta_logits
    )
    scaling = 1.0 / math.sqrt(queries.shape[-1])
    chain_index = lax.axis_index("ctx")
    hop_total = lax.axis_size("ctx") - 1
    first_position = chain_index * length
    starts = doc_starts_local(segment_ids, doc_starts, first_position)
    offsets = jnp.arange(length, dtype=jnp.int32)
    causal = (offsets[None, :] <= offsets[:, None])[None]
    local_mask = (causal & (offsets[None, None, :] + first_position >= starts[:, :, None]))[:, None]

    def hop_mask(distance):
        key_pos = (chain_index - distance) * length + offsets
        return (key_pos[None, None, :] >= starts[:, :, None])[:, None]

    masked_local = jnp.where(local_mask, scores_local, NEGATIVE)
    local_max = jnp.max(masked_local, axis=-1)
    local_sum = jnp.sum(jnp.exp(masked_local - local_max[..., None]), axis=-1)
    key_send = key_bar.astype(jnp.bfloat16)
    identity = jnp.broadcast_to(jnp.eye(factors.shape[-1], dtype=jnp.float32), factors.shape)
    stack_rot = jnp.zeros((hop_total,) + query_bar.shape, jnp.bfloat16)
    stack_factors = jnp.zeros((hop_total,) + factors.shape, jnp.float32)

    def rotate(hop_step, hop_keys, chain, run_max, run_sum):
        query_rot = jnp.einsum("shqa,shab->shqb", query_bar, chain, precision=HIGHEST).astype(
            jnp.bfloat16
        )
        masked = jnp.where(
            hop_mask(hop_step + 1), cross_scores(query_rot, hop_keys, scaling), NEGATIVE
        )
        new_max = jnp.maximum(run_max, jnp.max(masked, axis=-1))
        new_sum = run_sum * jnp.exp(run_max - new_max) + jnp.sum(
            jnp.exp(masked - new_max[..., None]), axis=-1
        )
        return (query_rot, new_max, new_sum)

    stack_keys = jnp.zeros((hop_total,) + key_send.shape, jnp.bfloat16)
    stack_values = jnp.zeros((hop_total,) + values_low.shape, jnp.bfloat16)

    def forward_hop(hop_step, loop_state):
        (
            send_keys,
            send_values,
            send_factor,
            kept_keys,
            kept_values,
            kept_rot,
            kept_factors,
            run_max,
            run_sum,
        ) = loop_state
        got_keys, got_values = passed_along((send_keys, send_values), "ctx", 1)
        got_factor = passed_along(send_factor.astype(jnp.bfloat16), "ctx", 1).astype(
            send_factor.dtype
        )
        query_rot, run_max, run_sum = rotate(hop_step, got_keys, got_factor, run_max, run_sum)
        kept_keys = lax.dynamic_update_index_in_dim(kept_keys, got_keys, hop_step, 0)
        kept_values = lax.dynamic_update_index_in_dim(kept_values, got_values, hop_step, 0)
        kept_rot = lax.dynamic_update_index_in_dim(kept_rot, query_rot, hop_step, 0)
        kept_factors = lax.dynamic_update_index_in_dim(kept_factors, got_factor, hop_step, 0)
        next_factor = jnp.einsum("shab,shbc->shac", factors, got_factor, precision=HIGHEST)
        return (
            got_keys,
            got_values,
            next_factor,
            kept_keys,
            kept_values,
            kept_rot,
            kept_factors,
            run_max,
            run_sum,
        )

    loop_state = lax.fori_loop(
        0,
        hop_total,
        forward_hop,
        (
            key_send,
            values_low,
            identity,
            stack_keys,
            stack_values,
            stack_rot,
            stack_factors,
            local_max,
            local_sum,
        ),
    )
    stack_keys, stack_values, stack_rot, stack_factors = (
        loop_state[3],
        loop_state[4],
        loop_state[5],
        loop_state[6],
    )
    run_max, run_sum = (loop_state[7], loop_state[8])

    def fetch(hop_step):
        return (
            lax.dynamic_index_in_dim(stack_keys, hop_step, 0, keepdims=False),
            lax.dynamic_index_in_dim(stack_values, hop_step, 0, keepdims=False),
        )

    log_total = run_max + jnp.log(run_sum)

    def recall(hop_step):
        hop_keys, hop_values = fetch(hop_step)
        hop_factor = lax.dynamic_index_in_dim(stack_factors, hop_step, 0, keepdims=False)
        query_rot = lax.dynamic_index_in_dim(stack_rot, hop_step, 0, keepdims=False)
        masked = jnp.where(
            hop_mask(hop_step + 1), cross_scores(query_rot, hop_keys, scaling), NEGATIVE
        )
        hop_probs = jnp.exp(masked - log_total[..., None])
        return (hop_keys, hop_values, hop_factor, query_rot, hop_probs)

    probs_local = jnp.exp(masked_local - log_total[..., None])
    probs_local_low = probs_local.astype(jnp.bfloat16)
    attn_acc = weighted_values(probs_local_low, values_low)
    attn_rest = weighted_values(
        (probs_local - probs_local_low.astype(jnp.float32)).astype(jnp.bfloat16), values_low
    )

    def value_hop(hop_step, running):
        total_low, total_rest = running
        hop_keys, hop_values, hop_factor, query_rot, hop_probs = recall(hop_step)
        hop_low = hop_probs.astype(jnp.bfloat16)
        total_low = total_low + weighted_values(hop_low, hop_values)
        total_rest = total_rest + weighted_values(
            (hop_probs - hop_low.astype(jnp.float32)).astype(jnp.bfloat16), hop_values
        )
        return (total_low, total_rest)

    attn_acc, attn_rest = lax.fori_loop(0, hop_total, value_hop, (attn_acc, attn_rest))
    attn_low = join_heads(attn_acc.astype(jnp.bfloat16))
    branch = lax.psum(project_back(attn_low, out_full), "tp")
    middle = residual + branch
    normed_two, factor_two = norm_rows(middle)
    h_two = (normed_two * gain_two_f).astype(jnp.bfloat16)
    gate_proj = project(h_two, gate_full)
    up_proj = project(h_two, up_full)
    gate_sigmoid = jax.nn.sigmoid(gate_proj)
    silu_gate = gate_proj * gate_sigmoid
    hidden_low = (silu_gate * up_proj).astype(jnp.bfloat16)
    mlp_out = lax.psum(project_back(hidden_low, down_full).astype(jnp.bfloat16), "tp").astype(
        jnp.float32
    )
    block_out = (middle + mlp_out).astype(jnp.bfloat16)
    down_grad = weight_grad(output_grad, hidden_low)
    d_hidden = project(output_grad, down_full)
    d_gate = (d_hidden * up_proj * gate_sigmoid * (1.0 + gate_proj * (1.0 - gate_sigmoid))).astype(
        jnp.bfloat16
    )
    d_up = (d_hidden * silu_gate).astype(jnp.bfloat16)
    gate_grad = weight_grad(h_two, d_gate)
    up_grad = weight_grad(h_two, d_up)
    d_two = lax.psum(project_back(d_gate, gate_full) + project_back(d_up, up_full), "tp")
    gain_two_grad = jnp.sum(d_two * normed_two, axis=(0, 1))
    d_middle = output_grad.astype(jnp.float32) + norm_back(
        d_two, normed_two, factor_two, gain_two_f
    )
    d_branch = d_middle.astype(jnp.bfloat16)
    out_grad = weight_grad(d_branch, attn_low)
    d_attn = split_heads(project(d_branch, out_full).astype(jnp.bfloat16), head_count)
    d_probs_local = jnp.einsum(
        "shqd,shkd->shqk", d_attn, values_low, preferred_element_type=jnp.float32
    )
    row_delta = jnp.sum(d_attn.astype(jnp.float32) * (attn_acc + attn_rest), axis=-1)
    zero_factor = jnp.zeros(factors.shape, jnp.float32)
    zero_bar = jnp.zeros(query_bar.shape, jnp.float32)

    def back_hop(back_step, loop_state):
        carry_keys, carry_values, carry_factor, d_bar, d_factors = loop_state
        hop_step = hop_total - 1 - back_step
        hop_keys, hop_values, hop_factor, query_rot, hop_probs = recall(hop_step)
        d_probs = jnp.einsum(
            "shqd,shkd->shqk", d_attn, hop_values, preferred_element_type=jnp.float32
        )
        d_cross = (hop_probs * (d_probs - row_delta[..., None])).astype(jnp.bfloat16)
        d_rot = (
            jnp.einsum("shqk,shkd->shqd", d_cross, hop_keys, preferred_element_type=jnp.float32)
            * scaling
        )
        d_bar = d_bar + jnp.einsum("shqb,shab->shqa", d_rot, hop_factor, precision=HIGHEST)
        factor_local = jnp.einsum("shqa,shqb->shab", query_bar, d_rot, precision=HIGHEST)
        keys_total = (
            carry_keys
            + jnp.einsum("shqk,shqd->shkd", d_cross, query_rot, preferred_element_type=jnp.float32)
            * scaling
        )
        values_total = carry_values + jnp.einsum(
            "shqk,shqd->shkd",
            hop_probs.astype(jnp.bfloat16),
            d_attn,
            preferred_element_type=jnp.float32,
        )
        factor_total = factor_local + jnp.einsum(
            "shba,shbc->shac", factors, carry_factor, precision=HIGHEST
        )
        d_factors = d_factors + jnp.einsum(
            "shac,shbc->shab", carry_factor, hop_factor, precision=HIGHEST
        )
        carry_keys, carry_values, carry_factor = (
            passed_along(keys_total.astype(jnp.bfloat16), "ctx", -1).astype(keys_total.dtype),
            passed_along(values_total.astype(jnp.bfloat16), "ctx", -1).astype(values_total.dtype),
            passed_along(factor_total.astype(jnp.bfloat16), "ctx", -1).astype(factor_total.dtype),
        )
        return (carry_keys, carry_values, carry_factor, d_bar, d_factors)

    zero_rows = jnp.zeros(key_send.shape, jnp.float32)
    loop_state = lax.fori_loop(
        0, hop_total, back_hop, (zero_rows, zero_rows, zero_factor, zero_bar, zero_factor)
    )
    carry_keys, carry_values, d_bar, d_factors = (
        loop_state[0],
        loop_state[1],
        loop_state[3],
        loop_state[4],
    )
    d_local = probs_local * (d_probs_local - row_delta[..., None])
    values_sum = carry_values + jnp.einsum(
        "shqk,shqd->shkd", probs_local_low, d_attn, preferred_element_type=jnp.float32
    )
    d_queries, d_keys, d_house, d_betas = local_back((d_local, d_bar, carry_keys, d_factors))
    query_low = join_heads(d_queries.astype(jnp.bfloat16))
    key_low = join_heads(d_keys.astype(jnp.bfloat16))
    value_low = join_heads(values_sum.astype(jnp.bfloat16))
    house_low = join_heads(d_house.astype(jnp.bfloat16))
    beta_low = d_betas.transpose(0, 2, 1).astype(jnp.bfloat16)
    query_grad = weight_grad(h_one, query_low)
    key_grad = weight_grad(h_one, key_low)
    value_grad = weight_grad(h_one, value_low)
    house_grad = weight_grad(h_one, house_low)
    beta_grad = weight_grad(h_one, beta_low)
    partial_one = (
        project_back(query_low, query_full)
        + project_back(key_low, key_full)
        + project_back(value_low, value_full)
    )
    partial_one = (
        partial_one + project_back(house_low, house_full) + project_back(beta_low, beta_full)
    )
    d_one = lax.psum(partial_one.astype(jnp.bfloat16), "tp").astype(jnp.float32)
    gain_one_grad = jnp.sum(d_one * normed_one, axis=(0, 1))
    input_grad = (d_middle + norm_back(d_one, normed_one, factor_one, gain_one_f)).astype(
        jnp.bfloat16
    )

    def scattered(partial):
        first = lax.psum_scatter(partial, "fsdp", scatter_dimension=0, tiled=True)
        return lax.psum_scatter(first, "ctx", scatter_dimension=0, tiled=True)

    results = tuple(
        (
            scattered(gain_one_grad.astype(jnp.bfloat16)).astype(jnp.float32),
            scattered(query_grad.astype(jnp.bfloat16)).astype(jnp.float32),
            scattered(key_grad.astype(jnp.bfloat16)).astype(jnp.float32),
            scattered(value_grad.astype(jnp.bfloat16)).astype(jnp.float32),
            scattered(house_grad.astype(jnp.bfloat16)).astype(jnp.float32),
            scattered(beta_grad.astype(jnp.bfloat16)).astype(jnp.float32),
            scattered(out_grad.astype(jnp.bfloat16)).astype(jnp.float32),
            scattered(gain_two_grad.astype(jnp.bfloat16)).astype(jnp.float32),
            scattered(gate_grad.astype(jnp.bfloat16)).astype(jnp.float32),
            scattered(up_grad.astype(jnp.bfloat16)).astype(jnp.float32),
            scattered(down_grad.astype(jnp.bfloat16)).astype(jnp.float32),
        )
    )
    return (block_out, input_grad) + results


def halves(value):
    high = value.astype(jnp.bfloat16)
    return high, (value - high.astype(jnp.float32)).astype(jnp.bfloat16)


AB = (((1,), (0,)), ((), ()))
ABT = (((1,), (1,)), ((), ()))
ATB = (((0,), (0,)), ((), ()))


def mm(a, b, dims=AB):
    return lax.dot_general(a, b, dims, preferred_element_type=jnp.float32)


def mm3(a, b, dims=AB):
    left, right = dims[0][0][0], dims[0][1][0]
    return mm(
        jnp.concatenate([a[0], a[1], a[0]], axis=left),
        jnp.concatenate([b[0], b[0], b[1]], axis=right),
        dims,
    )


def each(function, *lists):
    return [function(*values) for values in zip(*lists)]


def square_index(size):
    row = lax.broadcasted_iota(jnp.int32, (size, size), 0)
    return row, lax.broadcasted_iota(jnp.int32, (size, size), 1)


def unit_lower_inverses(strict):
    size = strict[0].shape[0]
    part, half = size // 4, size // 2
    lane = lax.broadcasted_iota(jnp.int32, (part, size), 1)
    row = lax.broadcasted_iota(jnp.int32, (part, size), 0)
    block = lane // part
    col = lane - block * part
    own = [block == b for b in range(4)]
    zero = jnp.zeros((part, size), jnp.bfloat16)

    def side_by_side(matrix, below):
        packed = jnp.zeros((part, size), jnp.float32)
        for b in range(4 - below):
            packed = jnp.where(own[b], matrix[(b + below) * part : (b + below + 1) * part], packed)
        return packed

    def stacked(pair, order=(0, 1, 2, 3)):
        return tuple(
            jnp.concatenate(
                [zero if b is None else jnp.where(own[b], value, zero) for b in order], axis=0
            )
            for value in pair
        )

    diagonal = [side_by_side(matrix, 0) for matrix in strict]
    inverse = [
        jnp.where(row == col, 1.0, 0.0) - jnp.where((row >> 1) == (col >> 1), matrix, 0.0)
        for matrix in diagonal
    ]
    level = 1
    while (1 << level) < part:
        joined = ((row >> (level + 1)) == (col >> (level + 1))) & ((row >> level) != (col >> level))
        pairs = each(halves, inverse)
        steps = [
            mm3(halves(jnp.where(joined, matrix, 0.0)), stacked(pair))
            for matrix, pair in zip(diagonal, pairs)
        ]
        inverse = [
            value - mm3(pair, stacked(halves(step)))
            for value, pair, step in zip(inverse, pairs, steps)
        ]
        level += 1
    pairs = each(halves, inverse)
    even = own[0] | own[2]
    steps = [
        mm3(halves(jnp.where(even, side_by_side(matrix, 1), 0.0)), stacked(pair))
        for matrix, pair in zip(strict, pairs)
    ]
    corners = [
        -mm3(pair, stacked(halves(step), (None, 0, None, 2))) for pair, step in zip(pairs, steps)
    ]

    def joined_block(value, corner, n):
        lanes = slice(n * half, (n + 1) * half)
        upper = jnp.where(own[2 * n], value, 0.0)[:, lanes]
        return jnp.concatenate([upper, jnp.where(own[2 * n], corner, value)[:, lanes]], axis=0)

    first = [joined_block(value, corner, 0) for value, corner in zip(inverse, corners)]
    last = [joined_block(value, corner, 1) for value, corner in zip(inverse, corners)]
    steps = [mm3(halves(matrix[half:, :half]), halves(value)) for matrix, value in zip(strict, first)]
    lower = [-mm3(halves(value), halves(step)) for value, step in zip(last, steps)]
    blank = jnp.zeros((half, half), jnp.float32)
    return [
        jnp.concatenate(
            [
                jnp.concatenate([top, blank], axis=1),
                jnp.concatenate([left, right], axis=1),
            ],
            axis=0,
        )
        for top, left, right in zip(first, lower, last)
    ]


def unit_rows(raw):
    norm = lax.rsqrt(jnp.sum(raw * raw, axis=1, keepdims=True) + EPSILON)
    return raw * norm, norm


def below(matrix, row, col):
    return jnp.where(row > col, matrix, 0.0)


def key_halves(house_raw, keys, betas):
    row, col = square_index(keys[0].shape[0])
    house = [unit_rows(raw)[0] for raw in house_raw]
    scaled = [halves(beta * value) for beta, value in zip(betas, house)]
    strict = [below(mm3(a, halves(b), ABT), row, col) for a, b in zip(scaled, house)]
    house_key = [halves(below(mm3(a, halves(b), ABT), row, col)) for a, b in zip(scaled, keys)]
    inverses = unit_lower_inverses(strict)
    return inverses, [mm3(halves(a), b) for a, b in zip(inverses, house_key)]


def query_halves(queries, values, house_raw, keys, inverses, key_side, allowed):
    row, col = square_index(keys[0].shape[0])
    scaling = 1.0 / math.sqrt(queries[0].shape[1])
    q = each(halves, queries)
    query_house = [
        halves(jnp.where(row >= col, mm3(a, halves(unit_rows(raw)[0]), ABT), 0.0))
        for a, raw in zip(q, house_raw)
    ]
    scores = [mm3(a, halves(b), ABT) for a, b in zip(q, keys)]
    scores = [score - mm3(a, halves(b)) for score, a, b in zip(scores, query_house, key_side)]
    masked = [jnp.where(allowed, score * scaling, NEGATIVE) for score in scores]
    weights = [jnp.exp(value - jnp.max(value, axis=1, keepdims=True)) for value in masked]
    probs = [value / jnp.sum(value, axis=1, keepdims=True) for value in weights]
    attn = [mm(prob.astype(jnp.bfloat16), value) for prob, value in zip(probs, values)]
    return attn, probs, [mm3(a, halves(b)) for a, b in zip(query_house, inverses)]


def heads_backward(queries, keys, house_raw, values, betas, probs, key_side, query_side, d_attn):
    row, col = square_index(keys[0].shape[0])
    scaling = 1.0 / math.sqrt(queries[0].shape[1])
    house, norm = zip(*[unit_rows(raw) for raw in house_raw])
    d_values = [mm(prob.astype(jnp.bfloat16), d, ATB) for prob, d in zip(probs, d_attn)]
    d_probs = [mm(d, value, ABT) for d, value in zip(d_attn, values)]
    d_scores = [
        halves(prob * (d - jnp.sum(prob * d, axis=1, keepdims=True)) * scaling)
        for prob, d in zip(probs, d_probs)
    ]
    q, k, w = each(halves, queries), each(halves, keys), each(halves, house)
    scaled = [halves(beta * value) for beta, value in zip(betas, house)]
    side = each(halves, query_side)
    d_side = [-mm3(d, halves(value), ABT) for d, value in zip(d_scores, key_side)]
    d_query_house = [halves(jnp.where(row >= col, d, 0.0)) for d in d_side]
    d_strict = [halves(below(-mm3(a, halves(d), ATB), row, col)) for a, d in zip(side, d_side)]
    d_house_key = [halves(below(-mm3(a, d, ATB), row, col)) for a, d in zip(side, d_scores)]
    d_queries = [mm3(d, a) + mm3(e, b) for d, a, e, b in zip(d_scores, k, d_query_house, w)]
    d_keys = [
        mm3(d, a, ATB) + mm3(e, b, ATB) for d, a, e, b in zip(d_scores, q, d_house_key, scaled)
    ]
    d_scaled = [mm3(d, a) + mm3(e, b) for d, a, e, b in zip(d_strict, w, d_house_key, k)]
    d_house = [
        mm3(d, a, ATB) + mm3(e, b, ATB) for d, a, e, b in zip(d_strict, scaled, d_query_house, q)
    ]
    d_betas = [jnp.sum(d * value, axis=1, keepdims=True) for d, value in zip(d_scaled, house)]
    d_house = [d + beta * e for d, beta, e in zip(d_house, betas, d_scaled)]
    d_house_raw = [
        n * (d - value * jnp.sum(d * value, axis=1, keepdims=True))
        for n, d, value in zip(norm, d_house, house)
    ]
    d_logits = [d * beta * (1.0 - 0.5 * beta) for d, beta in zip(d_betas, betas)]
    return d_queries, d_keys, d_house_raw, d_values, d_logits


def head_slices(ref, first, heads, head):
    return [ref[:, first + n * head : first + (n + 1) * head] for n in range(heads)]


def started(pairs, sems):
    copies = [
        pltpu.make_async_copy(source, target, sems.at[n]) for n, (source, target) in enumerate(pairs)
    ]
    for copy in copies:
        copy.start()
    return copies


def token_rows(places, n, k, quarter):
    return pl.ds(pl.multiple_of(places[8 + n] + places[18 + k], 16), quarter)


def placed(gathered, whole, places):
    quarter = gathered.shape[1] // 4
    return [
        (
            gathered.at[n, pl.ds(k * quarter, quarter)],
            whole.at[pl.ds(pl.multiple_of(places[18 + k] + n * quarter, 16), quarter)],
        )
        for n in range(4)
        for k in range(4)
    ]


def split_tokens(whole, parts, places):
    quarter = parts[0].shape[0] // 4
    for n in range(4):
        for k in range(4):
            parts[n][pl.ds(k * quarter, quarter)] = whole[token_rows(places, n, k, quarter)]


def wide_row(row, rows):
    return jnp.broadcast_to(row, (rows, row.shape[1])).astype(jnp.bfloat16)


def own_blocks(places, source, target, sequence=26, at=0):
    quarter = target.shape[-2]
    rows = pl.ds(pl.multiple_of(places[22], 16), quarter)
    return [(source.at[places[sequence + k], rows], target.at[k + at]) for k in range(4)]


def message_kernel(places, hidden_in, ids, gain_one, gain_two, *refs):
    messages, blocks, sems = refs[0:4], refs[4], refs[5]
    quarter, features = blocks.shape[1], blocks.shape[2]
    rows, depth = ids.shape[1], gain_one.shape[0]
    copies = started(own_blocks(places, hidden_in, blocks), sems)
    for k in range(4):
        messages[k][:, features:] = jnp.zeros((quarter, 640), jnp.bfloat16)
        own_ids = ids[pl.ds(places[26 + k], 1)].astype(jnp.float32)
        messages[k][:, features : features + rows] = wide_row(own_ids, quarter)
        at = features + 128
        messages[k][:, at : at + depth] = wide_row(gain_one[...].astype(jnp.float32)[None], quarter)
        at += 256
        messages[k][:, at : at + depth] = wide_row(gain_two[...].astype(jnp.float32)[None], quarter)
    for copy in copies:
        copy.wait()
    for k in range(4):
        messages[k][:, :features] = blocks[k]


def attention_pack_kernel(places, house, key, beta, query, value, out, first, second):
    for target, sources in ((first, (house, key, beta)), (second, (query, value, out))):
        at = 0
        for source in sources:
            width = source.shape[1]
            if width < 128:
                target[:, at : at + 128] = jnp.zeros((target.shape[0], 128), jnp.bfloat16)
            target[:, at : at + width] = source[...]
            at += width


def feed_forward_pack_kernel(places, output_grad, gate, up, down, *refs):
    messages, gives, keeps, blocks, sems = refs[0:4], refs[4:6], refs[6:8], refs[8], refs[9]
    copies = started(
        own_blocks(places, output_grad, blocks) + own_blocks(places, output_grad, blocks, 30, 4), sems
    )
    units = gate.shape[1] // 2
    part = units // 2
    for packs, start in ((keeps, places[23]), (gives, places[24])):
        for n in range(6):
            at = pl.ds(pl.multiple_of(start + n % 2 * part, 128), part)
            packs[n // 3][:, n % 3 * part : (n % 3 + 1) * part] = (gate, up, down)[n // 2][:, at]
    for copy in copies:
        copy.wait()
    for k in range(4):
        messages[k][0] = blocks[k]
        messages[k][1] = blocks[4 + k]


def out_message_kernel(places, *refs):
    out_parts, middle, messages = refs[0:4], refs[4], refs[5:9]
    quarter = middle.shape[0] // 4
    out = sum(part[...].astype(jnp.float32) for part in out_parts)
    own, pair = (middle[...] + out[0]).astype(jnp.bfloat16), out[1].astype(jnp.bfloat16)
    for k in range(4):
        messages[k][:quarter] = own[k * quarter : (k + 1) * quarter]
        messages[k][quarter:] = pair[(k ^ 2) * quarter : ((k ^ 2) + 1) * quarter]


def result_kernel(places, d_parts, d_middle, x, factor, gain, gain_two_grad, *messages):
    quarter, features = x.shape[0] // 4, x.shape[1]
    d_one = sum(d_parts[n].astype(jnp.float32) for n in range(4))
    normed = x[...] * factor[...]
    scaled = d_one * gain[...]
    mean = jnp.mean(scaled * normed, axis=1, keepdims=True)
    in_grad = (d_middle[...] + factor[...] * (scaled - normed * mean)).astype(jnp.bfloat16)
    gain_one_grad = jnp.sum(d_one * normed, axis=0, keepdims=True)
    row = lax.broadcasted_iota(jnp.int32, (quarter, 128), 0)
    for g, gains in enumerate((gain_one_grad, gain_two_grad[...])):
        packed = jnp.zeros((quarter, 128), jnp.float32)
        for n in range(features // 128):
            packed = jnp.where(row == n, gains[:, n * 128 : (n + 1) * 128], packed)
        at = features + g * 128
        for k in range(4):
            messages[k][:, at : at + 128] = packed.astype(jnp.bfloat16)
    for k in range(4):
        messages[k][:, :features] = in_grad[k * quarter : (k + 1) * quarter]


def spread_kernel(places, out_pieces, grad_pieces, out, grad, gains):
    quarter, features = out.shape[1] // 4, out.shape[2]
    for n in range(4):
        rows = slice(n * quarter, (n + 1) * quarter)
        for k in range(4):
            at = pl.ds(places[26 + k], 1)
            out[at, rows] = out_pieces[n, k * quarter : (k + 1) * quarter][None]
            grad[at, rows] = grad_pieces[n, k * quarter : (k + 1) * quarter, :features][None]
    gains[...] = sum(grad_pieces[n, :quarter, features:].astype(jnp.float32) for n in range(4))


def weights_in_place(pieces, whole, places, first=0, count=None):
    depth = pieces[0].shape[0]
    width = count or pieces[0].shape[1]
    return [
        (
            pieces[n].at[:, pl.ds(first, width)],
            whole.at[pl.ds(pl.multiple_of(places[n], 64), depth), pl.ds(0, width)],
        )
        for n in range(8)
    ]


def keys_kernel(heads, places, *refs):
    weights, xs, gain = refs[0:8], refs[8], refs[9]
    h_all, proj, inverses, key_side = refs[10:14]
    w_all, weight_sems, x_sems, x_all = refs[14:18]
    x_copies = started(placed(xs, x_all, places), x_sems)
    w_copies = started(weights_in_place(weights, w_all, places), weight_sems)
    for copy in x_copies:
        copy.wait()
    width = (proj.shape[1] - 128) // 2
    head = width // heads
    x = x_all[...].astype(jnp.float32)
    factor = lax.rsqrt(jnp.mean(x * x, axis=1, keepdims=True) + EPSILON)
    h_all[...] = (x * factor * gain[...]).astype(jnp.bfloat16)
    for copy in w_copies:
        copy.wait()
    proj[...] = mm(h_all[...], w_all[...])
    betas = 2.0 * jax.nn.sigmoid(proj[:, 2 * width :])
    results = key_halves(
        head_slices(proj, 0, heads, head),
        head_slices(proj, width, heads, head),
        [betas[:, n : n + 1] for n in range(heads)],
    )
    for n in range(heads):
        inverses[n], key_side[n] = results[0][n], results[1][n]


def queries_kernel(heads, places, *refs):
    weights, (h_all, proj_keys, inverses, key_side, id_row, id_col) = refs[0:8], refs[8:14]
    proj, attn, probs, query_side, parts = refs[14], refs[15], refs[16], refs[17], refs[18:22]
    w_all, total, sems = refs[22:25]
    for copy in started(weights_in_place(weights, w_all, places), sems):
        copy.wait()
    width = attn.shape[1]
    head = width // heads
    proj[...] = mm(h_all[...], w_all[:, : 2 * width])
    row, col = square_index(h_all.shape[0])
    results = query_halves(
        head_slices(proj, 0, heads, head),
        [value.astype(jnp.bfloat16) for value in head_slices(proj, width, heads, head)],
        head_slices(proj_keys, 0, heads, head),
        head_slices(proj_keys, width, heads, head),
        [inverses[n] for n in range(heads)],
        [key_side[n] for n in range(heads)],
        (col <= row) & (id_row[...] == id_col[...]),
    )
    for n in range(heads):
        attn[:, n * head : (n + 1) * head] = results[0][n].astype(jnp.bfloat16)
        probs[n], query_side[n] = results[1][n], results[2][n]
    total[...] = mm(attn[...], w_all[:, 2 * width :], ABT).astype(jnp.bfloat16)
    split_tokens(total, parts, places)


def feed_forward_kernel(places, *refs):
    weights, ins, grads = refs[0:16], refs[16:18], refs[18:22]
    two_parts, out_parts, keeps, sends = refs[22:30], refs[30:34], refs[34], refs[35]
    w_all, in_all, grad_all, total, weight_sems, in_sems, grad_sems = refs[36:43]
    rows, units, half = two_parts[0].shape[0], w_all.shape[1] // 3, w_all.shape[0] // 2

    def block(s, n):
        return pl.ds(pl.multiple_of(places[8 + n] * 4 + s * 4 * rows, 64), rows)

    depth, part = weights[0].shape[0], w_all.shape[1] // 2
    w_pairs = []
    for n in range(16):
        row = pl.ds(pl.multiple_of(places[n // 2], 64), depth)
        w_pairs.append((weights[n], w_all.at[row, pl.ds(n % 2 * part, part)]))
    w_copies = started(w_pairs, weight_sems)
    grad_copies = started(
        [
            (grads[n].at[s], grad_all.at[block(s, n)])
            for n in range(4)
            for s in range(2)
        ],
        grad_sems,
    )
    in_copies = started(
        [(ins[s].at[n], in_all.at[pl.ds((s * 4 + n) * rows, rows)]) for s in range(2) for n in range(4)],
        in_sems,
    )
    for copy in w_copies + grad_copies + in_copies:
        copy.wait()
    both = mm(in_all[...], w_all[:, : 2 * units])
    d_hidden = mm(grad_all[...], w_all[:, 2 * units :])
    gate, up = both[:, :units], both[:, units:]
    sigmoid = jax.nn.sigmoid(gate)
    silu = gate * sigmoid
    hidden = (silu * up).astype(jnp.bfloat16)
    d_gate = (d_hidden * up * sigmoid * (1.0 + gate * (1.0 - sigmoid))).astype(jnp.bfloat16)
    d_up = (d_hidden * silu).astype(jnp.bfloat16)
    for target in (keeps, sends):
        at = 2 * half
        for value in (d_gate, d_up, hidden):
            target[:, at : at + units] = value
            at += units
    d_both = keeps[:, 2 * half : 2 * half + 2 * units]
    total[...] = mm(d_both, w_all[:, : 2 * units], ABT).astype(jnp.bfloat16)
    for s in range(2):
        for n in range(4):
            two_parts[s * 4 + n][...] = total[block(s, n)]
    total[...] = mm(hidden, w_all[:, 2 * units :], ABT).astype(jnp.bfloat16)
    for s in range(2):
        for n in range(4):
            out_parts[n][s] = total[block(s, n)]
    for target, place in ((keeps, 12), (sends, 13)):
        lanes = pl.ds(pl.multiple_of(places[place], 128), half)
        target[:, :half] = in_all[:, lanes]
        target[:, half : 2 * half] = grad_all[:, lanes]


def attention_backward_kernel(heads, places, *refs):
    first, second, ds = refs[0:8], refs[8:16], refs[16]
    proj_keys, proj, probs, key_side, query_side, h_all, attn = refs[17:24]
    keeps, sends, parts = refs[24:27]
    w_first, w_second, d_all, d_attn, total, first_sems, second_sems, d_sems = refs[27:35]
    half, width = d_all.shape[1] // 2, d_attn.shape[1]
    d_keys_all = keeps.at[:, pl.ds(2 * half, 2 * width + 128)]
    d_queries_all = keeps.at[:, pl.ds(2 * half + 2 * width + 128, 2 * width)]
    second_copies = started(weights_in_place(second, w_second, places), second_sems)
    d_copies = started(placed(ds, d_all, places), d_sems)
    first_copies = started(weights_in_place(first, w_first, places), first_sems)
    for copy in d_copies + second_copies:
        copy.wait()
    head = width // heads
    d_attn[...] = mm(d_all[...], w_second[:, 2 * width :]).astype(jnp.bfloat16)
    betas = 2.0 * jax.nn.sigmoid(proj_keys[:, 2 * width :])
    lane = lax.broadcasted_iota(jnp.int32, betas.shape, 1)
    logits = jnp.zeros(betas.shape, jnp.float32)
    results = heads_backward(
        head_slices(proj, 0, heads, head),
        head_slices(proj_keys, width, heads, head),
        head_slices(proj_keys, 0, heads, head),
        [value.astype(jnp.bfloat16) for value in head_slices(proj, width, heads, head)],
        [betas[:, n : n + 1] for n in range(heads)],
        [probs[n] for n in range(heads)],
        [key_side[n] for n in range(heads)],
        [query_side[n] for n in range(heads)],
        head_slices(d_attn, 0, heads, head),
    )
    for n in range(heads):
        d_queries, d_keys, d_house, d_values, d_logit = [result[n] for result in results]
        low_at, high_at = slice(n * head, (n + 1) * head), slice(width + n * head, width + (n + 1) * head)
        d_keys_all[:, low_at] = d_house.astype(jnp.bfloat16)
        d_keys_all[:, high_at] = d_keys.astype(jnp.bfloat16)
        d_queries_all[:, low_at] = d_queries.astype(jnp.bfloat16)
        d_queries_all[:, high_at] = d_values.astype(jnp.bfloat16)
        logits = jnp.where(lane == n, d_logit, logits)
    d_keys_all[:, 2 * width :] = logits.astype(jnp.bfloat16)
    for copy in first_copies:
        copy.wait()
    keeps[:, keeps.shape[1] - width :] = attn[...]
    sends[:, 2 * half :] = keeps[:, 2 * half :]
    for target, place in ((keeps, 12), (sends, 13)):
        lanes = pl.ds(pl.multiple_of(places[place], 128), half)
        target[:, :half] = h_all[:, lanes]
        target[:, half : 2 * half] = d_all[:, lanes]
    total[...] = (
        mm(d_keys_all[...], w_first[...], ABT) + mm(d_queries_all[...], w_second[:, : 2 * width], ABT)
    ).astype(jnp.bfloat16)
    quarter = parts.shape[1] // 4
    for n in range(4):
        for k in range(4):
            rows = pl.ds(pl.multiple_of(places[18 + k] + n * quarter, 16), quarter)
            parts[n, k * quarter : (k + 1) * quarter] = total[rows]


def weight_grad_kernel(groups, places, mine, came, *refs):
    outs, total = refs[:-1], refs[-1]
    half, at = total.shape[0], 0
    for left, start, width in groups:
        lefts, rights = slice(left * half, (left + 1) * half), slice(start, start + width)
        total[:, at : at + width] = (
            mm(mine[:, lefts], mine[:, rights], ATB) + mm(came[:, lefts], came[:, rights], ATB)
        ).astype(jnp.bfloat16)
        at += width
    depth, at = outs[0].shape[1], 0
    for n in range(0, len(outs), 2):
        width = outs[n].shape[2]
        for k in range(4):
            rows = pl.ds(pl.multiple_of(places[14 + k], 64), depth)
            outs[n + k % 2][k // 2] = total[rows, at : at + width]
        at += width


VMEM_BYTES = 56 * 1024 * 1024


def call(kernel, outs, scratch, places, operands, spaces, micros, out_spaces=None):
    vmem = pl.BlockSpec(memory_space=pltpu.VMEM)
    kinds = {"v": vmem, "a": pl.BlockSpec(memory_space=pl.ANY)}
    return pl.pallas_call(
        kernel,
        out_shape=[jax.ShapeDtypeStruct(shape, kind) for shape, kind in outs],
        in_specs=[pl.BlockSpec(memory_space=pltpu.SMEM)] + [kinds[s] for s in spaces],
        out_specs=[kinds[s] for s in out_spaces or "v" * len(outs)],
        scratch_shapes=scratch,
        compiler_params=pltpu.CompilerParams(vmem_limit_bytes=VMEM_BYTES),
        cost_estimate=pl.CostEstimate(
            flops=int(micros * 1.1e9), transcendentals=0, bytes_accessed=int(micros * 3.6e6)
        ),
    )(places, *operands)


def swap(block, axis, distance):
    size = lax.axis_size(axis)
    return lax.ppermute(block, axis, [(i, i ^ distance) for i in range(size)])


def gathered_tp(block):
    return lax.all_gather(block, "tp", axis=0)


def all_tp(block):
    return [block] + [swap(block, "tp", n) for n in (1, 2, 3)]


def to_owners(messages):
    return [messages[0]] + [swap(messages[n], "ctx", n) for n in (1, 2, 3)]


def sum_tp(parts):
    return [parts[0]] + [swap(parts[n], "tp", n) for n in (1, 2, 3)]


def add_up(blocks):
    total = blocks[0].astype(jnp.float32)
    for block in blocks[1:]:
        total = total + block.astype(jnp.float32)
    return total


def other_core(block):
    return swap(block, "fsdp", 1)


def whole_sequences(
    hidden_in,
    segment_ids,
    doc_starts,
    norm1_gain,
    w_query,
    w_key,
    w_value,
    w_house,
    w_beta,
    w_out,
    norm2_gain,
    w_gate,
    w_up,
    w_down,
    output_grad,
):
    low, wide = jnp.bfloat16, jnp.float32
    core, chain, column = lax.axis_index("fsdp"), lax.axis_index("ctx"), lax.axis_index("tp")
    rows, features = hidden_in.shape[1], hidden_in.shape[2]
    depth, width, heads = w_query.shape[0], w_query.shape[1], w_beta.shape[1]
    length, half, quarter = 4 * rows, features // 2, rows // 4
    units, used = w_gate.shape[1] // 2, 4 * width + 128
    near = jnp.arange(4, dtype=jnp.int32)
    upper = (chain // 2).astype(jnp.int32)
    places = jnp.concatenate(
        [
            (core * 4 + (chain ^ near)) * depth,
            ((1 - core) * 4 + (chain ^ near)) * depth,
            (column ^ near) * quarter,
            jnp.stack([core, 1 - core]) * half,
            (chain ^ near) * depth,
            (chain ^ near) * rows,
            jnp.stack([column * quarter, upper * units, (1 - upper) * units, upper]),
            chain ^ near,
            chain ^ near ^ 2,
        ]
    ).astype(jnp.int32)
    step = lax.optimization_barrier
    block = pltpu.VMEM((4, quarter, features), low)
    token_messages = call(
        message_kernel,
        [((quarter, features + 640), low)] * 4,
        [block, pltpu.SemaphoreType.DMA((4,))],
        places,
        [hidden_in, segment_ids, norm1_gain, norm2_gain],
        "avvv",
        2,
    )
    first, second = call(
        attention_pack_kernel,
        [((depth, 2 * width + 128), low), ((depth, 3 * width), low)],
        [],
        places,
        [w_house, w_key, w_beta, w_query, w_value, w_out],
        "v" * 6,
        2,
    )
    packed = call(
        feed_forward_pack_kernel,
        [((2, quarter, features), low)] * 4
        + [((depth, 3 * units // 2), low)] * 4,
        [pltpu.VMEM((8, quarter, features), low), pltpu.SemaphoreType.DMA((8,))],
        places,
        [output_grad, w_gate, w_up, w_down],
        "avvv",
        3,
    )
    x_messages, first, second, grad_messages, gives, ffn_keeps = step(
        (to_owners(token_messages), first, second, packed[:4], packed[4:6], packed[6:8])
    )

    first_two, first_one = swap(first, "ctx", 2), swap(first, "ctx", 1)
    x_block = jnp.concatenate([message[:, :features] for message in x_messages])
    x_pieces = gathered_tp(x_block)
    info = jnp.stack([message[0, features:] for message in x_messages])
    chosen = near[:, None] == (near[None, :] ^ chain)
    info = jnp.sum(jnp.where(chosen[:, :, None], info[None].astype(wide), 0.0), axis=1)
    ids = info[:, :rows].reshape(length)
    gains = jnp.concatenate(
        [info[:, 128 : 128 + depth], info[:, 384 : 384 + depth]], axis=1
    ).astype(low)
    grad_messages = to_owners(grad_messages)
    first_two, first_one, x_pieces, first, gains, grad_messages, second = step(
        (first_two, first_one, x_pieces, first, gains, grad_messages, second)
    )

    first_three = swap(first_two, "ctx", 1)
    second_two = swap(second, "ctx", 2)
    grads = jnp.stack(
        [
            jnp.concatenate([message[0] for message in grad_messages]),
            jnp.concatenate([grad_messages[n ^ 2][1] for n in range(4)]),
        ]
    )
    own_grad = grads[0]
    grad_pieces = all_tp(grads)
    first_three, first_two, first_one, second_two, gains, second, grad_pieces, gives = step(
        (first_three, first_two, first_one, second_two, gains, second, grad_pieces, gives)
    )

    key_weights = [first, first_one, first_two, first_three]
    key_weights = key_weights + [other_core(piece) for piece in key_weights]
    gains_other = other_core(gains)
    gains = jnp.where(core == 0, jnp.stack([gains, gains_other]), jnp.stack([gains_other, gains]))
    gain_one = gains[:, :, :depth].reshape(1, features).astype(wide)
    gain_two = gains[:, :, depth:].reshape(1, features).astype(wide)
    second_one = swap(second, "ctx", 1)
    give_two = [swap(gives[0], "ctx", 2)]
    square = ((heads, length, length), wide)
    h_all, proj_keys, inverses, key_side = call(
        functools.partial(keys_kernel, heads),
        [((length, features), low), ((length, 2 * width + 128), wide), square, square],
        [
            pltpu.VMEM((features, 2 * width + 128), low),
            pltpu.SemaphoreType.DMA((8,)),
            pltpu.SemaphoreType.DMA((16,)),
            pltpu.VMEM((length, features), low),
        ],
        places,
        [*key_weights, x_pieces, gain_one],
        "a" * 9 + "v",
        20,
    )
    second_two, second_one, give_two, give_last, proj_keys, second = step(
        (second_two, second_one, give_two, gives[1], proj_keys, second)
    )
    second_three = swap(second_two, "ctx", 1)
    second_others = [other_core(piece) for piece in (second, second_one, second_two)]
    give_two = give_two + [swap(give_last, "ctx", 2)]
    second_three, second_others, proj_keys, give_two, ffn_keeps = step(
        (second_three, second_others, proj_keys, give_two, ffn_keeps)
    )
    query_weights = [
        second, second_one, second_two, second_three, *second_others, other_core(second_three)
    ]

    keep_one, give_three = [swap(ffn_keeps[0], "ctx", 1)], [swap(give_two[0], "ctx", 1)]
    outs = call(
        functools.partial(queries_kernel, heads),
        [((length, 2 * width), wide), ((length, width), low), square, square]
        + [((rows, features), low)] * 4,
        [
            pltpu.VMEM((features, 3 * width), low),
            pltpu.VMEM((length, features), low),
            pltpu.SemaphoreType.DMA((8,)),
        ],
        places,
        [*query_weights, h_all, proj_keys, inverses, key_side, ids[None, :], ids[:, None]],
        "a" * 8 + "v" * 6,
        9,
    )
    proj, attn, probs, query_side = outs[:4]
    give_two, branch_parts, keep_one, give_three, ffn_keeps = step(
        (give_two, outs[4:], keep_one, give_three, ffn_keeps)
    )
    keep_one = keep_one + [swap(ffn_keeps[1], "ctx", 1)]
    give_three = give_three + [swap(give_two[1], "ctx", 1)]
    residual = x_block.astype(wide)
    normed_one, factor_one = norm_rows(residual)
    middle = residual + add_up(sum_tp(branch_parts))
    normed_two, factor_two = norm_rows(middle)
    h_two = (normed_two * gain_two).astype(low)
    give_two, give_three, keep_one, h_two = step((give_two, give_three, keep_one, h_two))

    h_pair = swap(h_two, "ctx", 2)
    h_own = gathered_tp(h_two)
    h_pair, give_three, h_own, keep_one, give_two = step(
        (h_pair, give_three, h_own, keep_one, give_two)
    )
    ffn_weights = [*ffn_keeps, *keep_one, *give_two, *give_three]
    ffn_weights = ffn_weights + [other_core(piece) for piece in ffn_weights]
    h_pair = gathered_tp(h_pair)

    tokens = 2 * length
    pair = ((2, rows, features), low)
    outs = call(
        feed_forward_kernel,
        [((rows, features), low)] * 8 + [pair] * 4 + [((tokens, features + 3 * units), low)] * 2,
        [
            pltpu.VMEM((features, 3 * units), low),
            pltpu.VMEM((tokens, features), low),
            pltpu.VMEM((tokens, features), low),
            pltpu.VMEM((tokens, features), low),
            pltpu.SemaphoreType.DMA((16,)),
            pltpu.SemaphoreType.DMA((8,)),
            pltpu.SemaphoreType.DMA((8,)),
        ],
        places,
        [*ffn_weights, h_own, h_pair, *grad_pieces],
        "a" * 22,
        12,
    )
    own_parts, pair_parts, out_parts, keeps, sends = outs[:4], outs[4:8], outs[8:12], outs[12], outs[13]

    def grads_of(mine, came, groups, pieces=1):
        total = sum(group[2] for group in groups)
        return call(
            functools.partial(weight_grad_kernel, groups),
            [((2, depth, total // pieces), low)] * (2 * pieces),
            [pltpu.VMEM((half, total), low)],
            places,
            [mine, came],
            "vv",
            total / 400.0,
        )

    pair_sum = add_up(sum_tp(pair_parts)).astype(low)
    came, pair_sum, own_parts = step((other_core(sends), pair_sum, own_parts))

    two_other = swap(pair_sum, "ctx", 2)
    own_sum = add_up(sum_tp(own_parts))
    ffn_grads = grads_of(
        keeps, came, ((0, features, 2 * units), (1, features + 2 * units, units)), 2
    )
    d_two = own_sum + two_other.astype(wide)
    gain_two_grad = jnp.sum(d_two * normed_two, axis=0)
    d_middle = own_grad.astype(wide) + norm_back(d_two, normed_two, factor_two, gain_two)
    d_low, ffn_grads = step((d_middle.astype(low), tuple(ffn_grads)))

    ffn_came = [swap(ffn_grads[1], "ctx", 1)]
    d_pieces = gathered_tp(d_low)
    ffn_sums = [add_up([ffn_grads[0], ffn_came[0]])]
    ffn_leave = ffn_sums[0][1].astype(low)
    d_pieces, out_parts, ffn_leave, ffn_far = step((d_pieces, out_parts, ffn_leave, ffn_grads[3]))

    ffn_other = [swap(ffn_leave, "ctx", 2)]
    ffn_came = ffn_came + [swap(ffn_far, "ctx", 1)]
    out_received = sum_tp(out_parts)
    back = call(
        functools.partial(attention_backward_kernel, heads),
        [((length, features + used + width), low)] * 2 + [((4, rows, features), low)],
        [
            pltpu.VMEM((features, 2 * width + 128), low),
            pltpu.VMEM((features, 3 * width), low),
            pltpu.VMEM((length, features), low),
            pltpu.VMEM((length, width), low),
            pltpu.VMEM((length, features), low),
            pltpu.SemaphoreType.DMA((8,)),
            pltpu.SemaphoreType.DMA((8,)),
            pltpu.SemaphoreType.DMA((16,)),
        ],
        places,
        [*key_weights, *query_weights, d_pieces, proj_keys, proj, probs, key_side, query_side, h_all, attn],
        "a" * 17 + "v" * 7,
        14,
    )
    ffn_sums = ffn_sums + [add_up([ffn_grads[2], ffn_came[1]])]
    ffn_leave, ffn_other, out_received, (keeps, sends, d_parts) = step(
        (ffn_sums[1][1].astype(low), ffn_other, out_received, tuple(back))
    )

    came, keeps, d_parts = step((other_core(sends), keeps, d_parts))

    query_start = features + 2 * width + 128
    near_two, far_two = grads_of(
        keeps, came, ((0, query_start, 2 * width), (1, query_start + 2 * width, width))
    )
    two_came = swap(far_two, "ctx", 1)
    ffn_other = ffn_other + [swap(ffn_leave, "ctx", 2)]
    near_one, far_one = grads_of(keeps, came, ((0, features, 2 * width + 128),))
    out_messages = call(
        out_message_kernel,
        [((2 * quarter, features), low)] * 4,
        [],
        places,
        [*out_received, middle],
        "v" * 5,
        2,
    )
    out_messages = to_owners(out_messages)
    d_received = lax.all_to_all(d_parts, "tp", 0, 0)
    messages = call(
        result_kernel,
        [((quarter, features + 256), low)] * 4,
        [],
        places,
        [d_received, d_middle, residual, factor_one, gain_one, gain_two_grad[None]],
        "v" * 6,
        3,
    )
    two_sum = add_up([near_two, two_came])
    ffn_other, two_leave, near_one, far_one, messages, out_messages = step(
        (ffn_other, two_sum[1].astype(low), near_one, far_one, tuple(messages), out_messages)
    )

    one_came = swap(far_one, "ctx", 1)
    query_other = swap(two_leave, "ctx", 2)
    messages, out_messages = step((to_owners(messages), out_messages))
    out_block = jnp.concatenate(
        [add_up([out_messages[n][:quarter], out_messages[n ^ 2][quarter:]]) for n in range(4)]
    ).astype(low)
    out_pieces = gathered_tp(out_block)
    owned = jnp.concatenate(
        [message[:, :features] for message in messages]
    )
    gain_sum = add_up([message[:, features:] for message in messages]).astype(low)
    owned = jnp.concatenate([owned, jnp.pad(gain_sum, ((0, 3 * quarter), (0, 0)))], axis=1)
    one_sum = add_up([near_one, one_came])
    one_leave, owned, query_other, out_pieces = step(
        (one_sum[1].astype(low), owned, query_other, out_pieces)
    )

    key_other = swap(one_leave, "ctx", 2)
    block_out, input_grad, gain_total = call(
        spread_kernel,
        [((4, rows, features), low)] * 2 + [((quarter, 256), wide)],
        [],
        places,
        [out_pieces, gathered_tp(owned)],
        "vv",
        3,
    )
    gain_total = gain_total + other_core(gain_total)
    gain_total = jnp.concatenate(
        [gain_total[: features // 128, :128], gain_total[: features // 128, 128:]]
    ).reshape(2, features)
    gain_total = lax.dynamic_slice_in_dim(gain_total, (core * 4 + chain) * depth, depth, axis=1)
    query_grads = two_sum[0] + query_other.astype(wide)
    key_grads = one_sum[0] + key_other.astype(wide)

    ffn_kept = jnp.concatenate([total[0] for total in ffn_sums], axis=1)
    ffn_other = jnp.concatenate(ffn_other, axis=1).astype(wide)

    def ffn_result(n):
        kept = ffn_kept[:, n * units : (n + 1) * units]
        came = ffn_other[:, n * units : (n + 1) * units]
        return jnp.concatenate(
            [jnp.where(upper == 1, came, kept), jnp.where(upper == 1, kept, came)], axis=1
        )

    return (
        block_out,
        input_grad,
        gain_total[0],
        query_grads[:, :width],
        key_grads[:, width : 2 * width],
        query_grads[:, width : 2 * width],
        key_grads[:, :width],
        key_grads[:, 2 * width : 2 * width + heads],
        query_grads[:, 2 * width :],
        gain_total[1],
        ffn_result(0),
        ffn_result(1),
        ffn_result(2),
    )


def shards(*args):
    sizes = [lax.axis_size(axis) for axis in ("fsdp", "ctx", "tp")]
    if sizes == [2, 4, 4] and args[0].shape[:2] == (4, 64):
        return whole_sequences(*args)
    return ring_of_groups(*args)


def solution(mesh):
    in_specs = (
        P("fsdp", "ctx", None),
        P("fsdp", "ctx"),
        P("fsdp", "ctx"),
        P(("fsdp", "ctx")),
        P(("fsdp", "ctx"), "tp"),
        P(("fsdp", "ctx"), "tp"),
        P(("fsdp", "ctx"), "tp"),
        P(("fsdp", "ctx"), "tp"),
        P(("fsdp", "ctx"), "tp"),
        P(("fsdp", "ctx"), "tp"),
        P(("fsdp", "ctx")),
        P(("fsdp", "ctx"), "tp"),
        P(("fsdp", "ctx"), "tp"),
        P(("fsdp", "ctx"), "tp"),
        P("fsdp", "ctx", None),
    )
    out_specs = (
        P("fsdp", "ctx", None),
        P("fsdp", "ctx", None),
        P(("fsdp", "ctx")),
        P(("fsdp", "ctx"), "tp"),
        P(("fsdp", "ctx"), "tp"),
        P(("fsdp", "ctx"), "tp"),
        P(("fsdp", "ctx"), "tp"),
        P(("fsdp", "ctx"), "tp"),
        P(("fsdp", "ctx"), "tp"),
        P(("fsdp", "ctx")),
        P(("fsdp", "ctx"), "tp"),
        P(("fsdp", "ctx"), "tp"),
        P(("fsdp", "ctx"), "tp"),
    )
    return jax.shard_map(shards, mesh=mesh, in_specs=in_specs, out_specs=out_specs, check_vma=False)
```

profile of v0, /device:TPU:0, one launch (start us, length us, event | category | flops | bytes accessed | tf_op | source)
XLA Modules:
  0.0 353.3 jit_solution(7337347499003589526)
XLA Ops:
  1.4 2.4 shard_map.237
  3.8 3.1 collective-permute-start
  6.9 2.6 collective-permute-start.1
  10.3 3.5 shard_map.239
  13.7 2.2 shard_map.238
  16.1 2.0 collective-permute-start.3
  18.1 2.5 collective-permute-start.4
  20.7 11.8 %all-gather = bf16[256,1536]{1,0:T(8,128)(2,1)} all-gather(bf16[64,1536]{1,0:T(8,128)(2,1)S(1)} %get-tuple-element.454), channel_id=2, replica_groups=mesh['fsdp'=2,'ctx'=4,'tp'=4] {'tp'}, dimensions={0}, use_global_device_ids=true | all-gather | bytes 983040 | tf_op jit(solution)/shard_map/all_gather | solution.py:969
  33.5 3.6 %collective-permute-start.7 = (bf16[2,16,1536]{2,1,0:T(8,128)(2,1)S(1)}, bf16[2,16,1536]{2,1,0:T(8,128)(2,1)S(1)}, u32[]{:S(2)}, u32[]{:S(2)}) collective-permute-start(bf16[2,16,1536]{2,1,0:T(8,128)(2,1)S(1)} %copy-done.52), channel_id=1, source_target_pairs={{0,12},{4,8},{8,4},{12,0},{1,13},{5,9},{9,5},{13,1},{2,14},{6,10},... | collective-permute-start | bytes 294920 | tf_op jit(solution)/shard_map/ppermute | solution.py:965
  37.4 4.1 %collective-permute-done.6 = bf16[2,16,1536]{2,1,0:T(8,128)(2,1)S(1)} collective-permute-done((bf16[2,16,1536]{2,1,0:T(8,128)(2,1)S(1)}, bf16[2,16,1536]{2,1,0:T(8,128)(2,1)S(1)}, u32[]{:S(2)}, u32[]{:S(2)}) %collective-permute-start.6) | collective-permute-done | bytes 98336 | tf_op jit(solution)/shard_map/ppermute | solution.py:965
  41.6 2.5 collective-permute-start.9
  44.3 1.5 collective-permute-start.10
  45.8 1.5 collective-permute-start.11
  48.2 17.2 %collective-permute-done.8.refs_3_ = bf16[192,896]{1,0:T(8,128)(2,1)} collective-permute-done((bf16[192,896]{1,0:T(8,128)(2,1)}, bf16[192,896]{1,0:T(8,128)(2,1)}, u32[]{:S(2)}, u32[]{:S(2)}) %collective-permute-start.8) | collective-permute-done | bytes 344096 | tf_op jit(solution)/shard_map/ppermute | solution.py:965
  66.7 1.4 collective-permute-done.19
  69.0 9.3 %shard_map.240 = (bf16[256,1536]{1,0:T(8,128)(2,1)}, f32[256,896]{1,0:T(8,128)}, f32[3,256,256]{2,1,0:T(8,128)}, f32[3,256,256]{2,1,0:T(8,128)}) custom-call(s32[34]{0:T(128)} %concatenate.63.places, bf16[192,896]{1,0:T(8,128)(2,1)} %get-tuple-element.244.refs_0_, bf16[192,896]{1,0:T(8,128)(2,1)} %collective-permute-done.4.refs_1_, ...), custom_call_target="tpu_custom_call" | custom-call | flops 22000001024 | bytes 72000000 | tf_op jit(solution)/shard_map/pallas_call | solution.py:950
  78.3 7.3 %collective-permute-done.14.refs_4_ = bf16[192,768]{1,0:T(8,128)(2,1)} collective-permute-done((bf16[192,768]{1,0:T(8,128)(2,1)}, bf16[192,768]{1,0:T(8,128)(2,1)}, u32[]{:S(2)}, u32[]{:S(2)}) %collective-permute-start.14) | collective-permute-done | bytes 294944 | tf_op jit(solution)/shard_map/ppermute | solution.py:965
  87.2 1.4 collective-permute-start.24
  88.6 13.6 %collective-permute-done.24.refs_5_ = bf16[192,768]{1,0:T(8,128)(2,1)} collective-permute-done((bf16[192,768]{1,0:T(8,128)(2,1)S(1)}, bf16[192,768]{1,0:T(8,128)(2,1)}, u32[]{:S(2)}, u32[]{:S(2)}) %collective-permute-start.24) | collective-permute-done | bytes 294944 | tf_op jit(solution)/shard_map/ppermute | solution.py:965
  102.2 2.1 collective-permute-done.20.refs_3_.refs_11_
  107.4 1.7 collective-permute-start.26
  110.2 7.8 %shard_map.241 = (f32[256,768]{1,0:T(8,128)}, bf16[256,384]{1,0:T(8,128)(2,1)}, f32[3,256,256]{2,1,0:T(8,128)}, f32[3,256,256]{2,1,0:T(8,128)}, bf16[64,1536]{1,...) custom-call(s32[34]{0:T(128)} %concatenate.63.places, ...), custom_call_target="tpu_custom_call" | custom-call | flops 9900000256 | bytes 32400000 | tf_op jit(solution)/shard_map/pallas_call | solution.py:950
  118.0 5.1 %collective-permute-done.27.refs_6_ = bf16[192,768]{1,0:T(8,128)(2,1)S(1)} collective-permute-done((bf16[192,768]{1,0:T(8,128)(2,1)}, bf16[192,768]{1,0:T(8,128)(2,1)S(1)}, u32[]{:S(2)}, u32[]{:S(2)}) %collective-permute-start.27) | collective-permute-done | bytes 294944 | tf_op jit(solution)/shard_map/ppermute | solution.py:965
  123.8 1.4 collective-permute-start.28
  125.3 1.7 collective-permute-start.29
  127.4 1.8 collective-permute-start.31
  129.4 2.4 collective-permute-done.28
  131.8 4.1 %collective-permute-done.29 = bf16[64,1536]{1,0:T(8,128)(2,1)S(1)} collective-permute-done((bf16[64,1536]{1,0:T(8,128)(2,1)}, bf16[64,1536]{1,0:T(8,128)(2,1)S(1)}, u32[]{:S(2)}, u32[]{:S(2)}) %collective-permute-start.29) | collective-permute-done | bytes 196640 | tf_op jit(solution)/shard_map/ppermute | solution.py:965
  135.9 1.2 multiply_reduce_fusion.3
  137.6 4.2 %collective-permute-done.32.refs_3_ = bf16[192,768]{1,0:T(8,128)(2,1)S(1)} collective-permute-done((bf16[192,768]{1,0:T(8,128)(2,1)S(1)}, bf16[192,768]{1,0:T(8,128)(2,1)S(1)}, u32[]{:S(2)}, u32[]{:S(2)}) %collective-permute-start.32) | collective-permute-done | bytes 294944 | tf_op jit(solution)/shard_map/ppermute | solution.py:965
  141.7 1.4 collective-permute-start.33
  143.7 13.2 %all-gather.1 = bf16[256,1536]{1,0:T(8,128)(2,1)} all-gather(bf16[64,1536]{1,0:T(8,128)(2,1)S(1)} %multiply_convert_fusion), channel_id=3, replica_groups=mesh['fsdp'=2,'ctx'=4,'tp'=4] {'tp'}, dimensions={0}, use_global_device_ids=true | all-gather | bytes 983040 | tf_op jit(solution)/shard_map/all_gather | solution.py:969
  158.7 12.9 %all-gather.2 = bf16[256,1536]{1,0:T(8,128)(2,1)} all-gather(bf16[64,1536]{1,0:T(8,128)(2,1)S(1)} %collective-permute-done.33), channel_id=4, replica_groups=mesh['fsdp'=2,'ctx'=4,'tp'=4] {'tp'}, dimensions={0}, use_global_device_ids=true | all-gather | bytes 983040 | tf_op jit(solution)/shard_map/all_gather | solution.py:969
  172.7 12.7 %shard_map.242 = (bf16[64,1536]{1,0:T(8,128)(2,1)}, bf16[64,1536]{1,0:T(8,128)(2,1)}, bf16[64,1536]{1,0:T(8,128)(2,1)}, bf16[64,1536]{1,0:T(8,128)(2,1)}, bf16[6...) custom-call(s32[34]{0:T(128)} %concatenate.63.places, ...), custom_call_target="tpu_custom_call" | custom-call | flops 13200000000 | bytes 43200000 | tf_op jit(solution)/shard_map/pallas_call | solution.py:950
  187.6 1.5 collective-permute-start.45
  189.1 4.4 %collective-permute-done.43 = bf16[64,1536]{1,0:T(8,128)(2,1)S(1)} collective-permute-done((bf16[64,1536]{1,0:T(8,128)(2,1)}, bf16[64,1536]{1,0:T(8,128)(2,1)S(1)}, u32[]{:S(2)}, u32[]{:S(2)}) %collective-permute-start.43) | collective-permute-done | bytes 196640 | tf_op jit(solution)/shard_map/ppermute | solution.py:965
  193.5 4.4 %collective-permute-done.44 = bf16[64,1536]{1,0:T(8,128)(2,1)S(1)} collective-permute-done((bf16[64,1536]{1,0:T(8,128)(2,1)}, bf16[64,1536]{1,0:T(8,128)(2,1)S(1)}, u32[]{:S(2)}, u32[]{:S(2)}) %collective-permute-start.44) | collective-permute-done | bytes 196640 | tf_op jit(solution)/shard_map/ppermute | solution.py:965
  198.9 1.7 copy-done.13
  202.6 1.5 collective-permute-start.48
  204.1 1.5 collective-permute-start.49
  205.6 7.0 %shard_map.243 = (bf16[2,192,768]{2,1,0:T(8,128)(2,1)}, bf16[2,192,768]{2,1,0:T(8,128)(2,1)}, bf16[2,192,768]{2,1,0:T(8,128)(2,1)}, bf16[2,192,768]{2,1,0:T(8,128)(2,1)}) custom-call(s32[34]{0:T(128)} %concatenate.63.places, bf16[512,3072]{1,0:T(8,128)(2,1)} %get-tuple-element.318.mine, bf16[512,3072]{1,0:T(8,128)(2,1)} %copy-done.13), custom_call_target="tpu_custom_call" | custom-call | flops 4224000000 | bytes 13824000 | tf_op jit(solution)/shard_map/pallas_call | solution.py:950
  212.6 2.0 collective-permute-done.49
  215.8 11.5 %all-gather.3 = bf16[256,1536]{1,0:T(8,128)(2,1)} all-gather(bf16[64,1536]{1,0:T(8,128)(2,1)S(1)} %get-tuple-element.325), channel_id=5, replica_groups=mesh['fsdp'=2,'ctx'=4,'tp'=4] {'tp'}, dimensions={0}, use_global_device_ids=true | all-gather | bytes 983040 | tf_op jit(solution)/shard_map/all_gather | solution.py:969
  227.4 2.6 collective-permute-done.50
  232.8 1.4 collective-permute-start.55
  234.2 3.4 collective-permute-start.52
  237.6 14.2 %shard_map.244 = (bf16[256,3584]{1,0:T(8,128)(2,1)}, bf16[256,3584]{1,0:T(8,128)(2,1)}, bf16[4,64,1536]{2,1,0:T(8,128)(2,1)}) custom-call(s32[34]{0:T(128)} %concatenate.63.places, bf16[192,896]{1,0:T(8,128)(2,1)} %get-tuple-element.244.refs_0_, bf16[192,896]{1,0:T(8,128)(2,1)} %collective-permute-done.4.refs_1_, ...), custom_call_target="tpu_custom_call" | custom-call | flops 15399999488 | bytes 50400000 | tf_op jit(solution)/shard_map/pallas_call | solution.py:950
  255.7 2.0 collective-permute-done.57.came
  257.7 4.5 %all-to-all-start = ((bf16[4,64,1536]{2,1,0:T(8,128)(2,1)}), bf16[4,64,1536]{2,1,0:T(8,128)(2,1)}, u32[]{:S(2)}, u32[]{:S(2)}) async-start(bf16[4,64,1536]{2,1,0:T(8,128)(2,1)} %get-tuple-element.358), calls=%async_computation | async-start | bytes 1572864 | tf_op jit(solution)/shard_map/all_to_all | solution.py:1266
  262.1 4.6 %shard_map.245 = (bf16[2,192,1152]{2,1,0:T(8,128)(2,1)}, bf16[2,192,1152]{2,1,0:T(8,128)(2,1)}) custom-call(s32[34]{0:T(128)} %concatenate.63.places, bf16[256,3584]{1,0:T(8,128)(2,1)} %get-tuple-element.352.mine, bf16[256,3584]{1,0:T(8,128)(2,1)} %collective-permute-done.57.came), custom_call_target="tpu_custom_call" | custom-call | flops 3168000000 | bytes 10368000 | tf_op jit(solution)/shard_map/pallas_call | solution.py:950
  266.7 1.1 collective-permute-start.58
  267.9 2.3 shard_map.248
  271.8 2.8 collective-permute-start.61
  275.3 4.2 %shard_map.246 = (bf16[2,192,896]{2,1,0:T(8,128)(2,1)}, bf16[2,192,896]{2,1,0:T(8,128)(2,1)}) custom-call(s32[34]{0:T(128)} %concatenate.63.places, bf16[256,3584]{1,0:T(8,128)(2,1)} %get-tuple-element.352.mine, bf16[256,3584]{1,0:T(8,128)(2,1)} %collective-permute-done.57.came), custom_call_target="tpu_custom_call" | custom-call | flops 2464000000 | bytes 8064000 | tf_op jit(solution)/shard_map/pallas_call | solution.py:950
  279.5 2.4 shard_map.247
  281.9 18.2 %collective-permute-done.58 = bf16[2,192,1152]{2,1,0:T(8,128)(2,1)} collective-permute-done((bf16[2,192,1152]{2,1,0:T(8,128)(2,1)}, bf16[2,192,1152]{2,1,0:T(8,128)(2,1)}, u32[]{:S(2)}, u32[]{:S(2)}) %collective-permute-start.58) | collective-permute-done | bytes 884768 | tf_op jit(solution)/shard_map/ppermute | solution.py:965
  300.1 1.4 convert_add_fusion
  302.3 2.1 collective-permute-start.64
  304.4 1.6 collective-permute-start.65
  306.1 2.8 collective-permute-start.66
  312.4 13.2 %all_gather.42.out_pieces = bf16[4,64,1536]{2,1,0:T(8,128)(2,1)} all-gather(bf16[1,64,1536]{2,1,0:T(8,128)(2,1)S(1)} %pad_maximum_fusion.7), channel_id=1, replica_groups=mesh['fsdp'=2,'ctx'=4,'tp'=4] {'tp'}, dimensions={0}, use_global_device_ids=true | all-gather | bytes 983040 | tf_op jit(solution)/shard_map/all_gather | solution.py:969
  325.6 7.3 %collective-permute-done.62 = bf16[2,192,896]{2,1,0:T(8,128)(2,1)S(1)} collective-permute-done((bf16[2,192,896]{2,1,0:T(8,128)(2,1)S(1)}, bf16[2,192,896]{2,1,0:T(8,128)(2,1)S(1)}, u32[]{:S(2)}, u32[]{:S(2)}) %collective-permute-start.62) | collective-permute-done | bytes 688160 | tf_op jit(solution)/shard_map/ppermute | solution.py:965
  334.2 12.8 %all-gather.4 = bf16[256,1792]{1,0:T(8,128)(2,1)} all-gather(bf16[64,1792]{1,0:T(8,128)(2,1)S(1)} %fusion.7), channel_id=6, replica_groups=mesh['fsdp'=2,'ctx'=4,'tp'=4] {'tp'}, dimensions={0}, use_global_device_ids=true | all-gather | bytes 1146880 | tf_op jit(solution)/shard_map/all_gather | solution.py:969
  346.9 2.7 shard_map.249
  (293 shorter events, 41.4 us)
Async XLA Ops:
  3.8 12.2 %collective-permute-start = (bf16[16,2176]{1,0:T(8,128)(2,1)}, bf16[16,2176]{1,0:T(8,128)(2,1)S(1)}, u32[]{:S(2)}, u32[]{:S(2)}) collective-permute-start(bf16[16,2176]{1,0:T(8,128)(2,1)} %get-tuple-element.207), channel_id=1, source_target_pairs={{0,4},{4,0},{8,12},{12,8},{1,5},{5,1},{9,13},{13,9},{2,6},{6,2},{1... | collective-permute-start | bytes 208904 | tf_op jit(solution)/shard_map/ppermute | solution.py:965
  6.9 9.1 %collective-permute-start.1 = (bf16[16,2176]{1,0:T(8,128)(2,1)}, bf16[16,2176]{1,0:T(8,128)(2,1)S(1)}, u32[]{:S(2)}, u32[]{:S(2)}) collective-permute-start(bf16[16,2176]{1,0:T(8,128)(2,1)} %get-tuple-element.208), channel_id=1, source_target_pairs={{0,8},{4,12},{8,0},{12,4},{1,9},{5,13},{9,1},{13,5},{2,10},{6,14},... | collective-permute-start | bytes 208904 | tf_op jit(solution)/shard_map/ppermute | solution.py:965
  9.5 6.5 %collective-permute-start.2 = (bf16[16,2176]{1,0:T(8,128)(2,1)}, bf16[16,2176]{1,0:T(8,128)(2,1)S(1)}, u32[]{:S(2)}, u32[]{:S(2)}) collective-permute-start(bf16[16,2176]{1,0:T(8,128)(2,1)} %get-tuple-element.209), channel_id=1, source_target_pairs={{0,12},{4,8},{8,4},{12,0},{1,13},{5,9},{9,5},{13,1},{2,14},{6,10},... | collective-permute-start | bytes 208904 | tf_op jit(solution)/shard_map/ppermute | solution.py:965
  16.1 25.4 %collective-permute-start.3 = (bf16[192,896]{1,0:T(8,128)(2,1)}, bf16[192,896]{1,0:T(8,128)(2,1)}, u32[]{:S(2)}, u32[]{:S(2)}) collective-permute-start(bf16[192,896]{1,0:T(8,128)(2,1)} %get-tuple-element.244.refs_0_), channel_id=1, source_target_pairs={{0,8},{4,12},{8,0},{12,4},{1,9},{5,13},{9,1},{13,5},{2,10},{6,14},... | collective-permute-start | bytes 1032200 | tf_op jit(solution)/shard_map/ppermute | solution.py:965
  18.1 23.5 %collective-permute-start.4 = (bf16[192,896]{1,0:T(8,128)(2,1)}, bf16[192,896]{1,0:T(8,128)(2,1)}, u32[]{:S(2)}, u32[]{:S(2)}) collective-permute-start(bf16[192,896]{1,0:T(8,128)(2,1)} %get-tuple-element.244.refs_0_), channel_id=1, source_target_pairs={{0,4},{4,0},{8,12},{12,8},{1,5},{5,1},{9,13},{13,9},{2,6},{6,2},{1... | collective-permute-start | bytes 1032200 | tf_op jit(solution)/shard_map/ppermute | solution.py:965
  32.7 4.7 %collective-permute-start.5 = (bf16[2,16,1536]{2,1,0:T(8,128)(2,1)S(1)}, bf16[2,16,1536]{2,1,0:T(8,128)(2,1)S(1)}, u32[]{:S(2)}, u32[]{:S(2)}) collective-permute-start(bf16[2,16,1536]{2,1,0:T(8,128)(2,1)S(1)} %copy-done.54), channel_id=1, source_target_pairs={{0,4},{4,0},{8,12},{12,8},{1,5},{5,1},{9,13},{13,9},{2,6},{6,2},{1... | collective-permute-start | bytes 294920 | tf_op jit(solution)/shard_map/ppermute | solution.py:965
  32.8 8.8 %collective-permute-start.6 = (bf16[2,16,1536]{2,1,0:T(8,128)(2,1)S(1)}, bf16[2,16,1536]{2,1,0:T(8,128)(2,1)S(1)}, u32[]{:S(2)}, u32[]{:S(2)}) collective-permute-start(bf16[2,16,1536]{2,1,0:T(8,128)(2,1)S(1)} %copy-done.53), channel_id=1, source_target_pairs={{0,8},{4,12},{8,0},{12,4},{1,9},{5,13},{9,1},{13,5},{2,10},{6,14},... | collective-permute-start | bytes 294920 | tf_op jit(solution)/shard_map/ppermute | solution.py:965
  33.5 8.0 %collective-permute-start.7 = (bf16[2,16,1536]{2,1,0:T(8,128)(2,1)S(1)}, bf16[2,16,1536]{2,1,0:T(8,128)(2,1)S(1)}, u32[]{:S(2)}, u32[]{:S(2)}) collective-permute-start(bf16[2,16,1536]{2,1,0:T(8,128)(2,1)S(1)} %copy-done.52), channel_id=1, source_target_pairs={{0,12},{4,8},{8,4},{12,0},{1,13},{5,9},{9,5},{13,1},{2,14},{6,10},... | collective-permute-start | bytes 294920 | tf_op jit(solution)/shard_map/ppermute | solution.py:965
  41.6 23.8 %collective-permute-start.9 = (bf16[192,1152]{1,0:T(8,128)(2,1)S(1)}, bf16[192,1152]{1,0:T(8,128)(2,1)S(1)}, u32[]{:S(2)}, u32[]{:S(2)}) collective-permute-start(bf16[192,1152]{1,0:T(8,128)(2,1)S(1)} %copy-done.17), channel_id=1, source_target_pairs={{0,8},{4,12},{8,0},{12,4},{1,9},{5,13},{9,1},{13,5},{2,10},{6,14},... | collective-permute-start | bytes 1327112 | tf_op jit(solution)/shard_map/ppermute | solution.py:965
  44.3 21.2 %collective-permute-start.10 = (bf16[2,64,1536]{2,1,0:T(8,128)(2,1)S(1)}, bf16[2,64,1536]{2,1,0:T(8,128)(2,1)S(1)}, u32[]{:S(2)}, u32[]{:S(2)}) collective-permute-start(bf16[2,64,1536]{2,1,0:T(8,128)(2,1)S(1)} %pad_maximum_fusion.4.refs_18_), channel_id=1, source_target_pairs={{0,1},{1,0},{2,3},{3,2},{4,5},{5,4},{6,7},{7,6},{8,9},{9,8},{10,11... | collective-permute-start | bytes 1179656 | tf_op jit(solution)/shard_map/ppermute | solution.py:965
  45.8 19.7 %collective-permute-start.11 = (bf16[2,64,1536]{2,1,0:T(8,128)(2,1)S(1)}, bf16[2,64,1536]{2,1,0:T(8,128)(2,1)S(1)}, u32[]{:S(2)}, u32[]{:S(2)}) collective-permute-start(bf16[2,64,1536]{2,1,0:T(8,128)(2,1)S(1)} %pad_maximum_fusion.4.refs_18_), channel_id=1, source_target_pairs={{0,2},{1,3},{2,0},{3,1},{4,6},{5,7},{6,4},{7,5},{8,10},{9,11},{10,... | collective-permute-start | bytes 1179656 | tf_op jit(solution)/shard_map/ppermute | solution.py:965
  47.3 18.2 %collective-permute-start.12 = (bf16[2,64,1536]{2,1,0:T(8,128)(2,1)S(1)}, bf16[2,64,1536]{2,1,0:T(8,128)(2,1)S(1)}, u32[]{:S(2)}, u32[]{:S(2)}) collective-permute-start(bf16[2,64,1536]{2,1,0:T(8,128)(2,1)S(1)} %pad_maximum_fusion.4.refs_18_), channel_id=1, source_target_pairs={{0,3},{1,2},{2,1},{3,0},{4,7},{5,6},{6,5},{7,4},{8,11},{9,10},{10,... | collective-permute-start | bytes 1179656 | tf_op jit(solution)/shard_map/ppermute | solution.py:965
  47.8 17.6 %collective-permute-start.8 = (bf16[192,896]{1,0:T(8,128)(2,1)}, bf16[192,896]{1,0:T(8,128)(2,1)}, u32[]{:S(2)}, u32[]{:S(2)}) collective-permute-start(bf16[192,896]{1,0:T(8,128)(2,1)} %collective-permute-done.3.refs_2_), channel_id=1, source_target_pairs={{0,4},{4,0},{8,12},{12,8},{1,5},{5,1},{9,13},{13,9},{2,6},{6,2},{1... | collective-permute-start | bytes 1032200 | tf_op jit(solution)/shard_map/ppermute | solution.py:965
  65.5 3.4 collective-permute-start.16
  68.1 18.5 %collective-permute-start.13 = (bf16[192,1152]{1,0:T(8,128)(2,1)S(1)}, bf16[192,1152]{1,0:T(8,128)(2,1)S(1)}, u32[]{:S(2)}, u32[]{:S(2)}) collective-permute-start(bf16[192,1152]{1,0:T(8,128)(2,1)S(1)} %copy-done.17), channel_id=1, source_target_pairs={{0,4},{4,0},{8,12},{12,8},{1,5},{5,1},{9,13},{13,9},{2,6},{6,2},{1... | collective-permute-start | bytes 1327112 | tf_op jit(solution)/shard_map/ppermute | solution.py:965
  68.8 16.7 %collective-permute-start.14 = (bf16[192,768]{1,0:T(8,128)(2,1)}, bf16[192,768]{1,0:T(8,128)(2,1)}, u32[]{:S(2)}, u32[]{:S(2)}) collective-permute-start(bf16[192,768]{1,0:T(8,128)(2,1)} %get-tuple-element.242), channel_id=1, source_target_pairs={{0,8},{4,12},{8,0},{12,4},{1,9},{5,13},{9,1},{13,5},{2,10},{6,14},... | collective-permute-start | bytes 884744 | tf_op jit(solution)/shard_map/ppermute | solution.py:965
  86.6 17.7 %collective-permute-start.20 = (bf16[192,1152]{1,0:T(8,128)(2,1)S(1)}, bf16[192,1152]{1,0:T(8,128)(2,1)S(1)}, u32[]{:S(2)}, u32[]{:S(2)}) collective-permute-start(bf16[192,1152]{1,0:T(8,128)(2,1)S(1)} %collective-permute-done.9.refs_2_.refs_10_), channel_id=1, source_target_pairs={{0,4},{4,0},{8,12},{12,8},{1,5},{5,1},{9,13},{13,9},{2,6},{6,2},{1... | collective-permute-start | bytes 1327112 | tf_op jit(solution)/shard_map/ppermute | solution.py:965
  86.6 17.7 %collective-permute-start.21 = (bf16[192,1152]{1,0:T(8,128)(2,1)S(1)}, bf16[192,1152]{1,0:T(8,128)(2,1)S(1)}, u32[]{:S(2)}, u32[]{:S(2)}) collective-permute-start(bf16[192,1152]{1,0:T(8,128)(2,1)S(1)} %copy-done.17), channel_id=1, source_target_pairs={{0,16},{16,0},{1,17},{17,1},{2,18},{18,2},{3,19},{19,3},{4,20},{20... | collective-permute-start | bytes 1327112 | tf_op jit(solution)/shard_map/ppermute | solution.py:965
  86.6 17.7 %collective-permute-start.22 = (bf16[192,1152]{1,0:T(8,128)(2,1)S(1)}, bf16[192,1152]{1,0:T(8,128)(2,1)S(1)}, u32[]{:S(2)}, u32[]{:S(2)}) collective-permute-start(bf16[192,1152]{1,0:T(8,128)(2,1)S(1)} %collective-permute-done.13.refs_1_.refs_9_), channel_id=1, source_target_pairs={{0,16},{16,0},{1,17},{17,1},{2,18},{18,2},{3,19},{19,3},{4,20},{20... | collective-permute-start | bytes 1327112 | tf_op jit(solution)/shard_map/ppermute | solution.py:965
  87.1 17.2 %collective-permute-start.23 = (bf16[192,1152]{1,0:T(8,128)(2,1)S(1)}, bf16[192,1152]{1,0:T(8,128)(2,1)S(1)}, u32[]{:S(2)}, u32[]{:S(2)}) collective-permute-start(bf16[192,1152]{1,0:T(8,128)(2,1)S(1)} %collective-permute-done.9.refs_2_.refs_10_), channel_id=1, source_target_pairs={{0,16},{16,0},{1,17},{17,1},{2,18},{18,2},{3,19},{19,3},{4,20},{20... | collective-permute-start | bytes 1327112 | tf_op jit(solution)/shard_map/ppermute | solution.py:965
  87.2 15.0 %collective-permute-start.24 = (bf16[192,768]{1,0:T(8,128)(2,1)S(1)}, bf16[192,768]{1,0:T(8,128)(2,1)}, u32[]{:S(2)}, u32[]{:S(2)}) collective-permute-start(bf16[192,768]{1,0:T(8,128)(2,1)S(1)} %copy-done.37), channel_id=1, source_target_pairs={{0,8},{4,12},{8,0},{12,4},{1,9},{5,13},{9,1},{13,5},{2,10},{6,14},... | collective-permute-start | bytes 884744 | tf_op jit(solution)/shard_map/ppermute | solution.py:965
  105.9 3.5 collective-permute-start.25
  107.4 10.6 %collective-permute-start.26 = (bf16[192,768]{1,0:T(8,128)(2,1)S(1)}, bf16[192,768]{1,0:T(8,128)(2,1)S(1)}, u32[]{:S(2)}, u32[]{:S(2)}) collective-permute-start(bf16[192,768]{1,0:T(8,128)(2,1)S(1)} %copy-done.35), channel_id=1, source_target_pairs={{0,4},{4,0},{8,12},{12,8},{1,5},{5,1},{9,13},{13,9},{2,6},{6,2},{1... | collective-permute-start | bytes 884744 | tf_op jit(solution)/shard_map/ppermute | solution.py:965
  109.1 14.0 %collective-permute-start.27 = (bf16[192,768]{1,0:T(8,128)(2,1)}, bf16[192,768]{1,0:T(8,128)(2,1)S(1)}, u32[]{:S(2)}, u32[]{:S(2)}) collective-permute-start(bf16[192,768]{1,0:T(8,128)(2,1)} %collective-permute-done.14.refs_4_), channel_id=1, source_target_pairs={{0,4},{4,0},{8,12},{12,8},{1,5},{5,1},{9,13},{13,9},{2,6},{6,2},{1... | collective-permute-start | bytes 884744 | tf_op jit(solution)/shard_map/ppermute | solution.py:965
  123.8 8.0 %collective-permute-start.28 = (bf16[64,1536]{1,0:T(8,128)(2,1)}, bf16[64,1536]{1,0:T(8,128)(2,1)S(1)}, u32[]{:S(2)}, u32[]{:S(2)}) collective-permute-start(bf16[64,1536]{1,0:T(8,128)(2,1)} %get-tuple-element.276), channel_id=1, source_target_pairs={{0,1},{1,0},{2,3},{3,2},{4,5},{5,4},{6,7},{7,6},{8,9},{9,8},{10,11... | collective-permute-start | bytes 589832 | tf_op jit(solution)/shard_map/ppermute | solution.py:965
  125.3 10.7 %collective-permute-start.29 = (bf16[64,1536]{1,0:T(8,128)(2,1)}, bf16[64,1536]{1,0:T(8,128)(2,1)S(1)}, u32[]{:S(2)}, u32[]{:S(2)}) collective-permute-start(bf16[64,1536]{1,0:T(8,128)(2,1)} %get-tuple-element.277), channel_id=1, source_target_pairs={{0,2},{1,3},{2,0},{3,1},{4,6},{5,7},{6,4},{7,5},{8,10},{9,11},{10,... | collective-permute-start | bytes 589832 | tf_op jit(solution)/shard_map/ppermute | solution.py:965
  126.9 9.0 %collective-permute-start.30 = (bf16[64,1536]{1,0:T(8,128)(2,1)}, bf16[64,1536]{1,0:T(8,128)(2,1)S(1)}, u32[]{:S(2)}, u32[]{:S(2)}) collective-permute-start(bf16[64,1536]{1,0:T(8,128)(2,1)} %get-tuple-element.278), channel_id=1, source_target_pairs={{0,3},{1,2},{2,1},{3,0},{4,7},{5,6},{6,5},{7,4},{8,11},{9,10},{10,... | collective-permute-start | bytes 589832 | tf_op jit(solution)/shard_map/ppermute | solution.py:965
  127.4 10.2 %collective-permute-start.31 = (bf16[192,768]{1,0:T(8,128)(2,1)}, bf16[192,768]{1,0:T(8,128)(2,1)S(1)}, u32[]{:S(2)}, u32[]{:S(2)}) collective-permute-start(bf16[192,768]{1,0:T(8,128)(2,1)} %collective-permute-done.24.refs_5_), channel_id=1, source_target_pairs={{0,4},{4,0},{8,12},{12,8},{1,5},{5,1},{9,13},{13,9},{2,6},{6,2},{1... | collective-permute-start | bytes 884744 | tf_op jit(solution)/shard_map/ppermute | solution.py:965
  129.1 12.6 %collective-permute-start.32 = (bf16[192,768]{1,0:T(8,128)(2,1)S(1)}, bf16[192,768]{1,0:T(8,128)(2,1)S(1)}, u32[]{:S(2)}, u32[]{:S(2)}) collective-permute-start(bf16[192,768]{1,0:T(8,128)(2,1)S(1)} %copy-done.36), channel_id=1, source_target_pairs={{0,4},{4,0},{8,12},{12,8},{1,5},{5,1},{9,13},{13,9},{2,6},{6,2},{1... | collective-permute-start | bytes 884744 | tf_op jit(solution)/shard_map/ppermute | solution.py:965
  141.7 15.1 %collective-permute-start.33 = (bf16[64,1536]{1,0:T(8,128)(2,1)S(1)}, bf16[64,1536]{1,0:T(8,128)(2,1)S(1)}, u32[]{:S(2)}, u32[]{:S(2)}) collective-permute-start(bf16[64,1536]{1,0:T(8,128)(2,1)S(1)} %multiply_convert_fusion), channel_id=1, source_target_pairs={{0,8},{4,12},{8,0},{12,4},{1,9},{5,13},{9,1},{13,5},{2,10},{6,14},... | collective-permute-start | bytes 589832 | tf_op jit(solution)/shard_map/ppermute | solution.py:965
  143.1 14.8 %collective-permute-start.35 = (bf16[192,768]{1,0:T(8,128)(2,1)S(1)}, bf16[192,768]{1,0:T(8,128)(2,1)S(1)}, u32[]{:S(2)}, u32[]{:S(2)}) collective-permute-start(bf16[192,768]{1,0:T(8,128)(2,1)S(1)} %copy-done.36), channel_id=1, source_target_pairs={{0,16},{16,0},{1,17},{17,1},{2,18},{18,2},{3,19},{19,3},{4,20},{20... | collective-permute-start | bytes 884744 | tf_op jit(solution)/shard_map/ppermute | solution.py:965
  143.2 14.4 %collective-permute-start.34 = (bf16[192,768]{1,0:T(8,128)(2,1)S(1)}, bf16[192,768]{1,0:T(8,128)(2,1)S(1)}, u32[]{:S(2)}, u32[]{:S(2)}) collective-permute-start(bf16[192,768]{1,0:T(8,128)(2,1)S(1)} %copy-done.35), channel_id=1, source_target_pairs={{0,16},{16,0},{1,17},{17,1},{2,18},{18,2},{3,19},{19,3},{4,20},{20... | collective-permute-start | bytes 884744 | tf_op jit(solution)/shard_map/ppermute | solution.py:965
  157.0 14.6 %collective-permute-start.37 = (bf16[192,768]{1,0:T(8,128)(2,1)S(1)}, bf16[192,768]{1,0:T(8,128)(2,1)S(1)}, u32[]{:S(2)}, u32[]{:S(2)}) collective-permute-start(bf16[192,768]{1,0:T(8,128)(2,1)S(1)} %collective-permute-done.32.refs_3_), channel_id=1, source_target_pairs={{0,16},{16,0},{1,17},{17,1},{2,18},{18,2},{3,19},{19,3},{4,20},{20... | collective-permute-start | bytes 884744 | tf_op jit(solution)/shard_map/ppermute | solution.py:965
  157.5 14.2 %collective-permute-start.38 = (bf16[192,768]{1,0:T(8,128)(2,1)}, bf16[192,768]{1,0:T(8,128)(2,1)S(1)}, u32[]{:S(2)}, u32[]{:S(2)}) collective-permute-start(bf16[192,768]{1,0:T(8,128)(2,1)} %collective-permute-done.14.refs_4_), channel_id=1, source_target_pairs={{0,16},{16,0},{1,17},{17,1},{2,18},{18,2},{3,19},{19,3},{4,20},{20... | collective-permute-start | bytes 884744 | tf_op jit(solution)/shard_map/ppermute | solution.py:965
  157.5 14.1 %collective-permute-start.39 = (bf16[192,768]{1,0:T(8,128)(2,1)}, bf16[192,768]{1,0:T(8,128)(2,1)S(1)}, u32[]{:S(2)}, u32[]{:S(2)}) collective-permute-start(bf16[192,768]{1,0:T(8,128)(2,1)} %collective-permute-done.24.refs_5_), channel_id=1, source_target_pairs={{0,16},{16,0},{1,17},{17,1},{2,18},{18,2},{3,19},{19,3},{4,20},{20... | collective-permute-start | bytes 884744 | tf_op jit(solution)/shard_map/ppermute | solution.py:965
  158.0 13.7 %collective-permute-start.40 = (bf16[192,768]{1,0:T(8,128)(2,1)S(1)}, bf16[192,768]{1,0:T(8,128)(2,1)S(1)}, u32[]{:S(2)}, u32[]{:S(2)}) collective-permute-start(bf16[192,768]{1,0:T(8,128)(2,1)S(1)} %copy-done.41), channel_id=1, source_target_pairs={{0,16},{16,0},{1,17},{17,1},{2,18},{18,2},{3,19},{19,3},{4,20},{20... | collective-permute-start | bytes 884744 | tf_op jit(solution)/shard_map/ppermute | solution.py:965
  158.5 13.2 %collective-permute-start.41 = (bf16[192,768]{1,0:T(8,128)(2,1)S(1)}, bf16[192,768]{1,0:T(8,128)(2,1)S(1)}, u32[]{:S(2)}, u32[]{:S(2)}) collective-permute-start(bf16[192,768]{1,0:T(8,128)(2,1)S(1)} %collective-permute-done.31.refs_7_), channel_id=1, source_target_pairs={{0,16},{16,0},{1,17},{17,1},{2,18},{18,2},{3,19},{19,3},{4,20},{20... | collective-permute-start | bytes 884744 | tf_op jit(solution)/shard_map/ppermute | solution.py:965
  185.4 13.5 %collective-permute-start.42 = (bf16[512,3072]{1,0:T(8,128)(2,1)}, bf16[512,3072]{1,0:T(8,128)(2,1)S(1)}, u32[]{:S(2)}, u32[]{:S(2)}) collective-permute-start(bf16[512,3072]{1,0:T(8,128)(2,1)} %get-tuple-element.304), channel_id=1, source_target_pairs={{0,16},{16,0},{1,17},{17,1},{2,18},{18,2},{3,19},{19,3},{4,20},{20... | collective-permute-start | bytes 9437192 | tf_op jit(solution)/shard_map/ppermute | solution.py:965
  185.5 8.0 %collective-permute-start.43 = (bf16[64,1536]{1,0:T(8,128)(2,1)}, bf16[64,1536]{1,0:T(8,128)(2,1)S(1)}, u32[]{:S(2)}, u32[]{:S(2)}) collective-permute-start(bf16[64,1536]{1,0:T(8,128)(2,1)} %get-tuple-element.306), channel_id=1, source_target_pairs={{0,1},{1,0},{2,3},{3,2},{4,5},{5,4},{6,7},{7,6},{8,9},{9,8},{10,11... | collective-permute-start | bytes 589832 | tf_op jit(solution)/shard_map/ppermute | solution.py:965
  186.5 11.4 %collective-permute-start.44 = (bf16[64,1536]{1,0:T(8,128)(2,1)}, bf16[64,1536]{1,0:T(8,128)(2,1)S(1)}, u32[]{:S(2)}, u32[]{:S(2)}) collective-permute-start(bf16[64,1536]{1,0:T(8,128)(2,1)} %get-tuple-element.307), channel_id=1, source_target_pairs={{0,2},{1,3},{2,0},{3,1},{4,6},{5,7},{6,4},{7,5},{8,10},{9,11},{10,... | collective-permute-start | bytes 589832 | tf_op jit(solution)/shard_map/ppermute | solution.py:965
  187.6 10.3 %collective-permute-start.45 = (bf16[64,1536]{1,0:T(8,128)(2,1)}, bf16[64,1536]{1,0:T(8,128)(2,1)S(1)}, u32[]{:S(2)}, u32[]{:S(2)}) collective-permute-start(bf16[64,1536]{1,0:T(8,128)(2,1)} %get-tuple-element.308), channel_id=1, source_target_pairs={{0,3},{1,2},{2,1},{3,0},{4,7},{5,6},{6,5},{7,4},{8,11},{9,10},{10,... | collective-permute-start | bytes 589832 | tf_op jit(solution)/shard_map/ppermute | solution.py:965
  200.6 12.0 %collective-permute-start.46 = (bf16[64,1536]{1,0:T(8,128)(2,1)}, bf16[64,1536]{1,0:T(8,128)(2,1)S(1)}, u32[]{:S(2)}, u32[]{:S(2)}) collective-permute-start(bf16[64,1536]{1,0:T(8,128)(2,1)} %get-tuple-element.314), channel_id=1, source_target_pairs={{0,1},{1,0},{2,3},{3,2},{4,5},{5,4},{6,7},{7,6},{8,9},{9,8},{10,11... | collective-permute-start | bytes 589832 | tf_op jit(solution)/shard_map/ppermute | solution.py:965
  201.7 10.9 %collective-permute-start.47 = (bf16[64,1536]{1,0:T(8,128)(2,1)}, bf16[64,1536]{1,0:T(8,128)(2,1)S(1)}, u32[]{:S(2)}, u32[]{:S(2)}) collective-permute-start(bf16[64,1536]{1,0:T(8,128)(2,1)} %get-tuple-element.315), channel_id=1, source_target_pairs={{0,2},{1,3},{2,0},{3,1},{4,6},{5,7},{6,4},{7,5},{8,10},{9,11},{10,... | collective-permute-start | bytes 589832 | tf_op jit(solution)/shard_map/ppermute | solution.py:965
  202.6 10.0 %collective-permute-start.48 = (bf16[64,1536]{1,0:T(8,128)(2,1)}, bf16[64,1536]{1,0:T(8,128)(2,1)S(1)}, u32[]{:S(2)}, u32[]{:S(2)}) collective-permute-start(bf16[64,1536]{1,0:T(8,128)(2,1)} %get-tuple-element.316), channel_id=1, source_target_pairs={{0,3},{1,2},{2,1},{3,0},{4,7},{5,6},{6,5},{7,4},{8,11},{9,10},{10,... | collective-permute-start | bytes 589832 | tf_op jit(solution)/shard_map/ppermute | solution.py:965
  204.1 10.5 %collective-permute-start.49 = (bf16[64,1536]{1,0:T(8,128)(2,1)S(1)}, bf16[64,1536]{1,0:T(8,128)(2,1)S(1)}, u32[]{:S(2)}, u32[]{:S(2)}) collective-permute-start(bf16[64,1536]{1,0:T(8,128)(2,1)S(1)} %add_convert_fusion), channel_id=1, source_target_pairs={{0,8},{4,12},{8,0},{12,4},{1,9},{5,13},{9,1},{13,5},{2,10},{6,14},... | collective-permute-start | bytes 589832 | tf_op jit(solution)/shard_map/ppermute | solution.py:965
  215.8 14.2 %collective-permute-start.50 = (bf16[2,192,768]{2,1,0:T(8,128)(2,1)S(1)}, bf16[2,192,768]{2,1,0:T(8,128)(2,1)S(1)}, u32[]{:S(2)}, u32[]{:S(2)}) collective-permute-start(bf16[2,192,768]{2,1,0:T(8,128)(2,1)S(1)} %copy-done.16), channel_id=1, source_target_pairs={{0,4},{4,0},{8,12},{12,8},{1,5},{5,1},{9,13},{13,9},{2,6},{6,2},{1... | collective-permute-start | bytes 1769480 | tf_op jit(solution)/shard_map/ppermute | solution.py:965
  230.2 21.6 %collective-permute-start.51 = (bf16[2,192,768]{2,1,0:T(8,128)(2,1)S(1)}, bf16[2,192,768]{2,1,0:T(8,128)(2,1)S(1)}, u32[]{:S(2)}, u32[]{:S(2)}) collective-permute-start(bf16[2,192,768]{2,1,0:T(8,128)(2,1)S(1)} %copy-done.15), channel_id=1, source_target_pairs={{0,4},{4,0},{8,12},{12,8},{1,5},{5,1},{9,13},{13,9},{2,6},{6,2},{1... | collective-permute-start | bytes 1769480 | tf_op jit(solution)/shard_map/ppermute | solution.py:965
  230.7 21.3 %collective-permute-start.53 = (bf16[2,64,1536]{2,1,0:T(8,128)(2,1)S(1)}, bf16[2,64,1536]{2,1,0:T(8,128)(2,1)S(1)}, u32[]{:S(2)}, u32[]{:S(2)}) collective-permute-start(bf16[2,64,1536]{2,1,0:T(8,128)(2,1)S(1)} %copy-done.30), channel_id=1, source_target_pairs={{0,1},{1,0},{2,3},{3,2},{4,5},{5,4},{6,7},{7,6},{8,9},{9,8},{10,11... | collective-permute-start | bytes 1179656 | tf_op jit(solution)/shard_map/ppermute | solution.py:965
  231.9 20.2 %collective-permute-start.54 = (bf16[2,64,1536]{2,1,0:T(8,128)(2,1)S(1)}, bf16[2,64,1536]{2,1,0:T(8,128)(2,1)S(1)}, u32[]{:S(2)}, u32[]{:S(2)}) collective-permute-start(bf16[2,64,1536]{2,1,0:T(8,128)(2,1)S(1)} %copy-done.29), channel_id=1, source_target_pairs={{0,2},{1,3},{2,0},{3,1},{4,6},{5,7},{6,4},{7,5},{8,10},{9,11},{10,... | collective-permute-start | bytes 1179656 | tf_op jit(solution)/shard_map/ppermute | solution.py:965
  232.8 19.3 %collective-permute-start.55 = (bf16[2,64,1536]{2,1,0:T(8,128)(2,1)S(1)}, bf16[2,64,1536]{2,1,0:T(8,128)(2,1)S(1)}, u32[]{:S(2)}, u32[]{:S(2)}) collective-permute-start(bf16[2,64,1536]{2,1,0:T(8,128)(2,1)S(1)} %copy-done.28), channel_id=1, source_target_pairs={{0,3},{1,2},{2,1},{3,0},{4,7},{5,6},{6,5},{7,4},{8,11},{9,10},{10,... | collective-permute-start | bytes 1179656 | tf_op jit(solution)/shard_map/ppermute | solution.py:965
  234.2 17.8 %collective-permute-start.52 = (bf16[192,768]{1,0:T(8,128)(2,1)S(1)}, bf16[192,768]{1,0:T(8,128)(2,1)S(1)}, u32[]{:S(2)}, u32[]{:S(2)}) collective-permute-start(bf16[192,768]{1,0:T(8,128)(2,1)S(1)} %fusion.5), channel_id=1, source_target_pairs={{0,8},{4,12},{8,0},{12,4},{1,9},{5,13},{9,1},{13,5},{2,10},{6,14},... | collective-permute-start | bytes 884744 | tf_op jit(solution)/shard_map/ppermute | solution.py:965
  253.5 4.1 %collective-permute-start.57 = (bf16[256,3584]{1,0:T(8,128)(2,1)}, bf16[256,3584]{1,0:T(8,128)(2,1)}, u32[]{:S(2)}, u32[]{:S(2)}) collective-permute-start(bf16[256,3584]{1,0:T(8,128)(2,1)} %get-tuple-element.349), channel_id=1, source_target_pairs={{0,16},{16,0},{1,17},{17,1},{2,18},{18,2},{3,19},{19,3},{4,20},{20... | collective-permute-start | bytes 5505032 | tf_op jit(solution)/shard_map/ppermute | solution.py:965
  257.7 21.9 %all-to-all-start = ((bf16[4,64,1536]{2,1,0:T(8,128)(2,1)}), bf16[4,64,1536]{2,1,0:T(8,128)(2,1)}, u32[]{:S(2)}, u32[]{:S(2)}) async-start(bf16[4,64,1536]{2,1,0:T(8,128)(2,1)} %get-tuple-element.358), calls=%async_computation | async-start | bytes 1572864 | tf_op jit(solution)/shard_map/all_to_all | solution.py:1266
  266.7 33.3 %collective-permute-start.58 = (bf16[2,192,1152]{2,1,0:T(8,128)(2,1)}, bf16[2,192,1152]{2,1,0:T(8,128)(2,1)}, u32[]{:S(2)}, u32[]{:S(2)}) collective-permute-start(bf16[2,192,1152]{2,1,0:T(8,128)(2,1)} %get-tuple-element.355), channel_id=1, source_target_pairs={{0,4},{4,0},{8,12},{12,8},{1,5},{5,1},{9,13},{13,9},{2,6},{6,2},{1... | collective-permute-start | bytes 2654216 | tf_op jit(solution)/shard_map/ppermute | solution.py:965
  270.2 31.4 %collective-permute-start.59 = (bf16[32,1536]{1,0:T(8,128)(2,1)}, bf16[32,1536]{1,0:T(8,128)(2,1)S(1)}, u32[]{:S(2)}, u32[]{:S(2)}) collective-permute-start(bf16[32,1536]{1,0:T(8,128)(2,1)} %get-tuple-element.368), channel_id=1, source_target_pairs={{0,4},{4,0},{8,12},{12,8},{1,5},{5,1},{9,13},{13,9},{2,6},{6,2},{1... | collective-permute-start | bytes 294920 | tf_op jit(solution)/shard_map/ppermute | solution.py:965
  271.1 30.5 %collective-permute-start.60 = (bf16[32,1536]{1,0:T(8,128)(2,1)}, bf16[32,1536]{1,0:T(8,128)(2,1)S(1)}, u32[]{:S(2)}, u32[]{:S(2)}) collective-permute-start(bf16[32,1536]{1,0:T(8,128)(2,1)} %get-tuple-element.369), channel_id=1, source_target_pairs={{0,8},{4,12},{8,0},{12,4},{1,9},{5,13},{9,1},{13,5},{2,10},{6,14},... | collective-permute-start | bytes 294920 | tf_op jit(solution)/shard_map/ppermute | solution.py:965
  271.8 29.8 %collective-permute-start.61 = (bf16[32,1536]{1,0:T(8,128)(2,1)}, bf16[32,1536]{1,0:T(8,128)(2,1)S(1)}, u32[]{:S(2)}, u32[]{:S(2)}) collective-permute-start(bf16[32,1536]{1,0:T(8,128)(2,1)} %get-tuple-element.370), channel_id=1, source_target_pairs={{0,12},{4,8},{8,4},{12,0},{1,13},{5,9},{9,5},{13,1},{2,14},{6,10},... | collective-permute-start | bytes 294920 | tf_op jit(solution)/shard_map/ppermute | solution.py:965
  274.6 27.0 %collective-permute-start.56 = (bf16[192,768]{1,0:T(8,128)(2,1)S(1)}, bf16[192,768]{1,0:T(8,128)(2,1)S(1)}, u32[]{:S(2)}, u32[]{:S(2)}) collective-permute-start(bf16[192,768]{1,0:T(8,128)(2,1)S(1)} %fusion.6), channel_id=1, source_target_pairs={{0,8},{4,12},{8,0},{12,4},{1,9},{5,13},{9,1},{13,5},{2,10},{6,14},... | collective-permute-start | bytes 884744 | tf_op jit(solution)/shard_map/ppermute | solution.py:965
  301.6 10.6 %collective-permute-start.63 = (bf16[16,1792]{1,0:T(8,128)(2,1)S(1)}, bf16[16,1792]{1,0:T(8,128)(2,1)S(1)}, u32[]{:S(2)}, u32[]{:S(2)}) collective-permute-start(bf16[16,1792]{1,0:T(8,128)(2,1)S(1)} %copy-done.57), channel_id=1, source_target_pairs={{0,4},{4,0},{8,12},{12,8},{1,5},{5,1},{9,13},{13,9},{2,6},{6,2},{1... | collective-permute-start | bytes 172040 | tf_op jit(solution)/shard_map/ppermute | solution.py:965
  302.3 9.9 %collective-permute-start.64 = (bf16[16,1792]{1,0:T(8,128)(2,1)S(1)}, bf16[16,1792]{1,0:T(8,128)(2,1)S(1)}, u32[]{:S(2)}, u32[]{:S(2)}) collective-permute-start(bf16[16,1792]{1,0:T(8,128)(2,1)S(1)} %copy-done.56), channel_id=1, source_target_pairs={{0,8},{4,12},{8,0},{12,4},{1,9},{5,13},{9,1},{13,5},{2,10},{6,14},... | collective-permute-start | bytes 172040 | tf_op jit(solution)/shard_map/ppermute | solution.py:965
  304.4 7.7 %collective-permute-start.65 = (bf16[16,1792]{1,0:T(8,128)(2,1)S(1)}, bf16[16,1792]{1,0:T(8,128)(2,1)S(1)}, u32[]{:S(2)}, u32[]{:S(2)}) collective-permute-start(bf16[16,1792]{1,0:T(8,128)(2,1)S(1)} %copy-done.55), channel_id=1, source_target_pairs={{0,12},{4,8},{8,4},{12,0},{1,13},{5,9},{9,5},{13,1},{2,14},{6,10},... | collective-permute-start | bytes 172040 | tf_op jit(solution)/shard_map/ppermute | solution.py:965
  306.1 26.8 %collective-permute-start.62 = (bf16[2,192,896]{2,1,0:T(8,128)(2,1)S(1)}, bf16[2,192,896]{2,1,0:T(8,128)(2,1)S(1)}, u32[]{:S(2)}, u32[]{:S(2)}) collective-permute-start(bf16[2,192,896]{2,1,0:T(8,128)(2,1)S(1)} %copy-done.14), channel_id=1, source_target_pairs={{0,4},{4,0},{8,12},{12,8},{1,5},{5,1},{9,13},{13,9},{2,6},{6,2},{1... | collective-permute-start | bytes 2064392 | tf_op jit(solution)/shard_map/ppermute | solution.py:965
  306.1 27.0 %collective-permute-start.66 = (bf16[192,1152]{1,0:T(8,128)(2,1)S(1)}, bf16[192,1152]{1,0:T(8,128)(2,1)S(1)}, u32[]{:S(2)}, u32[]{:S(2)}) collective-permute-start(bf16[192,1152]{1,0:T(8,128)(2,1)S(1)} %fusion.3), channel_id=1, source_target_pairs={{0,8},{4,12},{8,0},{12,4},{1,9},{5,13},{9,1},{13,5},{2,10},{6,14},... | collective-permute-start | bytes 1327112 | tf_op jit(solution)/shard_map/ppermute | solution.py:965
  333.1 18.6 %collective-permute-start.68 = (bf16[192,896]{1,0:T(8,128)(2,1)S(1)}, bf16[192,896]{1,0:T(8,128)(2,1)S(1)}, u32[]{:S(2)}, u32[]{:S(2)}) collective-permute-start(bf16[192,896]{1,0:T(8,128)(2,1)S(1)} %fusion.4), channel_id=1, source_target_pairs={{0,8},{4,12},{8,0},{12,4},{1,9},{5,13},{9,1},{13,5},{2,10},{6,14},... | collective-permute-start | bytes 1032200 | tf_op jit(solution)/shard_map/ppermute | solution.py:965
  (64 other events, 715.8 us)
where the time goes:
time: 354 us; the launch traced here: 353 us
  waiting for transfers between devices  105 us (30%)
  blocking collectives  75.4 us (21%)
  Pallas kernels  75.1 us (21%)
  starting transfers between devices  70 us (20%)
  local copies, waits for them, and re-layouts  15.7 us (4%)
  other arithmetic  10.3 us (3%)
    ppermute x69, waiting for transfers between devices, swap(): return lax.ppermute(block, axis, [(i, i ^ distance) for i in range(size)])  105 us
    all_gather x6, blocking collectives, gathered_tp(): return lax.all_gather(block, 'tp', axis=0)  75.4 us
    pallas_call x13, Pallas kernels, call(): pl.pallas_call(kernel, out_shape=[jax.ShapeDtypeStruct(shape, kind) for s...  75.1 us
    ppermute x69, starting transfers between devices, swap(): return lax.ppermute(block, axis, [(i, i ^ distance) for i in range(size)])  65.5 us
    unnamed x118, local copies, waits for them, and re-layouts  8.79 us
  transfers between devices with their start and end apart: 70, of which 22 were waited for; matrix products, arithmetic and copies ran while one was open for 4% of the time, Pallas kernels for 17%

commit v1 on v0

--- a/solution.py
+++ b/solution.py
@@ -676,15 +676,14 @@
         messages[k][:, :features] = blocks[k]
 
 
-def attention_pack_kernel(places, house, key, beta, query, value, out, first, second):
-    for target, sources in ((first, (house, key, beta)), (second, (query, value, out))):
-        at = 0
-        for source in sources:
-            width = source.shape[1]
-            if width < 128:
-                target[:, at : at + 128] = jnp.zeros((target.shape[0], 128), jnp.bfloat16)
-            target[:, at : at + width] = source[...]
-            at += width
+def attention_pack_kernel(places, house, key, beta, query, value, out, pack):
+    at = 0
+    for source in (house, key, beta, query, value, out):
+        width = source.shape[1]
+        if width < 128:
+            pack[:, at : at + 128] = jnp.zeros((pack.shape[0], 128), jnp.bfloat16)
+        pack[:, at : at + width] = source[...]
+        at += max(width, 128)
 
 
 def feed_forward_pack_kernel(places, output_grad, gate, up, down, *refs):
@@ -715,13 +714,15 @@
         messages[k][quarter:] = pair[(k ^ 2) * quarter : ((k ^ 2) + 1) * quarter]
 
 
-def result_kernel(places, d_parts, d_middle, x, factor, gain, gain_two_grad, *messages):
-    quarter, features = x.shape[0] // 4, x.shape[1]
+def result_kernel(places, d_parts, d_middle, block, gain, gain_two_grad, *messages):
+    quarter, features = block.shape[0] // 4, block.shape[1]
     d_one = sum(d_parts[n].astype(jnp.float32) for n in range(4))
-    normed = x[...] * factor[...]
+    x = block[...].astype(jnp.float32)
+    factor = lax.rsqrt(jnp.mean(x * x, axis=1, keepdims=True) + EPSILON)
+    normed = x * factor
     scaled = d_one * gain[...]
     mean = jnp.mean(scaled * normed, axis=1, keepdims=True)
-    in_grad = (d_middle[...] + factor[...] * (scaled - normed * mean)).astype(jnp.bfloat16)
+    in_grad = (d_middle[...] + factor * (scaled - normed * mean)).astype(jnp.bfloat16)
     gain_one_grad = jnp.sum(d_one * normed, axis=0, keepdims=True)
     row = lax.broadcasted_iota(jnp.int32, (quarter, 128), 0)
     for g, gains in enumerate((gain_one_grad, gain_two_grad[...])):
@@ -735,15 +736,20 @@
         messages[k][:, :features] = in_grad[k * quarter : (k + 1) * quarter]
 
 
-def spread_kernel(places, out_pieces, grad_pieces, out, grad, gains):
-    quarter, features = out.shape[1] // 4, out.shape[2]
+def spread_kernel(places, pieces, whole):
+    quarter, features = whole.shape[1] // 4, whole.shape[2]
     for n in range(4):
-        rows = slice(n * quarter, (n + 1) * quarter)
         for k in range(4):
-            at = pl.ds(places[26 + k], 1)
-            out[at, rows] = out_pieces[n, k * quarter : (k + 1) * quarter][None]
-            grad[at, rows] = grad_pieces[n, k * quarter : (k + 1) * quarter, :features][None]
-    gains[...] = sum(grad_pieces[n, :quarter, features:].astype(jnp.float32) for n in range(4))
+            rows = slice(k * quarter, (k + 1) * quarter)
+            whole[pl.ds(places[26 + k], 1), n * quarter : (n + 1) * quarter] = pieces[
+                n, rows, :features
+            ][None]
+
+
+def gradient_spread_kernel(places, pieces, whole, gains):
+    quarter, features = whole.shape[1] // 4, whole.shape[2]
+    spread_kernel(places, pieces, whole)
+    gains[...] = sum(pieces[n, :quarter, features:].astype(jnp.float32) for n in range(4))
 
 
 def weights_in_place(pieces, whole, places, first=0, count=None):
@@ -763,7 +769,7 @@
     h_all, proj, inverses, key_side = refs[10:14]
     w_all, weight_sems, x_sems, x_all = refs[14:18]
     x_copies = started(placed(xs, x_all, places), x_sems)
-    w_copies = started(weights_in_place(weights, w_all, places), weight_sems)
+    w_copies = started(weights_in_place(weights, w_all, places, 0, w_all.shape[1]), weight_sems)
     for copy in x_copies:
         copy.wait()
     width = (proj.shape[1] - 128) // 2
@@ -788,7 +794,8 @@
     weights, (h_all, proj_keys, inverses, key_side, id_row, id_col) = refs[0:8], refs[8:14]
     proj, attn, probs, query_side, parts = refs[14], refs[15], refs[16], refs[17], refs[18:22]
     w_all, total, sems = refs[22:25]
-    for copy in started(weights_in_place(weights, w_all, places), sems):
+    skip = weights[0].shape[1] - w_all.shape[1]
+    for copy in started(weights_in_place(weights, w_all, places, skip, w_all.shape[1]), sems):
         copy.wait()
     width = attn.shape[1]
     head = width // heads
@@ -868,16 +875,17 @@
 
 
 def attention_backward_kernel(heads, places, *refs):
-    first, second, ds = refs[0:8], refs[8:16], refs[16]
-    proj_keys, proj, probs, key_side, query_side, h_all, attn = refs[17:24]
-    keeps, sends, parts = refs[24:27]
-    w_first, w_second, d_all, d_attn, total, first_sems, second_sems, d_sems = refs[27:35]
+    weights, ds = refs[0:8], refs[8]
+    proj_keys, proj, probs, key_side, query_side, h_all, attn = refs[9:16]
+    keeps, sends, parts = refs[16:19]
+    w_first, w_second, d_all, d_attn, total, first_sems, second_sems, d_sems = refs[19:27]
     half, width = d_all.shape[1] // 2, d_attn.shape[1]
     d_keys_all = keeps.at[:, pl.ds(2 * half, 2 * width + 128)]
     d_queries_all = keeps.at[:, pl.ds(2 * half + 2 * width + 128, 2 * width)]
-    second_copies = started(weights_in_place(second, w_second, places), second_sems)
+    cut, rest = w_first.shape[1], w_second.shape[1]
+    second_copies = started(weights_in_place(weights, w_second, places, cut, rest), second_sems)
     d_copies = started(placed(ds, d_all, places), d_sems)
-    first_copies = started(weights_in_place(first, w_first, places), first_sems)
+    first_copies = started(weights_in_place(weights, w_first, places, 0, cut), first_sems)
     for copy in d_copies + second_copies:
         copy.wait()
     head = width // heads
@@ -955,7 +963,7 @@
         scratch_shapes=scratch,
         compiler_params=pltpu.CompilerParams(vmem_limit_bytes=VMEM_BYTES),
         cost_estimate=pl.CostEstimate(
-            flops=int(micros * 1.1e9), transcendentals=0, bytes_accessed=int(micros * 3.6e6)
+            flops=int(micros * 1e6), transcendentals=0, bytes_accessed=int(micros * 1e4)
         ),
     )(places, *operands)
 
@@ -1041,9 +1049,9 @@
         "avvv",
         2,
     )
-    first, second = call(
+    (pack,) = call(
         attention_pack_kernel,
-        [((depth, 2 * width + 128), low), ((depth, 3 * width), low)],
+        [((depth, used + width), low)],
         [],
         places,
         [w_house, w_key, w_beta, w_query, w_value, w_out],
@@ -1060,11 +1068,11 @@
         "avvv",
         3,
     )
-    x_messages, first, second, grad_messages, gives, ffn_keeps = step(
-        (to_owners(token_messages), first, second, packed[:4], packed[4:6], packed[6:8])
-    )
-
-    first_two, first_one = swap(first, "ctx", 2), swap(first, "ctx", 1)
+    x_messages, pack, grad_messages, gives, ffn_keeps = step(
+        (to_owners(token_messages), pack, packed[:4], packed[4:6], packed[6:8])
+    )
+
+    pack_two, pack_one = swap(pack, "ctx", 2), swap(pack, "ctx", 1)
     x_block = jnp.concatenate([message[:, :features] for message in x_messages])
     x_pieces = gathered_tp(x_block)
     info = jnp.stack([message[0, features:] for message in x_messages])
@@ -1074,13 +1082,25 @@
     gains = jnp.concatenate(
         [info[:, 128 : 128 + depth], info[:, 384 : 384 + depth]], axis=1
     ).astype(low)
+    id_row, id_col = ids[None, :], ids[:, None]
+    id_row, id_col, pack_two, pack_one, x_pieces, pack, gains, grad_messages, gives = step(
+        (id_row, id_col, pack_two, pack_one, x_pieces, pack, gains, grad_messages, gives)
+    )
+
+    pack_three = swap(pack_two, "ctx", 1)
     grad_messages = to_owners(grad_messages)
-    first_two, first_one, x_pieces, first, gains, grad_messages, second = step(
-        (first_two, first_one, x_pieces, first, gains, grad_messages, second)
-    )
-
-    first_three = swap(first_two, "ctx", 1)
-    second_two = swap(second, "ctx", 2)
+    pack_three, pack_two, pack_one, pack, gains, gives, grad_messages, ffn_keeps = step(
+        (pack_three, pack_two, pack_one, pack, gains, gives, grad_messages, ffn_keeps)
+    )
+
+    attn_weights = [pack, pack_one, pack_two, pack_three]
+    attn_weights = attn_weights + [other_core(piece) for piece in attn_weights]
+    gains_other = other_core(gains)
+    gains = jnp.where(core == 0, jnp.stack([gains, gains_other]), jnp.stack([gains_other, gains]))
+    gain_one = gains[:, :, :depth].reshape(1, features).astype(wide)
+    gain_two = gains[:, :, depth:].reshape(1, features).astype(wide)
+    give_two = [swap(gives[0], "ctx", 2)]
+    keep_one = [swap(ffn_keeps[0], "ctx", 1)]
     grads = jnp.stack(
         [
             jnp.concatenate([message[0] for message in grad_messages]),
@@ -1089,18 +1109,6 @@
     )
     own_grad = grads[0]
     grad_pieces = all_tp(grads)
-    first_three, first_two, first_one, second_two, gains, second, grad_pieces, gives = step(
-        (first_three, first_two, first_one, second_two, gains, second, grad_pieces, gives)
-    )
-
-    key_weights = [first, first_one, first_two, first_three]
-    key_weights = key_weights + [other_core(piece) for piece in key_weights]
-    gains_other = other_core(gains)
-    gains = jnp.where(core == 0, jnp.stack([gains, gains_other]), jnp.stack([gains_other, gains]))
-    gain_one = gains[:, :, :depth].reshape(1, features).astype(wide)
-    gain_two = gains[:, :, depth:].reshape(1, features).astype(wide)
-    second_one = swap(second, "ctx", 1)
-    give_two = [swap(gives[0], "ctx", 2)]
     square = ((heads, length, length), wide)
     h_all, proj_keys, inverses, key_side = call(
         functools.partial(keys_kernel, heads),
@@ -1112,24 +1120,10 @@
             pltpu.VMEM((length, features), low),
         ],
         places,
-        [*key_weights, x_pieces, gain_one],
+        [*attn_weights, x_pieces, gain_one],
         "a" * 9 + "v",
         20,
     )
-    second_two, second_one, give_two, give_last, proj_keys, second = step(
-        (second_two, second_one, give_two, gives[1], proj_keys, second)
-    )
-    second_three = swap(second_two, "ctx", 1)
-    second_others = [other_core(piece) for piece in (second, second_one, second_two)]
-    give_two = give_two + [swap(give_last, "ctx", 2)]
-    second_three, second_others, proj_keys, give_two, ffn_keeps = step(
-        (second_three, second_others, proj_keys, give_two, ffn_keeps)
-    )
-    query_weights = [
-        second, second_one, second_two, second_three, *second_others, other_core(second_three)
-    ]
-
-    keep_one, give_three = [swap(ffn_keeps[0], "ctx", 1)], [swap(give_two[0], "ctx", 1)]
     outs = call(
         functools.partial(queries_kernel, heads),
         [((length, 2 * width), wide), ((length, width), low), square, square]
@@ -1140,24 +1134,24 @@
             pltpu.SemaphoreType.DMA((8,)),
         ],
         places,
-        [*query_weights, h_all, proj_keys, inverses, key_side, ids[None, :], ids[:, None]],
+        [*attn_weights, h_all, proj_keys, inverses, key_side, id_row, id_col],
         "a" * 8 + "v" * 6,
         9,
     )
     proj, attn, probs, query_side = outs[:4]
-    give_two, branch_parts, keep_one, give_three, ffn_keeps = step(
-        (give_two, outs[4:], keep_one, give_three, ffn_keeps)
-    )
-    keep_one = keep_one + [swap(ffn_keeps[1], "ctx", 1)]
-    give_three = give_three + [swap(give_two[1], "ctx", 1)]
-    residual = x_block.astype(wide)
-    normed_one, factor_one = norm_rows(residual)
-    middle = residual + add_up(sum_tp(branch_parts))
+    give_two, branch_parts, keep_one, grad_pieces, give_last, ffn_keeps = step(
+        (give_two, outs[4:], keep_one, grad_pieces, gives[1], ffn_keeps)
+    )
+    give_two = give_two + [swap(give_last, "ctx", 2)]
+    give_three = [swap(give_two[0], "ctx", 1)]
+    middle = x_block.astype(wide) + add_up(sum_tp(branch_parts))
     normed_two, factor_two = norm_rows(middle)
     h_two = (normed_two * gain_two).astype(low)
-    give_two, give_three, keep_one, h_two = step((give_two, give_three, keep_one, h_two))
+    give_two, give_three, ffn_keeps, h_two = step((give_two, give_three, ffn_keeps, h_two))
 
     h_pair = swap(h_two, "ctx", 2)
+    give_three = give_three + [swap(give_two[1], "ctx", 1)]
+    keep_one = keep_one + [swap(ffn_keeps[1], "ctx", 1)]
     h_own = gathered_tp(h_two)
     h_pair, give_three, h_own, keep_one, give_two = step(
         (h_pair, give_three, h_own, keep_one, give_two)
@@ -1208,7 +1202,7 @@
         keeps, came, ((0, features, 2 * units), (1, features + 2 * units, units)), 2
     )
     d_two = own_sum + two_other.astype(wide)
-    gain_two_grad = jnp.sum(d_two * normed_two, axis=0)
+    gain_two_grad = jnp.sum(d_two * normed_two, axis=0, keepdims=True)
     d_middle = own_grad.astype(wide) + norm_back(d_two, normed_two, factor_two, gain_two)
     d_low, ffn_grads = step((d_middle.astype(low), tuple(ffn_grads)))
 
@@ -1235,8 +1229,8 @@
             pltpu.SemaphoreType.DMA((16,)),
         ],
         places,
-        [*key_weights, *query_weights, d_pieces, proj_keys, proj, probs, key_side, query_side, h_all, attn],
-        "a" * 17 + "v" * 7,
+        [*attn_weights, d_pieces, proj_keys, proj, probs, key_side, query_side, h_all, attn],
+        "a" * 9 + "v" * 7,
         14,
     )
     ffn_sums = ffn_sums + [add_up([ffn_grads[2], ffn_came[1]])]
@@ -1244,15 +1238,17 @@
         (ffn_sums[1][1].astype(low), ffn_other, out_received, tuple(back))
     )
 
-    came, keeps, d_parts = step((other_core(sends), keeps, d_parts))
-
+    came, keeps, d_parts, out_received, ffn_leave = step(
+        (other_core(sends), keeps, d_parts, out_received, ffn_leave)
+    )
+
+    ffn_other = ffn_other + [swap(ffn_leave, "ctx", 2)]
     query_start = features + 2 * width + 128
     near_two, far_two = grads_of(
         keeps, came, ((0, query_start, 2 * width), (1, query_start + 2 * width, width))
     )
+    out_received, near_two, far_two, keeps = step((out_received, near_two, far_two, keeps))
     two_came = swap(far_two, "ctx", 1)
-    ffn_other = ffn_other + [swap(ffn_leave, "ctx", 2)]
-    near_one, far_one = grads_of(keeps, came, ((0, features, 2 * width + 128),))
     out_messages = call(
         out_message_kernel,
         [((2 * quarter, features), low)] * 4,
@@ -1262,49 +1258,52 @@
         "v" * 5,
         2,
     )
+    out_messages, keeps = step((tuple(out_messages), keeps))
     out_messages = to_owners(out_messages)
+    near_one, far_one = grads_of(keeps, came, ((0, features, 2 * width + 128),))
+    d_parts, near_one, far_one = step((d_parts, near_one, far_one))
     d_received = lax.all_to_all(d_parts, "tp", 0, 0)
     messages = call(
         result_kernel,
         [((quarter, features + 256), low)] * 4,
         [],
         places,
-        [d_received, d_middle, residual, factor_one, gain_one, gain_two_grad[None]],
-        "v" * 6,
+        [d_received, d_middle, x_block, gain_one, gain_two_grad],
+        "v" * 5,
         3,
     )
     two_sum = add_up([near_two, two_came])
-    ffn_other, two_leave, near_one, far_one, messages, out_messages = step(
-        (ffn_other, two_sum[1].astype(low), near_one, far_one, tuple(messages), out_messages)
+    two_leave, near_one, far_one, messages, out_messages, ffn_other = step(
+        (two_sum[1].astype(low), near_one, far_one, tuple(messages), out_messages, ffn_other)
     )
 
     one_came = swap(far_one, "ctx", 1)
     query_other = swap(two_leave, "ctx", 2)
-    messages, out_messages = step((to_owners(messages), out_messages))
+    messages = step(to_owners(messages))
+    owned = jnp.concatenate([message[:, :features] for message in messages])
+    gain_sum = add_up([message[:, features:] for message in messages]).astype(low)
+    owned = jnp.concatenate([owned, jnp.pad(gain_sum, ((0, 3 * quarter), (0, 0)))], axis=1)
+    input_grad, gain_total = call(
+        gradient_spread_kernel,
+        [((4, rows, features), low), ((quarter, 256), wide)],
+        [],
+        places,
+        [gathered_tp(owned)],
+        "v",
+        3,
+    )
+    one_sum = add_up([near_one, one_came])
     out_block = jnp.concatenate(
         [add_up([out_messages[n][:quarter], out_messages[n ^ 2][quarter:]]) for n in range(4)]
     ).astype(low)
-    out_pieces = gathered_tp(out_block)
-    owned = jnp.concatenate(
-        [message[:, :features] for message in messages]
-    )
-    gain_sum = add_up([message[:, features:] for message in messages]).astype(low)
-    owned = jnp.concatenate([owned, jnp.pad(gain_sum, ((0, 3 * quarter), (0, 0)))], axis=1)
-    one_sum = add_up([near_one, one_came])
-    one_leave, owned, query_other, out_pieces = step(
-        (one_sum[1].astype(low), owned, query_other, out_pieces)
+    one_leave, input_grad, gain_total, query_other, out_block = step(
+        (one_sum[1].astype(low), input_grad, gain_total, query_other, out_block)
     )
 
     key_other = swap(one_leave, "ctx", 2)
-    block_out, input_grad, gain_total = call(
-        spread_kernel,
-        [((4, rows, features), low)] * 2 + [((quarter, 256), wide)],
-        [],
-        places,
-        [out_pieces, gathered_tp(owned)],
-        "vv",
-        3,
-    )
+    block_out = call(
+        spread_kernel, [((4, rows, features), low)], [], places, [gathered_tp(out_block)], "v", 2
+    )[0]
     gain_total = gain_total + other_core(gain_total)
     gain_total = jnp.concatenate(
         [gain_total[: features // 128, :128], gain_total[: features // 128, 128:]]

time: 354 us -> 343 us (0.969)
  waiting for transfers between devices: 105 us -> 96.8 us
    ppermute x69 -> x62, waiting for transfers between devices: 105 us -> 93.5 us  [swap(): return lax.ppermute(block, axis, [(i, i ^ distance) for i in range(size)])]
    unnamed x118 -> x106, local copies, waits for them, and re-layouts: 8.79 us -> 6.63 us
    pallas_call x13 -> x14, Pallas kernels: 75.1 us -> 76.7 us  [call(): pl.pallas_call(kernel, out_shape=[jax.ShapeDtypeStruct(shape, kind) for s...]
    ppermute x69 -> x62, starting transfers between devices: 65.5 us -> 64.8 us  [swap(): return lax.ppermute(block, axis, [(i, i ^ distance) for i in range(size)])]
  transfers between devices with their start and end apart: 70 -> 63, of which waited for: 22 -> 25; matrix products, arithmetic and copies ran while one was open for 4% -> 4% of each run, Pallas kernels for 17% -> 17%
where the time goes in v1:
time: 343 us; the launch traced here: 342 us
  waiting for transfers between devices  96.8 us (28%)
  Pallas kernels  76.7 us (22%)
  blocking collectives  73.3 us (21%)
  starting transfers between devices  69.3 us (20%)
  local copies, waits for them, and re-layouts  13 us (4%)
  other arithmetic  11 us (3%)
    ppermute x62, waiting for transfers between devices, swap(): return lax.ppermute(block, axis, [(i, i ^ distance) for i in range(size)])  93.5 us
    pallas_call x14, Pallas kernels, call(): pl.pallas_call(kernel, out_shape=[jax.ShapeDtypeStruct(shape, kind) for s...  76.7 us
    all_gather x6, blocking collectives, gathered_tp(): return lax.all_gather(block, 'tp', axis=0)  73.3 us
    ppermute x62, starting transfers between devices, swap(): return lax.ppermute(block, axis, [(i, i ^ distance) for i in range(size)])  64.8 us
  transfers between devices with their start and end apart: 63, of which 25 were waited for; matrix products, arithmetic and copies ran while one was open for 4% of the time, Pallas kernels for 17%

profile of v1, /device:TPU:0, one launch (start us, length us, event | category | flops | bytes accessed | tf_op | source)
XLA Modules:
  0.0 341.8 jit_solution(11984926417660102644)
XLA Ops:
  1.5 2.4 shard_map.237
  3.9 3.1 collective-permute-start
  7.0 2.6 collective-permute-start.1
  9.6 1.4 copy.32.beta
  11.0 2.2 shard_map.238.refs_0_
  13.2 3.5 %shard_map.239 = (bf16[2,16,1536]{2,1,0:T(8,128)(2,1)}, bf16[2,16,1536]{2,1,0:T(8,128)(2,1)}, bf16[2,16,1536]{2,1,0:T(8,128)(2,1)}, bf16[2,16,1536]{2,1,0:T(8,12...) custom-call(s32[34]{0:T(128)} %concatenate.48.places, ...), custom_call_target="tpu_custom_call" | custom-call | flops 3000000 | bytes 30000 | tf_op jit(solution)/shard_map/pallas_call | solution.py:958
  17.9 3.5 %collective-permute-start.3 = (bf16[192,2048]{1,0:T(8,128)(2,1)S(1)}, bf16[192,2048]{1,0:T(8,128)(2,1)S(1)}, u32[]{:S(2)}, u32[]{:S(2)}) collective-permute-start(bf16[192,2048]{1,0:T(8,128)(2,1)S(1)} %copy-done), channel_id=1, source_target_pairs={{0,8},{4,12},{8,0},{12,4},{1,9},{5,13},{9,1},{13,5},{2,10},{6,14},... | collective-permute-start | bytes 2359304 | tf_op jit(solution)/shard_map/ppermute | solution.py:973
  22.3 12.0 %all-gather = bf16[256,1536]{1,0:T(8,128)(2,1)} all-gather(bf16[64,1536]{1,0:T(8,128)(2,1)S(1)} %pad_maximum_fusion.5.block), channel_id=2, replica_groups=mesh['fsdp'=2,'ctx'=4,'tp'=4] {'tp'}, dimensions={0}, use_global_device_ids=true | all-gather | bytes 983040 | tf_op jit(solution)/shard_map/all_gather | solution.py:977
  34.3 18.0 %collective-permute-done.4.refs_1_ = bf16[192,2048]{1,0:T(8,128)(2,1)S(1)} collective-permute-done((bf16[192,2048]{1,0:T(8,128)(2,1)S(1)}, bf16[192,2048]{1,0:T(8,128)(2,1)S(1)}, u32[]{:S(2)}, u32[]{:S(2)}) %collective-permute-start.4) | collective-permute-done | bytes 786464 | tf_op jit(solution)/shard_map/ppermute | solution.py:973
  52.3 2.4 collective-permute-done.3.refs_2_
  55.0 1.8 collective-permute-start.6
  57.7 1.7 collective-permute-start.8
  59.4 17.0 %collective-permute-done.6 = bf16[2,16,1536]{2,1,0:T(8,128)(2,1)S(1)} collective-permute-done((bf16[2,16,1536]{2,1,0:T(8,128)(2,1)S(1)}, bf16[2,16,1536]{2,1,0:T(8,128)(2,1)S(1)}, u32[]{:S(2)}, u32[]{:S(2)}) %collective-permute-start.6) | collective-permute-done | bytes 98336 | tf_op jit(solution)/shard_map/ppermute | solution.py:973
  76.4 2.9 collective-permute-done.8
  81.4 2.4 collective-permute-start.18
  87.3 2.3 collective-permute-start.15
  90.4 9.3 %shard_map.240 = (bf16[256,1536]{1,0:T(8,128)(2,1)}, f32[256,896]{1,0:T(8,128)}, f32[3,256,256]{2,1,0:T(8,128)}, f32[3,256,256]{2,1,0:T(8,128)}) custom-call(s32[34]{0:T(128)} %concatenate.48.places, bf16[192,2048]{1,0:T(8,128)(2,1)} %shard_map.238.refs_0_, bf16[192,2048]{1,0:T(8,128)(2,1)} %copy-done.3, bf16[192,2048]{1,0:T(8,128)(2,1)} %copy-done.4, ...), custom_call_target="tpu_custom_call" | custom-call | flops 20000000 | bytes 200000 | tf_op jit(solution)/shard_map/pallas_call | solution.py:958
  99.7 7.8 %shard_map.241 = (f32[256,768]{1,0:T(8,128)}, bf16[256,384]{1,0:T(8,128)(2,1)}, f32[3,256,256]{2,1,0:T(8,128)}, f32[3,256,256]{2,1,0:T(8,128)}, bf16[64,1536]{1,...) custom-call(s32[34]{0:T(128)} %concatenate.48.places, ...), custom_call_target="tpu_custom_call" | custom-call | flops 9000000 | bytes 90000 | tf_op jit(solution)/shard_map/pallas_call | solution.py:958
  111.8 2.0 collective-permute-start.23
  113.9 1.8 collective-permute-done.19
  115.7 2.1 collective-permute-done.20
  117.9 1.5 collective-permute-done.21
  120.7 5.2 %collective-permute-done.22.refs_5_ = bf16[192,768]{1,0:T(8,128)(2,1)S(1)} collective-permute-done((bf16[192,768]{1,0:T(8,128)(2,1)S(1)}, bf16[192,768]{1,0:T(8,128)(2,1)S(1)}, u32[]{:S(2)}, u32[]{:S(2)}) %collective-permute-start.22) | collective-permute-done | bytes 294944 | tf_op jit(solution)/shard_map/ppermute | solution.py:973
  126.1 1.9 collective-permute-start.26
  129.1 12.6 %all-gather.1 = bf16[256,1536]{1,0:T(8,128)(2,1)} all-gather(bf16[64,1536]{1,0:T(8,128)(2,1)S(1)} %multiply_convert_fusion), channel_id=3, replica_groups=mesh['fsdp'=2,'ctx'=4,'tp'=4] {'tp'}, dimensions={0}, use_global_device_ids=true | all-gather | bytes 983040 | tf_op jit(solution)/shard_map/all_gather | solution.py:977
  141.7 1.5 collective-permute-done.24
  143.2 2.2 collective-permute-done.26.refs_3_
  147.7 13.2 %all-gather.2 = bf16[256,1536]{1,0:T(8,128)(2,1)} all-gather(bf16[64,1536]{1,0:T(8,128)(2,1)S(1)} %collective-permute-done.24), channel_id=4, replica_groups=mesh['fsdp'=2,'ctx'=4,'tp'=4] {'tp'}, dimensions={0}, use_global_device_ids=true | all-gather | bytes 983040 | tf_op jit(solution)/shard_map/all_gather | solution.py:977
  162.0 12.7 %shard_map.242 = (bf16[64,1536]{1,0:T(8,128)(2,1)}, bf16[64,1536]{1,0:T(8,128)(2,1)}, bf16[64,1536]{1,0:T(8,128)(2,1)}, bf16[64,1536]{1,0:T(8,128)(2,1)}, bf16[6...) custom-call(s32[34]{0:T(128)} %concatenate.48.places, ...), custom_call_target="tpu_custom_call" | custom-call | flops 12000000 | bytes 120000 | tf_op jit(solution)/shard_map/pallas_call | solution.py:958
  176.8 1.5 collective-permute-start.38
  178.3 4.4 %collective-permute-done.36 = bf16[64,1536]{1,0:T(8,128)(2,1)S(1)} collective-permute-done((bf16[64,1536]{1,0:T(8,128)(2,1)}, bf16[64,1536]{1,0:T(8,128)(2,1)S(1)}, u32[]{:S(2)}, u32[]{:S(2)}) %collective-permute-start.36) | collective-permute-done | bytes 196640 | tf_op jit(solution)/shard_map/ppermute | solution.py:973
  182.7 4.7 %collective-permute-done.37 = bf16[64,1536]{1,0:T(8,128)(2,1)S(1)} collective-permute-done((bf16[64,1536]{1,0:T(8,128)(2,1)}, bf16[64,1536]{1,0:T(8,128)(2,1)S(1)}, u32[]{:S(2)}, u32[]{:S(2)}) %collective-permute-start.37) | collective-permute-done | bytes 196640 | tf_op jit(solution)/shard_map/ppermute | solution.py:973
  190.5 1.5 collective-permute-start.41
  192.9 7.0 %shard_map.243 = (bf16[2,192,768]{2,1,0:T(8,128)(2,1)}, bf16[2,192,768]{2,1,0:T(8,128)(2,1)}, bf16[2,192,768]{2,1,0:T(8,128)(2,1)}, bf16[2,192,768]{2,1,0:T(8,128)(2,1)}) custom-call(s32[34]{0:T(128)} %concatenate.48.places, bf16[512,3072]{1,0:T(8,128)(2,1)} %get-tuple-element.310.mine, bf16[512,3072]{1,0:T(8,128)(2,1)} %copy-done.8), custom_call_target="tpu_custom_call" | custom-call | flops 3840000 | bytes 38400 | tf_op jit(solution)/shard_map/pallas_call | solution.py:958
  199.8 2.6 collective-permute-done.42
  203.7 11.8 %all-gather.3 = bf16[256,1536]{1,0:T(8,128)(2,1)} all-gather(bf16[64,1536]{1,0:T(8,128)(2,1)S(1)} %get-tuple-element.317), channel_id=5, replica_groups=mesh['fsdp'=2,'ctx'=4,'tp'=4] {'tp'}, dimensions={0}, use_global_device_ids=true | all-gather | bytes 983040 | tf_op jit(solution)/shard_map/all_gather | solution.py:977
  215.5 3.3 collective-permute-done.43
  219.3 2.1 collective-permute-start.45
  223.4 1.5 collective-permute-start.48
  224.9 14.3 %shard_map.244 = (bf16[256,3584]{1,0:T(8,128)(2,1)}, bf16[256,3584]{1,0:T(8,128)(2,1)}, bf16[4,64,1536]{2,1,0:T(8,128)(2,1)}) custom-call(s32[34]{0:T(128)} %concatenate.48.places, bf16[192,2048]{1,0:T(8,128)(2,1)} %shard_map.238.refs_0_, bf16[192,2048]{1,0:T(8,128)(2,1)} %copy-done.3, bf16[192,2048]{1,0:T(8,128)(2,1)} %copy-done.4, ...), custom_call_target="tpu_custom_call" | custom-call | flops 14000000 | bytes 140000 | tf_op jit(solution)/shard_map/pallas_call | solution.py:958
  240.7 3.8 %collective-permute-done.49.came = bf16[256,3584]{1,0:T(8,128)(2,1)S(1)} collective-permute-done((bf16[256,3584]{1,0:T(8,128)(2,1)S(1)}, bf16[256,3584]{1,0:T(8,128)(2,1)S(1)}, u32[]{:S(2)}, u32[]{:S(2)}) %collective-permute-start.49) | collective-permute-done | bytes 1835040 | tf_op jit(solution)/shard_map/ppermute | solution.py:973
  244.5 1.2 copy-done.2
  245.7 4.6 %shard_map.245 = (bf16[2,192,1152]{2,1,0:T(8,128)(2,1)}, bf16[2,192,1152]{2,1,0:T(8,128)(2,1)}) custom-call(s32[34]{0:T(128)} %concatenate.48.places, bf16[256,3584]{1,0:T(8,128)(2,1)} %get-tuple-element.367.mine, bf16[256,3584]{1,0:T(8,128)(2,1)} %copy-done.2), custom_call_target="tpu_custom_call" | custom-call | flops 2880000 | bytes 28800 | tf_op jit(solution)/shard_map/pallas_call | solution.py:958
  250.6 2.3 shard_map.246
  252.9 4.2 %shard_map.247 = (bf16[2,192,896]{2,1,0:T(8,128)(2,1)}, bf16[2,192,896]{2,1,0:T(8,128)(2,1)}) custom-call(s32[34]{0:T(128)} %concatenate.48.places, bf16[256,3584]{1,0:T(8,128)(2,1)} %get-tuple-element.367.mine, bf16[256,3584]{1,0:T(8,128)(2,1)} %copy-done.2), custom_call_target="tpu_custom_call" | custom-call | flops 2240000 | bytes 22400 | tf_op jit(solution)/shard_map/pallas_call | solution.py:958
  257.2 4.5 %all-to-all-start = ((bf16[4,64,1536]{2,1,0:T(8,128)(2,1)}), bf16[4,64,1536]{2,1,0:T(8,128)(2,1)}, u32[]{:S(2)}, u32[]{:S(2)}) async-start(bf16[4,64,1536]{2,1,0:T(8,128)(2,1)} %get-tuple-element.372), calls=%async_computation | async-start | bytes 1572864 | tf_op jit(solution)/shard_map/all_to_all | solution.py:1265
  262.3 2.5 collective-permute-start.54
  265.0 2.1 collective-permute-start.52
  267.1 2.1 collective-permute-start.53
  269.2 3.3 all-to-all-done.d_parts
  272.6 2.3 shard_map.248
  274.9 6.2 %collective-permute-done.50 = bf16[2,192,1152]{2,1,0:T(8,128)(2,1)} collective-permute-done((bf16[2,192,1152]{2,1,0:T(8,128)(2,1)}, bf16[2,192,1152]{2,1,0:T(8,128)(2,1)}, u32[]{:S(2)}, u32[]{:S(2)}) %collective-permute-start.50) | collective-permute-done | bytes 884768 | tf_op jit(solution)/shard_map/ppermute | solution.py:973
  281.1 1.3 convert_add_fusion
  282.5 3.3 collective-permute-done.52
  285.8 1.6 collective-permute-start.56
  288.5 1.8 collective-permute-start.58
  290.3 1.3 collective-permute-start.59
  291.6 1.3 collective-permute-start.55
  296.3 7.5 %collective-permute-done.57 = bf16[16,1792]{1,0:T(8,128)(2,1)S(1)} collective-permute-done((bf16[16,1792]{1,0:T(8,128)(2,1)S(1)}, bf16[16,1792]{1,0:T(8,128)(2,1)S(1)}, u32[]{:S(2)}, u32[]{:S(2)}) %collective-permute-start.57) | collective-permute-done | bytes 57376 | tf_op jit(solution)/shard_map/ppermute | solution.py:973
  303.9 11.6 %all-gather.4 = bf16[256,1792]{1,0:T(8,128)(2,1)} all-gather(bf16[64,1792]{1,0:T(8,128)(2,1)S(1)} %fusion.7), channel_id=6, replica_groups=mesh['fsdp'=2,'ctx'=4,'tp'=4] {'tp'}, dimensions={0}, use_global_device_ids=true | all-gather | bytes 1146880 | tf_op jit(solution)/shard_map/all_gather | solution.py:977
  315.5 2.1 shard_map.249
  320.1 3.9 %collective-permute-start.61 = (bf16[192,896]{1,0:T(8,128)(2,1)S(1)}, bf16[192,896]{1,0:T(8,128)(2,1)S(1)}, u32[]{:S(2)}, u32[]{:S(2)}) collective-permute-start(bf16[192,896]{1,0:T(8,128)(2,1)S(1)} %fusion.4), channel_id=1, source_target_pairs={{0,8},{4,12},{8,0},{12,4},{1,9},{5,13},{9,1},{13,5},{2,10},{6,14},... | collective-permute-start | bytes 1032200 | tf_op jit(solution)/shard_map/ppermute | solution.py:973
  324.1 12.3 %all-gather.5 = bf16[256,1536]{1,0:T(8,128)(2,1)} all-gather(bf16[64,1536]{1,0:T(8,128)(2,1)S(1)} %pad_maximum_fusion.7), channel_id=7, replica_groups=mesh['fsdp'=2,'ctx'=4,'tp'=4] {'tp'}, dimensions={0}, use_global_device_ids=true | all-gather | bytes 983040 | tf_op jit(solution)/shard_map/all_gather | solution.py:977
  336.4 2.1 shard_map.250
  (266 shorter events, 43.2 us)
Async XLA Ops:
  3.9 12.8 %collective-permute-start = (bf16[16,2176]{1,0:T(8,128)(2,1)}, bf16[16,2176]{1,0:T(8,128)(2,1)S(1)}, u32[]{:S(2)}, u32[]{:S(2)}) collective-permute-start(bf16[16,2176]{1,0:T(8,128)(2,1)} %get-tuple-element.211), channel_id=1, source_target_pairs={{0,4},{4,0},{8,12},{12,8},{1,5},{5,1},{9,13},{13,9},{2,6},{6,2},{1... | collective-permute-start | bytes 208904 | tf_op jit(solution)/shard_map/ppermute | solution.py:973
  7.0 9.8 %collective-permute-start.1 = (bf16[16,2176]{1,0:T(8,128)(2,1)}, bf16[16,2176]{1,0:T(8,128)(2,1)S(1)}, u32[]{:S(2)}, u32[]{:S(2)}) collective-permute-start(bf16[16,2176]{1,0:T(8,128)(2,1)} %get-tuple-element.212), channel_id=1, source_target_pairs={{0,8},{4,12},{8,0},{12,4},{1,9},{5,13},{9,1},{13,5},{2,10},{6,14},... | collective-permute-start | bytes 208904 | tf_op jit(solution)/shard_map/ppermute | solution.py:973
  9.6 7.2 %collective-permute-start.2 = (bf16[16,2176]{1,0:T(8,128)(2,1)}, bf16[16,2176]{1,0:T(8,128)(2,1)S(1)}, u32[]{:S(2)}, u32[]{:S(2)}) collective-permute-start(bf16[16,2176]{1,0:T(8,128)(2,1)} %get-tuple-element.213), channel_id=1, source_target_pairs={{0,12},{4,8},{8,4},{12,0},{1,13},{5,9},{9,5},{13,1},{2,14},{6,10},... | collective-permute-start | bytes 208904 | tf_op jit(solution)/shard_map/ppermute | solution.py:973
  16.9 35.4 %collective-permute-start.4 = (bf16[192,2048]{1,0:T(8,128)(2,1)S(1)}, bf16[192,2048]{1,0:T(8,128)(2,1)S(1)}, u32[]{:S(2)}, u32[]{:S(2)}) collective-permute-start(bf16[192,2048]{1,0:T(8,128)(2,1)S(1)} %copy-done), channel_id=1, source_target_pairs={{0,4},{4,0},{8,12},{12,8},{1,5},{5,1},{9,13},{13,9},{2,6},{6,2},{1... | collective-permute-start | bytes 2359304 | tf_op jit(solution)/shard_map/ppermute | solution.py:973
  17.9 36.9 %collective-permute-start.3 = (bf16[192,2048]{1,0:T(8,128)(2,1)S(1)}, bf16[192,2048]{1,0:T(8,128)(2,1)S(1)}, u32[]{:S(2)}, u32[]{:S(2)}) collective-permute-start(bf16[192,2048]{1,0:T(8,128)(2,1)S(1)} %copy-done), channel_id=1, source_target_pairs={{0,8},{4,12},{8,0},{12,4},{1,9},{5,13},{9,1},{13,5},{2,10},{6,14},... | collective-permute-start | bytes 2359304 | tf_op jit(solution)/shard_map/ppermute | solution.py:973
  54.8 24.5 %collective-permute-start.5 = (bf16[192,2048]{1,0:T(8,128)(2,1)S(1)}, bf16[192,2048]{1,0:T(8,128)(2,1)S(1)}, u32[]{:S(2)}, u32[]{:S(2)}) collective-permute-start(bf16[192,2048]{1,0:T(8,128)(2,1)S(1)} %collective-permute-done.3.refs_2_), channel_id=1, source_target_pairs={{0,4},{4,0},{8,12},{12,8},{1,5},{5,1},{9,13},{13,9},{2,6},{6,2},{1... | collective-permute-start | bytes 2359304 | tf_op jit(solution)/shard_map/ppermute | solution.py:973
  55.0 21.4 %collective-permute-start.6 = (bf16[2,16,1536]{2,1,0:T(8,128)(2,1)S(1)}, bf16[2,16,1536]{2,1,0:T(8,128)(2,1)S(1)}, u32[]{:S(2)}, u32[]{:S(2)}) collective-permute-start(bf16[2,16,1536]{2,1,0:T(8,128)(2,1)S(1)} %copy-done.48), channel_id=1, source_target_pairs={{0,4},{4,0},{8,12},{12,8},{1,5},{5,1},{9,13},{13,9},{2,6},{6,2},{1... | collective-permute-start | bytes 294920 | tf_op jit(solution)/shard_map/ppermute | solution.py:973
  56.8 19.6 %collective-permute-start.7 = (bf16[2,16,1536]{2,1,0:T(8,128)(2,1)S(1)}, bf16[2,16,1536]{2,1,0:T(8,128)(2,1)S(1)}, u32[]{:S(2)}, u32[]{:S(2)}) collective-permute-start(bf16[2,16,1536]{2,1,0:T(8,128)(2,1)S(1)} %copy-done.47), channel_id=1, source_target_pairs={{0,8},{4,12},{8,0},{12,4},{1,9},{5,13},{9,1},{13,5},{2,10},{6,14},... | collective-permute-start | bytes 294920 | tf_op jit(solution)/shard_map/ppermute | solution.py:973
  57.7 21.5 %collective-permute-start.8 = (bf16[2,16,1536]{2,1,0:T(8,128)(2,1)S(1)}, bf16[2,16,1536]{2,1,0:T(8,128)(2,1)S(1)}, u32[]{:S(2)}, u32[]{:S(2)}) collective-permute-start(bf16[2,16,1536]{2,1,0:T(8,128)(2,1)S(1)} %copy-done.46), channel_id=1, source_target_pairs={{0,12},{4,8},{8,4},{12,0},{1,13},{5,9},{9,5},{13,1},{2,14},{6,10},... | collective-permute-start | bytes 294920 | tf_op jit(solution)/shard_map/ppermute | solution.py:973
  79.3 2.1 collective-permute-start.14
  79.4 4.4 %collective-permute-start.10 = (bf16[192,2048]{1,0:T(8,128)(2,1)S(1)}, bf16[192,2048]{1,0:T(8,128)(2,1)S(1)}, u32[]{:S(2)}, u32[]{:S(2)}) collective-permute-start(bf16[192,2048]{1,0:T(8,128)(2,1)S(1)} %copy-done), channel_id=1, source_target_pairs={{0,16},{16,0},{1,17},{17,1},{2,18},{18,2},{3,19},{19,3},{4,20},{20... | collective-permute-start | bytes 2359304 | tf_op jit(solution)/shard_map/ppermute | solution.py:973
  79.9 4.4 %collective-permute-start.11 = (bf16[192,2048]{1,0:T(8,128)(2,1)S(1)}, bf16[192,2048]{1,0:T(8,128)(2,1)S(1)}, u32[]{:S(2)}, u32[]{:S(2)}) collective-permute-start(bf16[192,2048]{1,0:T(8,128)(2,1)S(1)} %collective-permute-done.4.refs_1_), channel_id=1, source_target_pairs={{0,16},{16,0},{1,17},{17,1},{2,18},{18,2},{3,19},{19,3},{4,20},{20... | collective-permute-start | bytes 2359304 | tf_op jit(solution)/shard_map/ppermute | solution.py:973
  80.0 7.3 %collective-permute-start.12 = (bf16[192,2048]{1,0:T(8,128)(2,1)S(1)}, bf16[192,2048]{1,0:T(8,128)(2,1)}, u32[]{:S(2)}, u32[]{:S(2)}) collective-permute-start(bf16[192,2048]{1,0:T(8,128)(2,1)S(1)} %collective-permute-done.3.refs_2_), channel_id=1, source_target_pairs={{0,16},{16,0},{1,17},{17,1},{2,18},{18,2},{3,19},{19,3},{4,20},{20... | collective-permute-start | bytes 2359304 | tf_op jit(solution)/shard_map/ppermute | solution.py:973
  80.4 6.9 %collective-permute-start.13 = (bf16[192,2048]{1,0:T(8,128)(2,1)S(1)}, bf16[192,2048]{1,0:T(8,128)(2,1)}, u32[]{:S(2)}, u32[]{:S(2)}) collective-permute-start(bf16[192,2048]{1,0:T(8,128)(2,1)S(1)} %collective-permute-done.5.refs_3_), channel_id=1, source_target_pairs={{0,16},{16,0},{1,17},{17,1},{2,18},{18,2},{3,19},{19,3},{4,20},{20... | collective-permute-start | bytes 2359304 | tf_op jit(solution)/shard_map/ppermute | solution.py:973
  81.4 26.2 %collective-permute-start.18 = (bf16[2,64,1536]{2,1,0:T(8,128)(2,1)}, bf16[2,64,1536]{2,1,0:T(8,128)(2,1)}, u32[]{:S(2)}, u32[]{:S(2)}) collective-permute-start(bf16[2,64,1536]{2,1,0:T(8,128)(2,1)} %pad_maximum_fusion.4.refs_18_), channel_id=1, source_target_pairs={{0,3},{1,2},{2,1},{3,0},{4,7},{5,6},{6,5},{7,4},{8,11},{9,10},{10,... | collective-permute-start | bytes 1179656 | tf_op jit(solution)/shard_map/ppermute | solution.py:973
  83.8 23.7 %collective-permute-start.17 = (bf16[2,64,1536]{2,1,0:T(8,128)(2,1)}, bf16[2,64,1536]{2,1,0:T(8,128)(2,1)S(1)}, u32[]{:S(2)}, u32[]{:S(2)}) collective-permute-start(bf16[2,64,1536]{2,1,0:T(8,128)(2,1)} %pad_maximum_fusion.4.refs_18_), channel_id=1, source_target_pairs={{0,2},{1,3},{2,0},{3,1},{4,6},{5,7},{6,4},{7,5},{8,10},{9,11},{10,... | collective-permute-start | bytes 1179656 | tf_op jit(solution)/shard_map/ppermute | solution.py:973
  85.6 22.0 %collective-permute-start.16 = (bf16[2,64,1536]{2,1,0:T(8,128)(2,1)}, bf16[2,64,1536]{2,1,0:T(8,128)(2,1)S(1)}, u32[]{:S(2)}, u32[]{:S(2)}) collective-permute-start(bf16[2,64,1536]{2,1,0:T(8,128)(2,1)} %pad_maximum_fusion.4.refs_18_), channel_id=1, source_target_pairs={{0,1},{1,0},{2,3},{3,2},{4,5},{5,4},{6,7},{7,6},{8,9},{9,8},{10,11... | collective-permute-start | bytes 1179656 | tf_op jit(solution)/shard_map/ppermute | solution.py:973
  87.3 20.2 %collective-permute-start.9 = (bf16[192,768]{1,0:T(8,128)(2,1)}, bf16[192,768]{1,0:T(8,128)(2,1)}, u32[]{:S(2)}, u32[]{:S(2)}) collective-permute-start(bf16[192,768]{1,0:T(8,128)(2,1)} %get-tuple-element.249), channel_id=1, source_target_pairs={{0,8},{4,12},{8,0},{12,4},{1,9},{5,13},{9,1},{13,5},{2,10},{6,14},... | collective-permute-start | bytes 884744 | tf_op jit(solution)/shard_map/ppermute | solution.py:973
  87.3 20.2 %collective-permute-start.15 = (bf16[192,768]{1,0:T(8,128)(2,1)}, bf16[192,768]{1,0:T(8,128)(2,1)}, u32[]{:S(2)}, u32[]{:S(2)}) collective-permute-start(bf16[192,768]{1,0:T(8,128)(2,1)} %get-tuple-element.277.refs_0_), channel_id=1, source_target_pairs={{0,4},{4,0},{8,12},{12,8},{1,5},{5,1},{9,13},{13,9},{2,6},{6,2},{1... | collective-permute-start | bytes 884744 | tf_op jit(solution)/shard_map/ppermute | solution.py:973
  107.6 8.1 %collective-permute-start.19 = (bf16[64,1536]{1,0:T(8,128)(2,1)}, bf16[64,1536]{1,0:T(8,128)(2,1)S(1)}, u32[]{:S(2)}, u32[]{:S(2)}) collective-permute-start(bf16[64,1536]{1,0:T(8,128)(2,1)} %get-tuple-element.270), channel_id=1, source_target_pairs={{0,1},{1,0},{2,3},{3,2},{4,5},{5,4},{6,7},{7,6},{8,9},{9,8},{10,11... | collective-permute-start | bytes 589832 | tf_op jit(solution)/shard_map/ppermute | solution.py:973
  108.8 9.0 %collective-permute-start.20 = (bf16[64,1536]{1,0:T(8,128)(2,1)}, bf16[64,1536]{1,0:T(8,128)(2,1)S(1)}, u32[]{:S(2)}, u32[]{:S(2)}) collective-permute-start(bf16[64,1536]{1,0:T(8,128)(2,1)} %get-tuple-element.271), channel_id=1, source_target_pairs={{0,2},{1,3},{2,0},{3,1},{4,6},{5,7},{6,4},{7,5},{8,10},{9,11},{10,... | collective-permute-start | bytes 589832 | tf_op jit(solution)/shard_map/ppermute | solution.py:973
  110.0 9.4 %collective-permute-start.21 = (bf16[64,1536]{1,0:T(8,128)(2,1)}, bf16[64,1536]{1,0:T(8,128)(2,1)S(1)}, u32[]{:S(2)}, u32[]{:S(2)}) collective-permute-start(bf16[64,1536]{1,0:T(8,128)(2,1)} %get-tuple-element.272), channel_id=1, source_target_pairs={{0,3},{1,2},{2,1},{3,0},{4,7},{5,6},{6,5},{7,4},{8,11},{9,10},{10,... | collective-permute-start | bytes 589832 | tf_op jit(solution)/shard_map/ppermute | solution.py:973
  111.2 14.6 %collective-permute-start.22 = (bf16[192,768]{1,0:T(8,128)(2,1)S(1)}, bf16[192,768]{1,0:T(8,128)(2,1)S(1)}, u32[]{:S(2)}, u32[]{:S(2)}) collective-permute-start(bf16[192,768]{1,0:T(8,128)(2,1)S(1)} %copy-done.45), channel_id=1, source_target_pairs={{0,8},{4,12},{8,0},{12,4},{1,9},{5,13},{9,1},{13,5},{2,10},{6,14},... | collective-permute-start | bytes 884744 | tf_op jit(solution)/shard_map/ppermute | solution.py:973
  111.8 14.1 %collective-permute-start.23 = (bf16[192,768]{1,0:T(8,128)(2,1)}, bf16[192,768]{1,0:T(8,128)(2,1)S(1)}, u32[]{:S(2)}, u32[]{:S(2)}) collective-permute-start(bf16[192,768]{1,0:T(8,128)(2,1)} %collective-permute-done.9.refs_4_), channel_id=1, source_target_pairs={{0,4},{4,0},{8,12},{12,8},{1,5},{5,1},{9,13},{13,9},{2,6},{6,2},{1... | collective-permute-start | bytes 884744 | tf_op jit(solution)/shard_map/ppermute | solution.py:973
  120.5 82.2 %copy-start.1 = (f32[64,1536]{1,0:T(8,128)}, f32[64,1536]{1,0:T(8,128)S(1)}, u32[]{:S(2)}) copy-start(f32[64,1536]{1,0:T(8,128)S(1)} %get-tuple-element.452.refs_4_) | copy-start | bytes 1179652
  126.0 17.2 %collective-permute-start.25 = (bf16[192,768]{1,0:T(8,128)(2,1)S(1)}, bf16[192,768]{1,0:T(8,128)(2,1)S(1)}, u32[]{:S(2)}, u32[]{:S(2)}) collective-permute-start(bf16[192,768]{1,0:T(8,128)(2,1)S(1)} %collective-permute-done.22.refs_5_), channel_id=1, source_target_pairs={{0,4},{4,0},{8,12},{12,8},{1,5},{5,1},{9,13},{13,9},{2,6},{6,2},{1... | collective-permute-start | bytes 884744 | tf_op jit(solution)/shard_map/ppermute | solution.py:973
  126.1 19.3 %collective-permute-start.26 = (bf16[192,768]{1,0:T(8,128)(2,1)S(1)}, bf16[192,768]{1,0:T(8,128)(2,1)S(1)}, u32[]{:S(2)}, u32[]{:S(2)}) collective-permute-start(bf16[192,768]{1,0:T(8,128)(2,1)S(1)} %copy-done.20), channel_id=1, source_target_pairs={{0,4},{4,0},{8,12},{12,8},{1,5},{5,1},{9,13},{13,9},{2,6},{6,2},{1... | collective-permute-start | bytes 884744 | tf_op jit(solution)/shard_map/ppermute | solution.py:973
  128.0 15.2 %collective-permute-start.24 = (bf16[64,1536]{1,0:T(8,128)(2,1)S(1)}, bf16[64,1536]{1,0:T(8,128)(2,1)S(1)}, u32[]{:S(2)}, u32[]{:S(2)}) collective-permute-start(bf16[64,1536]{1,0:T(8,128)(2,1)S(1)} %multiply_convert_fusion), channel_id=1, source_target_pairs={{0,8},{4,12},{8,0},{12,4},{1,9},{5,13},{9,1},{13,5},{2,10},{6,14},... | collective-permute-start | bytes 589832 | tf_op jit(solution)/shard_map/ppermute | solution.py:973
  128.6 17.8 %collective-permute-start.28 = (bf16[192,768]{1,0:T(8,128)(2,1)S(1)}, bf16[192,768]{1,0:T(8,128)(2,1)S(1)}, u32[]{:S(2)}, u32[]{:S(2)}) collective-permute-start(bf16[192,768]{1,0:T(8,128)(2,1)S(1)} %copy-done.20), channel_id=1, source_target_pairs={{0,16},{16,0},{1,17},{17,1},{2,18},{18,2},{3,19},{19,3},{4,20},{20... | collective-permute-start | bytes 884744 | tf_op jit(solution)/shard_map/ppermute | solution.py:973
  128.6 17.3 %collective-permute-start.27 = (bf16[192,768]{1,0:T(8,128)(2,1)S(1)}, bf16[192,768]{1,0:T(8,128)(2,1)S(1)}, u32[]{:S(2)}, u32[]{:S(2)}) collective-permute-start(bf16[192,768]{1,0:T(8,128)(2,1)S(1)} %copy-done.19), channel_id=1, source_target_pairs={{0,16},{16,0},{1,17},{17,1},{2,18},{18,2},{3,19},{19,3},{4,20},{20... | collective-permute-start | bytes 884744 | tf_op jit(solution)/shard_map/ppermute | solution.py:973
  145.4 2.2 collective-permute-start.29
  145.4 15.5 %collective-permute-start.30 = (bf16[192,768]{1,0:T(8,128)(2,1)S(1)}, bf16[192,768]{1,0:T(8,128)(2,1)S(1)}, u32[]{:S(2)}, u32[]{:S(2)}) collective-permute-start(bf16[192,768]{1,0:T(8,128)(2,1)S(1)} %collective-permute-done.26.refs_3_), channel_id=1, source_target_pairs={{0,16},{16,0},{1,17},{17,1},{2,18},{18,2},{3,19},{19,3},{4,20},{20... | collective-permute-start | bytes 884744 | tf_op jit(solution)/shard_map/ppermute | solution.py:973
  145.9 15.0 %collective-permute-start.31 = (bf16[192,768]{1,0:T(8,128)(2,1)}, bf16[192,768]{1,0:T(8,128)(2,1)S(1)}, u32[]{:S(2)}, u32[]{:S(2)}) collective-permute-start(bf16[192,768]{1,0:T(8,128)(2,1)} %collective-permute-done.9.refs_4_), channel_id=1, source_target_pairs={{0,16},{16,0},{1,17},{17,1},{2,18},{18,2},{3,19},{19,3},{4,20},{20... | collective-permute-start | bytes 884744 | tf_op jit(solution)/shard_map/ppermute | solution.py:973
  145.9 15.0 %collective-permute-start.32 = (bf16[192,768]{1,0:T(8,128)(2,1)S(1)}, bf16[192,768]{1,0:T(8,128)(2,1)S(1)}, u32[]{:S(2)}, u32[]{:S(2)}) collective-permute-start(bf16[192,768]{1,0:T(8,128)(2,1)S(1)} %collective-permute-done.22.refs_5_), channel_id=1, source_target_pairs={{0,16},{16,0},{1,17},{17,1},{2,18},{18,2},{3,19},{19,3},{4,20},{20... | collective-permute-start | bytes 884744 | tf_op jit(solution)/shard_map/ppermute | solution.py:973
  146.4 14.5 %collective-permute-start.33 = (bf16[192,768]{1,0:T(8,128)(2,1)S(1)}, bf16[192,768]{1,0:T(8,128)(2,1)S(1)}, u32[]{:S(2)}, u32[]{:S(2)}) collective-permute-start(bf16[192,768]{1,0:T(8,128)(2,1)S(1)} %collective-permute-done.23.refs_6_), channel_id=1, source_target_pairs={{0,16},{16,0},{1,17},{17,1},{2,18},{18,2},{3,19},{19,3},{4,20},{20... | collective-permute-start | bytes 884744 | tf_op jit(solution)/shard_map/ppermute | solution.py:973
  147.5 13.4 %collective-permute-start.34 = (bf16[192,768]{1,0:T(8,128)(2,1)S(1)}, bf16[192,768]{1,0:T(8,128)(2,1)S(1)}, u32[]{:S(2)}, u32[]{:S(2)}) collective-permute-start(bf16[192,768]{1,0:T(8,128)(2,1)S(1)} %collective-permute-done.25.refs_7_), channel_id=1, source_target_pairs={{0,16},{16,0},{1,17},{17,1},{2,18},{18,2},{3,19},{19,3},{4,20},{20... | collective-permute-start | bytes 884744 | tf_op jit(solution)/shard_map/ppermute | solution.py:973
  174.7 13.7 %collective-permute-start.35 = (bf16[512,3072]{1,0:T(8,128)(2,1)}, bf16[512,3072]{1,0:T(8,128)(2,1)S(1)}, u32[]{:S(2)}, u32[]{:S(2)}) collective-permute-start(bf16[512,3072]{1,0:T(8,128)(2,1)} %get-tuple-element.296), channel_id=1, source_target_pairs={{0,16},{16,0},{1,17},{17,1},{2,18},{18,2},{3,19},{19,3},{4,20},{20... | collective-permute-start | bytes 9437192 | tf_op jit(solution)/shard_map/ppermute | solution.py:973
  174.7 8.0 %collective-permute-start.36 = (bf16[64,1536]{1,0:T(8,128)(2,1)}, bf16[64,1536]{1,0:T(8,128)(2,1)S(1)}, u32[]{:S(2)}, u32[]{:S(2)}) collective-permute-start(bf16[64,1536]{1,0:T(8,128)(2,1)} %get-tuple-element.298), channel_id=1, source_target_pairs={{0,1},{1,0},{2,3},{3,2},{4,5},{5,4},{6,7},{7,6},{8,9},{9,8},{10,11... | collective-permute-start | bytes 589832 | tf_op jit(solution)/shard_map/ppermute | solution.py:973
  176.0 11.4 %collective-permute-start.37 = (bf16[64,1536]{1,0:T(8,128)(2,1)}, bf16[64,1536]{1,0:T(8,128)(2,1)S(1)}, u32[]{:S(2)}, u32[]{:S(2)}) collective-permute-start(bf16[64,1536]{1,0:T(8,128)(2,1)} %get-tuple-element.299), channel_id=1, source_target_pairs={{0,2},{1,3},{2,0},{3,1},{4,6},{5,7},{6,4},{7,5},{8,10},{9,11},{10,... | collective-permute-start | bytes 589832 | tf_op jit(solution)/shard_map/ppermute | solution.py:973
  176.8 10.5 %collective-permute-start.38 = (bf16[64,1536]{1,0:T(8,128)(2,1)}, bf16[64,1536]{1,0:T(8,128)(2,1)S(1)}, u32[]{:S(2)}, u32[]{:S(2)}) collective-permute-start(bf16[64,1536]{1,0:T(8,128)(2,1)} %get-tuple-element.300), channel_id=1, source_target_pairs={{0,3},{1,2},{2,1},{3,0},{4,7},{5,6},{6,5},{7,4},{8,11},{9,10},{10,... | collective-permute-start | bytes 589832 | tf_op jit(solution)/shard_map/ppermute | solution.py:973
  188.4 11.4 %collective-permute-start.39 = (bf16[64,1536]{1,0:T(8,128)(2,1)}, bf16[64,1536]{1,0:T(8,128)(2,1)S(1)}, u32[]{:S(2)}, u32[]{:S(2)}) collective-permute-start(bf16[64,1536]{1,0:T(8,128)(2,1)} %get-tuple-element.306), channel_id=1, source_target_pairs={{0,1},{1,0},{2,3},{3,2},{4,5},{5,4},{6,7},{7,6},{8,9},{9,8},{10,11... | collective-permute-start | bytes 589832 | tf_op jit(solution)/shard_map/ppermute | solution.py:973
  189.3 10.5 %collective-permute-start.40 = (bf16[64,1536]{1,0:T(8,128)(2,1)}, bf16[64,1536]{1,0:T(8,128)(2,1)S(1)}, u32[]{:S(2)}, u32[]{:S(2)}) collective-permute-start(bf16[64,1536]{1,0:T(8,128)(2,1)} %get-tuple-element.307), channel_id=1, source_target_pairs={{0,2},{1,3},{2,0},{3,1},{4,6},{5,7},{6,4},{7,5},{8,10},{9,11},{10,... | collective-permute-start | bytes 589832 | tf_op jit(solution)/shard_map/ppermute | solution.py:973
  190.5 9.3 %collective-permute-start.41 = (bf16[64,1536]{1,0:T(8,128)(2,1)}, bf16[64,1536]{1,0:T(8,128)(2,1)S(1)}, u32[]{:S(2)}, u32[]{:S(2)}) collective-permute-start(bf16[64,1536]{1,0:T(8,128)(2,1)} %get-tuple-element.308), channel_id=1, source_target_pairs={{0,3},{1,2},{2,1},{3,0},{4,7},{5,6},{6,5},{7,4},{8,11},{9,10},{10,... | collective-permute-start | bytes 589832 | tf_op jit(solution)/shard_map/ppermute | solution.py:973
  192.0 10.5 %collective-permute-start.42 = (bf16[64,1536]{1,0:T(8,128)(2,1)S(1)}, bf16[64,1536]{1,0:T(8,128)(2,1)S(1)}, u32[]{:S(2)}, u32[]{:S(2)}) collective-permute-start(bf16[64,1536]{1,0:T(8,128)(2,1)S(1)} %add_convert_fusion), channel_id=1, source_target_pairs={{0,8},{4,12},{8,0},{12,4},{1,9},{5,13},{9,1},{13,5},{2,10},{6,14},... | collective-permute-start | bytes 589832 | tf_op jit(solution)/shard_map/ppermute | solution.py:973
  203.7 15.1 %collective-permute-start.43 = (bf16[2,192,768]{2,1,0:T(8,128)(2,1)S(1)}, bf16[2,192,768]{2,1,0:T(8,128)(2,1)S(1)}, u32[]{:S(2)}, u32[]{:S(2)}) collective-permute-start(bf16[2,192,768]{2,1,0:T(8,128)(2,1)S(1)} %copy-done.41), channel_id=1, source_target_pairs={{0,4},{4,0},{8,12},{12,8},{1,5},{5,1},{9,13},{13,9},{2,6},{6,2},{1... | collective-permute-start | bytes 1769480 | tf_op jit(solution)/shard_map/ppermute | solution.py:973
  219.0 20.6 %collective-permute-start.44 = (bf16[2,192,768]{2,1,0:T(8,128)(2,1)S(1)}, bf16[2,192,768]{2,1,0:T(8,128)(2,1)S(1)}, u32[]{:S(2)}, u32[]{:S(2)}) collective-permute-start(bf16[2,192,768]{2,1,0:T(8,128)(2,1)S(1)} %copy-done.40), channel_id=1, source_target_pairs={{0,4},{4,0},{8,12},{12,8},{1,5},{5,1},{9,13},{13,9},{2,6},{6,2},{1... | collective-permute-start | bytes 1769480 | tf_op jit(solution)/shard_map/ppermute | solution.py:973
  219.3 20.4 %collective-permute-start.45 = (bf16[192,768]{1,0:T(8,128)(2,1)S(1)}, bf16[192,768]{1,0:T(8,128)(2,1)S(1)}, u32[]{:S(2)}, u32[]{:S(2)}) collective-permute-start(bf16[192,768]{1,0:T(8,128)(2,1)S(1)} %fusion.5), channel_id=1, source_target_pairs={{0,8},{4,12},{8,0},{12,4},{1,9},{5,13},{9,1},{13,5},{2,10},{6,14},... | collective-permute-start | bytes 884744 | tf_op jit(solution)/shard_map/ppermute | solution.py:973
  221.4 18.3 %collective-permute-start.46 = (bf16[2,64,1536]{2,1,0:T(8,128)(2,1)S(1)}, bf16[2,64,1536]{2,1,0:T(8,128)(2,1)S(1)}, u32[]{:S(2)}, u32[]{:S(2)}) collective-permute-start(bf16[2,64,1536]{2,1,0:T(8,128)(2,1)S(1)} %copy-done.44), channel_id=1, source_target_pairs={{0,1},{1,0},{2,3},{3,2},{4,5},{5,4},{6,7},{7,6},{8,9},{9,8},{10,11... | collective-permute-start | bytes 1179656 | tf_op jit(solution)/shard_map/ppermute | solution.py:973
  222.3 17.6 %collective-permute-start.47 = (bf16[2,64,1536]{2,1,0:T(8,128)(2,1)S(1)}, bf16[2,64,1536]{2,1,0:T(8,128)(2,1)S(1)}, u32[]{:S(2)}, u32[]{:S(2)}) collective-permute-start(bf16[2,64,1536]{2,1,0:T(8,128)(2,1)S(1)} %copy-done.43), channel_id=1, source_target_pairs={{0,2},{1,3},{2,0},{3,1},{4,6},{5,7},{6,4},{7,5},{8,10},{9,11},{10,... | collective-permute-start | bytes 1179656 | tf_op jit(solution)/shard_map/ppermute | solution.py:973
  223.4 16.4 %collective-permute-start.48 = (bf16[2,64,1536]{2,1,0:T(8,128)(2,1)S(1)}, bf16[2,64,1536]{2,1,0:T(8,128)(2,1)S(1)}, u32[]{:S(2)}, u32[]{:S(2)}) collective-permute-start(bf16[2,64,1536]{2,1,0:T(8,128)(2,1)S(1)} %copy-done.42), channel_id=1, source_target_pairs={{0,3},{1,2},{2,1},{3,0},{4,7},{5,6},{6,5},{7,4},{8,11},{9,10},{10,... | collective-permute-start | bytes 1179656 | tf_op jit(solution)/shard_map/ppermute | solution.py:973
  240.7 3.8 %collective-permute-start.49 = (bf16[256,3584]{1,0:T(8,128)(2,1)S(1)}, bf16[256,3584]{1,0:T(8,128)(2,1)S(1)}, u32[]{:S(2)}, u32[]{:S(2)}) collective-permute-start(bf16[256,3584]{1,0:T(8,128)(2,1)S(1)} %copy-done.39), channel_id=1, source_target_pairs={{0,16},{16,0},{1,17},{17,1},{2,18},{18,2},{3,19},{19,3},{4,20},{20... | collective-permute-start | bytes 5505032 | tf_op jit(solution)/shard_map/ppermute | solution.py:973
  250.3 30.8 %collective-permute-start.50 = (bf16[2,192,1152]{2,1,0:T(8,128)(2,1)}, bf16[2,192,1152]{2,1,0:T(8,128)(2,1)}, u32[]{:S(2)}, u32[]{:S(2)}) collective-permute-start(bf16[2,192,1152]{2,1,0:T(8,128)(2,1)} %get-tuple-element.356), channel_id=1, source_target_pairs={{0,4},{4,0},{8,12},{12,8},{1,5},{5,1},{9,13},{13,9},{2,6},{6,2},{1... | collective-permute-start | bytes 2654216 | tf_op jit(solution)/shard_map/ppermute | solution.py:973
  257.2 15.4 %all-to-all-start = ((bf16[4,64,1536]{2,1,0:T(8,128)(2,1)}), bf16[4,64,1536]{2,1,0:T(8,128)(2,1)}, u32[]{:S(2)}, u32[]{:S(2)}) async-start(bf16[4,64,1536]{2,1,0:T(8,128)(2,1)} %get-tuple-element.372), calls=%async_computation | async-start | bytes 1572864 | tf_op jit(solution)/shard_map/all_to_all | solution.py:1265
  262.3 23.5 %collective-permute-start.54 = (bf16[192,768]{1,0:T(8,128)(2,1)S(1)}, bf16[192,768]{1,0:T(8,128)(2,1)S(1)}, u32[]{:S(2)}, u32[]{:S(2)}) collective-permute-start(bf16[192,768]{1,0:T(8,128)(2,1)S(1)} %fusion.6), channel_id=1, source_target_pairs={{0,8},{4,12},{8,0},{12,4},{1,9},{5,13},{9,1},{13,5},{2,10},{6,14},... | collective-permute-start | bytes 884744 | tf_op jit(solution)/shard_map/ppermute | solution.py:973
  264.8 17.7 %collective-permute-start.51 = (bf16[32,1536]{1,0:T(8,128)(2,1)}, bf16[32,1536]{1,0:T(8,128)(2,1)S(1)}, u32[]{:S(2)}, u32[]{:S(2)}) collective-permute-start(bf16[32,1536]{1,0:T(8,128)(2,1)} %get-tuple-element.378), channel_id=1, source_target_pairs={{0,4},{4,0},{8,12},{12,8},{1,5},{5,1},{9,13},{13,9},{2,6},{6,2},{1... | collective-permute-start | bytes 294920 | tf_op jit(solution)/shard_map/ppermute | solution.py:973
  265.0 20.9 %collective-permute-start.52 = (bf16[32,1536]{1,0:T(8,128)(2,1)}, bf16[32,1536]{1,0:T(8,128)(2,1)S(1)}, u32[]{:S(2)}, u32[]{:S(2)}) collective-permute-start(bf16[32,1536]{1,0:T(8,128)(2,1)} %get-tuple-element.379), channel_id=1, source_target_pairs={{0,8},{4,12},{8,0},{12,4},{1,9},{5,13},{9,1},{13,5},{2,10},{6,14},... | collective-permute-start | bytes 294920 | tf_op jit(solution)/shard_map/ppermute | solution.py:973
  267.1 18.7 %collective-permute-start.53 = (bf16[32,1536]{1,0:T(8,128)(2,1)}, bf16[32,1536]{1,0:T(8,128)(2,1)S(1)}, u32[]{:S(2)}, u32[]{:S(2)}) collective-permute-start(bf16[32,1536]{1,0:T(8,128)(2,1)} %get-tuple-element.380), channel_id=1, source_target_pairs={{0,12},{4,8},{8,4},{12,0},{1,13},{5,9},{9,5},{13,1},{2,14},{6,10},... | collective-permute-start | bytes 294920 | tf_op jit(solution)/shard_map/ppermute | solution.py:973
  285.8 10.4 %collective-permute-start.56 = (bf16[16,1792]{1,0:T(8,128)(2,1)S(1)}, bf16[16,1792]{1,0:T(8,128)(2,1)S(1)}, u32[]{:S(2)}, u32[]{:S(2)}) collective-permute-start(bf16[16,1792]{1,0:T(8,128)(2,1)S(1)} %copy-done.51), channel_id=1, source_target_pairs={{0,4},{4,0},{8,12},{12,8},{1,5},{5,1},{9,13},{13,9},{2,6},{6,2},{1... | collective-permute-start | bytes 172040 | tf_op jit(solution)/shard_map/ppermute | solution.py:973
  287.5 16.3 %collective-permute-start.57 = (bf16[16,1792]{1,0:T(8,128)(2,1)S(1)}, bf16[16,1792]{1,0:T(8,128)(2,1)S(1)}, u32[]{:S(2)}, u32[]{:S(2)}) collective-permute-start(bf16[16,1792]{1,0:T(8,128)(2,1)S(1)} %copy-done.50), channel_id=1, source_target_pairs={{0,8},{4,12},{8,0},{12,4},{1,9},{5,13},{9,1},{13,5},{2,10},{6,14},... | collective-permute-start | bytes 172040 | tf_op jit(solution)/shard_map/ppermute | solution.py:973
  288.5 15.3 %collective-permute-start.58 = (bf16[16,1792]{1,0:T(8,128)(2,1)S(1)}, bf16[16,1792]{1,0:T(8,128)(2,1)S(1)}, u32[]{:S(2)}, u32[]{:S(2)}) collective-permute-start(bf16[16,1792]{1,0:T(8,128)(2,1)S(1)} %copy-done.49), channel_id=1, source_target_pairs={{0,12},{4,8},{8,4},{12,0},{1,13},{5,9},{9,5},{13,1},{2,14},{6,10},... | collective-permute-start | bytes 172040 | tf_op jit(solution)/shard_map/ppermute | solution.py:973
  290.3 27.8 %collective-permute-start.59 = (bf16[192,1152]{1,0:T(8,128)(2,1)S(1)}, bf16[192,1152]{1,0:T(8,128)(2,1)}, u32[]{:S(2)}, u32[]{:S(2)}) collective-permute-start(bf16[192,1152]{1,0:T(8,128)(2,1)S(1)} %fusion.3), channel_id=1, source_target_pairs={{0,8},{4,12},{8,0},{12,4},{1,9},{5,13},{9,1},{13,5},{2,10},{6,14},... | collective-permute-start | bytes 1327112 | tf_op jit(solution)/shard_map/ppermute | solution.py:973
  291.6 26.3 %collective-permute-start.55 = (bf16[2,192,896]{2,1,0:T(8,128)(2,1)}, bf16[2,192,896]{2,1,0:T(8,128)(2,1)S(1)}, u32[]{:S(2)}, u32[]{:S(2)}) collective-permute-start(bf16[2,192,896]{2,1,0:T(8,128)(2,1)} %get-tuple-element.384), channel_id=1, source_target_pairs={{0,4},{4,0},{8,12},{12,8},{1,5},{5,1},{9,13},{13,9},{2,6},{6,2},{1... | collective-permute-start | bytes 2064392 | tf_op jit(solution)/shard_map/ppermute | solution.py:973
  320.1 18.3 %collective-permute-start.60 = (f32[16,256]{1,0:T(8,128)S(1)}, f32[16,256]{1,0:T(8,128)S(1)}, u32[]{:S(2)}, u32[]{:S(2)}) collective-permute-start(f32[16,256]{1,0:T(8,128)S(1)} %copy-done.38), channel_id=1, source_target_pairs={{0,16},{16,0},{1,17},{17,1},{2,18},{18,2},{3,19},{19,3},{4,20},{20... | collective-permute-start | bytes 49160 | tf_op jit(solution)/shard_map/ppermute | solution.py:973
  320.1 20.1 %collective-permute-start.61 = (bf16[192,896]{1,0:T(8,128)(2,1)S(1)}, bf16[192,896]{1,0:T(8,128)(2,1)S(1)}, u32[]{:S(2)}, u32[]{:S(2)}) collective-permute-start(bf16[192,896]{1,0:T(8,128)(2,1)S(1)} %fusion.4), channel_id=1, source_target_pairs={{0,8},{4,12},{8,0},{12,4},{1,9},{5,13},{9,1},{13,5},{2,10},{6,14},... | collective-permute-start | bytes 1032200 | tf_op jit(solution)/shard_map/ppermute | solution.py:973
  (51 other events, 794.0 us)

commit v2 on v1

--- a/solution.py
+++ b/solution.py
@@ -1058,6 +1058,7 @@
         "v" * 6,
         2,
     )
+    x_messages, pack, output_grad = step((to_owners(token_messages), pack, output_grad))
     packed = call(
         feed_forward_pack_kernel,
         [((2, quarter, features), low)] * 4
@@ -1068,9 +1069,7 @@
         "avvv",
         3,
     )
-    x_messages, pack, grad_messages, gives, ffn_keeps = step(
-        (to_owners(token_messages), pack, packed[:4], packed[4:6], packed[6:8])
-    )
+    grad_messages, gives, ffn_keeps = packed[:4], packed[4:6], packed[6:8]
 
     pack_two, pack_one = swap(pack, "ctx", 2), swap(pack, "ctx", 1)
     x_block = jnp.concatenate([message[:, :features] for message in x_messages])
@@ -1088,17 +1087,17 @@
     )
 
     pack_three = swap(pack_two, "ctx", 1)
-    grad_messages = to_owners(grad_messages)
-    pack_three, pack_two, pack_one, pack, gains, gives, grad_messages, ffn_keeps = step(
-        (pack_three, pack_two, pack_one, pack, gains, gives, grad_messages, ffn_keeps)
-    )
-
-    attn_weights = [pack, pack_one, pack_two, pack_three]
-    attn_weights = attn_weights + [other_core(piece) for piece in attn_weights]
     gains_other = other_core(gains)
     gains = jnp.where(core == 0, jnp.stack([gains, gains_other]), jnp.stack([gains_other, gains]))
     gain_one = gains[:, :, :depth].reshape(1, features).astype(wide)
     gain_two = gains[:, :, depth:].reshape(1, features).astype(wide)
+    grad_messages = to_owners(grad_messages)
+    pack_three, pack_two, pack_one, pack, gain_one, gives, grad_messages, ffn_keeps = step(
+        (pack_three, pack_two, pack_one, pack, gain_one, gives, grad_messages, ffn_keeps)
+    )
+
+    attn_weights = [pack, pack_one, pack_two, pack_three]
+    attn_weights = attn_weights + [other_core(piece) for piece in attn_weights]
     give_two = [swap(gives[0], "ctx", 2)]
     keep_one = [swap(ffn_keeps[0], "ctx", 1)]
     grads = jnp.stack(
@@ -1238,17 +1237,6 @@
         (ffn_sums[1][1].astype(low), ffn_other, out_received, tuple(back))
     )
 
-    came, keeps, d_parts, out_received, ffn_leave = step(
-        (other_core(sends), keeps, d_parts, out_received, ffn_leave)
-    )
-
-    ffn_other = ffn_other + [swap(ffn_leave, "ctx", 2)]
-    query_start = features + 2 * width + 128
-    near_two, far_two = grads_of(
-        keeps, came, ((0, query_start, 2 * width), (1, query_start + 2 * width, width))
-    )
-    out_received, near_two, far_two, keeps = step((out_received, near_two, far_two, keeps))
-    two_came = swap(far_two, "ctx", 1)
     out_messages = call(
         out_message_kernel,
         [((2 * quarter, features), low)] * 4,
@@ -1258,7 +1246,17 @@
         "v" * 5,
         2,
     )
-    out_messages, keeps = step((tuple(out_messages), keeps))
+    came, keeps, d_parts, out_messages, ffn_leave = step(
+        (other_core(sends), keeps, d_parts, tuple(out_messages), ffn_leave)
+    )
+
+    ffn_other = ffn_other + [swap(ffn_leave, "ctx", 2)]
+    query_start = features + 2 * width + 128
+    near_two, far_two = grads_of(
+        keeps, came, ((0, query_start, 2 * width), (1, query_start + 2 * width, width))
+    )
+    out_messages, near_two, far_two, keeps = step((out_messages, near_two, far_two, keeps))
+    two_came = swap(far_two, "ctx", 1)
     out_messages = to_owners(out_messages)
     near_one, far_one = grads_of(keeps, came, ((0, features, 2 * width + 128),))
     d_parts, near_one, far_one = step((d_parts, near_one, far_one))

time: 343 us -> 338 us (0.985)
  waiting for transfers between devices: 96.8 us -> 83 us
  blocking collectives: 73.3 us -> 82.5 us
  starting transfers between devices: 69.3 us -> 65.4 us
    ppermute x62, waiting for transfers between devices: 93.5 us -> 79.2 us  [swap(): return lax.ppermute(block, axis, [(i, i ^ distance) for i in range(size)])]
    all_gather x6, blocking collectives: 73.3 us -> 82.5 us  [gathered_tp(): return lax.all_gather(block, 'tp', axis=0)]
    ppermute x62, starting transfers between devices: 64.8 us -> 61 us  [swap(): return lax.ppermute(block, axis, [(i, i ^ distance) for i in range(size)])]
  transfers between devices with their start and end apart: 63 -> 63, of which waited for: 25 -> 25; matrix products, arithmetic and copies ran while one was open for 4% -> 5% of each run, Pallas kernels for 17% -> 17%
where the time goes in v2:
time: 338 us; the launch traced here: 337 us
  waiting for transfers between devices  83 us (25%)
  blocking collectives  82.5 us (24%)
  Pallas kernels  76.7 us (23%)
  starting transfers between devices  65.4 us (19%)
  local copies, waits for them, and re-layouts  16.3 us (5%)
  other arithmetic  11 us (3%)
    all_gather x6, blocking collectives, gathered_tp(): return lax.all_gather(block, 'tp', axis=0)  82.5 us
    ppermute x62, waiting for transfers between devices, swap(): return lax.ppermute(block, axis, [(i, i ^ distance) for i in range(size)])  79.2 us
    pallas_call x14, Pallas kernels, call(): pl.pallas_call(kernel, out_shape=[jax.ShapeDtypeStruct(shape, kind) for s...  76.7 us
    ppermute x62, starting transfers between devices, swap(): return lax.ppermute(block, axis, [(i, i ^ distance) for i in range(size)])  61 us
  transfers between devices with their start and end apart: 63, of which 25 were waited for; matrix products, arithmetic and copies ran while one was open for 5% of the time, Pallas kernels for 17%

profile of v2, /device:TPU:0, one launch (start us, length us, event | category | flops | bytes accessed | tf_op | source)
XLA Modules:
  0.0 336.7 jit_solution(17459949136362504727)
XLA Ops:
  1.5 2.4 shard_map.237
  3.9 3.1 collective-permute-start
  7.0 2.6 collective-permute-start.1
  9.6 1.4 copy.32.beta
  11.0 2.2 shard_map.238.refs_0_
  13.2 1.5 collective-permute-done.1
  14.7 1.3 collective-permute-done.2
  17.0 1.7 collective-permute-start.3
  19.6 3.5 %shard_map.239 = (bf16[2,16,1536]{2,1,0:T(8,128)(2,1)}, bf16[2,16,1536]{2,1,0:T(8,128)(2,1)}, bf16[2,16,1536]{2,1,0:T(8,128)(2,1)}, bf16[2,16,1536]{2,1,0:T(8,12...) custom-call(s32[34]{0:T(128)} %concatenate.48.places, ...), custom_call_target="tpu_custom_call" | custom-call | flops 3000000 | bytes 30000 | tf_op jit(solution)/shard_map/pallas_call | solution.py:958
  23.2 12.8 %all-gather = bf16[256,1536]{1,0:T(8,128)(2,1)} all-gather(bf16[64,1536]{1,0:T(8,128)(2,1)S(1)} %pad_maximum_fusion.5.block), channel_id=2, replica_groups=mesh['fsdp'=2,'ctx'=4,'tp'=4] {'tp'}, dimensions={0}, use_global_device_ids=true | all-gather | bytes 983040 | tf_op jit(solution)/shard_map/all_gather | solution.py:977
  36.0 14.8 %collective-permute-done.4.refs_1_ = bf16[192,2048]{1,0:T(8,128)(2,1)S(1)} collective-permute-done((bf16[192,2048]{1,0:T(8,128)(2,1)}, bf16[192,2048]{1,0:T(8,128)(2,1)S(1)}, u32[]{:S(2)}, u32[]{:S(2)}) %collective-permute-start.4) | collective-permute-done | bytes 786464 | tf_op jit(solution)/shard_map/ppermute | solution.py:973
  50.8 2.9 collective-permute-start.5
  53.8 2.3 collective-permute-start.8
  56.1 2.0 collective-permute-start.9
  58.9 15.1 %collective-permute-done.7 = bf16[2,16,1536]{2,1,0:T(8,128)(2,1)} collective-permute-done((bf16[2,16,1536]{2,1,0:T(8,128)(2,1)}, bf16[2,16,1536]{2,1,0:T(8,128)(2,1)}, u32[]{:S(2)}, u32[]{:S(2)}) %collective-permute-start.7) | collective-permute-done | bytes 98336 | tf_op jit(solution)/shard_map/ppermute | solution.py:973
  74.0 1.9 collective-permute-done.9
  80.5 2.4 collective-permute-start.18
  85.8 2.4 collective-permute-start.15
  89.0 9.3 %shard_map.240 = (bf16[256,1536]{1,0:T(8,128)(2,1)}, f32[256,896]{1,0:T(8,128)}, f32[3,256,256]{2,1,0:T(8,128)}, f32[3,256,256]{2,1,0:T(8,128)}) custom-call(s32[34]{0:T(128)} %concatenate.48.places, bf16[192,2048]{1,0:T(8,128)(2,1)} %shard_map.238.refs_0_, bf16[192,2048]{1,0:T(8,128)(2,1)} %copy-done.3, bf16[192,2048]{1,0:T(8,128)(2,1)} %copy-done.4, ...), custom_call_target="tpu_custom_call" | custom-call | flops 20000000 | bytes 200000 | tf_op jit(solution)/shard_map/pallas_call | solution.py:958
  98.3 7.8 %shard_map.241 = (f32[256,768]{1,0:T(8,128)}, bf16[256,384]{1,0:T(8,128)(2,1)}, f32[3,256,256]{2,1,0:T(8,128)}, f32[3,256,256]{2,1,0:T(8,128)}, bf16[64,1536]{1,...) custom-call(s32[34]{0:T(128)} %concatenate.48.places, ...), custom_call_target="tpu_custom_call" | custom-call | flops 9000000 | bytes 90000 | tf_op jit(solution)/shard_map/pallas_call | solution.py:958
  106.2 1.6 collective-permute-start.19
  107.8 1.5 collective-permute-start.20
  111.6 2.6 collective-permute-done.19
  114.2 3.5 %collective-permute-done.20 = bf16[64,1536]{1,0:T(8,128)(2,1)S(1)} collective-permute-done((bf16[64,1536]{1,0:T(8,128)(2,1)}, bf16[64,1536]{1,0:T(8,128)(2,1)S(1)}, u32[]{:S(2)}, u32[]{:S(2)}) %collective-permute-start.20) | collective-permute-done | bytes 196640 | tf_op jit(solution)/shard_map/ppermute | solution.py:973
  117.7 1.2 multiply_reduce_fusion.2
  119.0 4.7 %collective-permute-done.22.refs_5_ = bf16[192,768]{1,0:T(8,128)(2,1)S(1)} collective-permute-done((bf16[192,768]{1,0:T(8,128)(2,1)S(1)}, bf16[192,768]{1,0:T(8,128)(2,1)S(1)}, u32[]{:S(2)}, u32[]{:S(2)}) %collective-permute-start.22) | collective-permute-done | bytes 294944 | tf_op jit(solution)/shard_map/ppermute | solution.py:973
  124.2 1.9 collective-permute-start.26
  126.7 13.2 %all-gather.1 = bf16[256,1536]{1,0:T(8,128)(2,1)} all-gather(bf16[64,1536]{1,0:T(8,128)(2,1)S(1)} %multiply_convert_fusion), channel_id=3, replica_groups=mesh['fsdp'=2,'ctx'=4,'tp'=4] {'tp'}, dimensions={0}, use_global_device_ids=true | all-gather | bytes 983040 | tf_op jit(solution)/shard_map/all_gather | solution.py:977
  140.9 2.2 collective-permute-done.26.refs_3_
  145.4 13.8 %all-gather.2 = bf16[256,1536]{1,0:T(8,128)(2,1)} all-gather(bf16[64,1536]{1,0:T(8,128)(2,1)S(1)} %collective-permute-done.24), channel_id=4, replica_groups=mesh['fsdp'=2,'ctx'=4,'tp'=4] {'tp'}, dimensions={0}, use_global_device_ids=true | all-gather | bytes 983040 | tf_op jit(solution)/shard_map/all_gather | solution.py:977
  160.4 12.7 %shard_map.242 = (bf16[64,1536]{1,0:T(8,128)(2,1)}, bf16[64,1536]{1,0:T(8,128)(2,1)}, bf16[64,1536]{1,0:T(8,128)(2,1)}, bf16[64,1536]{1,0:T(8,128)(2,1)}, bf16[6...) custom-call(s32[34]{0:T(128)} %concatenate.48.places, ...), custom_call_target="tpu_custom_call" | custom-call | flops 12000000 | bytes 120000 | tf_op jit(solution)/shard_map/pallas_call | solution.py:958
  175.2 1.5 collective-permute-start.38
  176.7 4.4 %collective-permute-done.36 = bf16[64,1536]{1,0:T(8,128)(2,1)S(1)} collective-permute-done((bf16[64,1536]{1,0:T(8,128)(2,1)}, bf16[64,1536]{1,0:T(8,128)(2,1)S(1)}, u32[]{:S(2)}, u32[]{:S(2)}) %collective-permute-start.36) | collective-permute-done | bytes 196640 | tf_op jit(solution)/shard_map/ppermute | solution.py:973
  181.1 4.4 %collective-permute-done.37 = bf16[64,1536]{1,0:T(8,128)(2,1)S(1)} collective-permute-done((bf16[64,1536]{1,0:T(8,128)(2,1)}, bf16[64,1536]{1,0:T(8,128)(2,1)S(1)}, u32[]{:S(2)}, u32[]{:S(2)}) %collective-permute-start.37) | collective-permute-done | bytes 196640 | tf_op jit(solution)/shard_map/ppermute | solution.py:973
  186.5 1.2 collective-permute-start.39
  188.6 1.5 collective-permute-start.41
  191.0 7.0 %shard_map.243 = (bf16[2,192,768]{2,1,0:T(8,128)(2,1)}, bf16[2,192,768]{2,1,0:T(8,128)(2,1)}, bf16[2,192,768]{2,1,0:T(8,128)(2,1)}, bf16[2,192,768]{2,1,0:T(8,128)(2,1)}) custom-call(s32[34]{0:T(128)} %concatenate.48.places, bf16[512,3072]{1,0:T(8,128)(2,1)} %get-tuple-element.291.mine, bf16[512,3072]{1,0:T(8,128)(2,1)} %copy-done.10), custom_call_target="tpu_custom_call" | custom-call | flops 3840000 | bytes 38400 | tf_op jit(solution)/shard_map/pallas_call | solution.py:958
  200.4 11.9 %all-gather.3 = bf16[256,1536]{1,0:T(8,128)(2,1)} all-gather(bf16[64,1536]{1,0:T(8,128)(2,1)S(1)} %get-tuple-element.298), channel_id=5, replica_groups=mesh['fsdp'=2,'ctx'=4,'tp'=4] {'tp'}, dimensions={0}, use_global_device_ids=true | all-gather | bytes 983040 | tf_op jit(solution)/shard_map/all_gather | solution.py:977
  212.3 3.2 collective-permute-done.43
  218.8 1.5 collective-permute-start.48
  220.2 14.2 %shard_map.244 = (bf16[256,3584]{1,0:T(8,128)(2,1)}, bf16[256,3584]{1,0:T(8,128)(2,1)}, bf16[4,64,1536]{2,1,0:T(8,128)(2,1)}) custom-call(s32[34]{0:T(128)} %concatenate.48.places, bf16[192,2048]{1,0:T(8,128)(2,1)} %shard_map.238.refs_0_, bf16[192,2048]{1,0:T(8,128)(2,1)} %copy-done.3, bf16[192,2048]{1,0:T(8,128)(2,1)} %copy-done.4, ...), custom_call_target="tpu_custom_call" | custom-call | flops 14000000 | bytes 140000 | tf_op jit(solution)/shard_map/pallas_call | solution.py:958
  234.5 1.8 collective-permute-done.44
  238.2 2.3 shard_map.245
  240.6 1.3 collective-permute-done.49.came
  241.8 1.3 copy-done.2
  243.1 4.6 %shard_map.246 = (bf16[2,192,1152]{2,1,0:T(8,128)(2,1)}, bf16[2,192,1152]{2,1,0:T(8,128)(2,1)}) custom-call(s32[34]{0:T(128)} %concatenate.48.places, bf16[256,3584]{1,0:T(8,128)(2,1)} %get-tuple-element.343.mine, bf16[256,3584]{1,0:T(8,128)(2,1)} %copy-done.2), custom_call_target="tpu_custom_call" | custom-call | flops 2880000 | bytes 28800 | tf_op jit(solution)/shard_map/pallas_call | solution.py:958
  247.7 4.3 %shard_map.247 = (bf16[2,192,896]{2,1,0:T(8,128)(2,1)}, bf16[2,192,896]{2,1,0:T(8,128)(2,1)}) custom-call(s32[34]{0:T(128)} %concatenate.48.places, bf16[256,3584]{1,0:T(8,128)(2,1)} %get-tuple-element.343.mine, bf16[256,3584]{1,0:T(8,128)(2,1)} %copy-done.2), custom_call_target="tpu_custom_call" | custom-call | flops 2240000 | bytes 22400 | tf_op jit(solution)/shard_map/pallas_call | solution.py:958
  252.0 4.4 %all-to-all-start = ((bf16[4,64,1536]{2,1,0:T(8,128)(2,1)}), bf16[4,64,1536]{2,1,0:T(8,128)(2,1)}, u32[]{:S(2)}, u32[]{:S(2)}) async-start(bf16[4,64,1536]{2,1,0:T(8,128)(2,1)} %get-tuple-element.348), calls=%async_computation | async-start | bytes 1572864 | tf_op jit(solution)/shard_map/all_to_all | solution.py:1263
  257.1 2.2 collective-permute-start.54
  259.8 2.3 collective-permute-start.52
  262.1 1.6 collective-permute-start.53
  263.8 3.9 %all-to-all-done.d_parts = bf16[4,64,1536]{2,1,0:T(8,128)(2,1)} async-done(((bf16[4,64,1536]{2,1,0:T(8,128)(2,1)}), bf16[4,64,1536]{2,1,0:T(8,128)(2,1)}, u32[]{:S(2)}, u32[]{:S(2)}) %all-to-all-start) | async-done | bytes 786464 | tf_op jit(solution)/shard_map/all_to_all | solution.py:1263
  267.6 2.3 shard_map.248
  269.9 9.0 %collective-permute-done.50 = bf16[2,192,1152]{2,1,0:T(8,128)(2,1)} collective-permute-done((bf16[2,192,1152]{2,1,0:T(8,128)(2,1)}, bf16[2,192,1152]{2,1,0:T(8,128)(2,1)}, u32[]{:S(2)}, u32[]{:S(2)}) %collective-permute-start.50) | collective-permute-done | bytes 884768 | tf_op jit(solution)/shard_map/ppermute | solution.py:973
  278.9 1.3 convert_add_fusion
  280.8 1.5 collective-permute-done.53
  282.4 2.6 collective-permute-start.57
  284.9 1.8 collective-permute-start.58
  286.7 2.6 collective-permute-start.55
  292.9 18.2 %all-gather.4 = bf16[256,1792]{1,0:T(8,128)(2,1)} all-gather(bf16[64,1792]{1,0:T(8,128)(2,1)S(1)} %fusion.7), channel_id=6, replica_groups=mesh['fsdp'=2,'ctx'=4,'tp'=4] {'tp'}, dimensions={0}, use_global_device_ids=true | all-gather | bytes 1146880 | tf_op jit(solution)/shard_map/all_gather | solution.py:977
  311.0 2.1 shard_map.249
  316.4 2.3 collective-permute-start.61
  318.7 12.7 %all-gather.5 = bf16[256,1536]{1,0:T(8,128)(2,1)} all-gather(bf16[64,1536]{1,0:T(8,128)(2,1)S(1)} %pad_maximum_fusion.7), channel_id=7, replica_groups=mesh['fsdp'=2,'ctx'=4,'tp'=4] {'tp'}, dimensions={0}, use_global_device_ids=true | all-gather | bytes 983040 | tf_op jit(solution)/shard_map/all_gather | solution.py:977
  331.4 2.1 shard_map.250
  (282 shorter events, 43.8 us)
Async XLA Ops:
  3.9 9.3 %collective-permute-start = (bf16[16,2176]{1,0:T(8,128)(2,1)}, bf16[16,2176]{1,0:T(8,128)(2,1)S(1)}, u32[]{:S(2)}, u32[]{:S(2)}) collective-permute-start(bf16[16,2176]{1,0:T(8,128)(2,1)} %get-tuple-element.199), channel_id=1, source_target_pairs={{0,4},{4,0},{8,12},{12,8},{1,5},{5,1},{9,13},{13,9},{2,6},{6,2},{1... | collective-permute-start | bytes 208904 | tf_op jit(solution)/shard_map/ppermute | solution.py:973
  7.0 7.7 %collective-permute-start.1 = (bf16[16,2176]{1,0:T(8,128)(2,1)}, bf16[16,2176]{1,0:T(8,128)(2,1)S(1)}, u32[]{:S(2)}, u32[]{:S(2)}) collective-permute-start(bf16[16,2176]{1,0:T(8,128)(2,1)} %get-tuple-element.200), channel_id=1, source_target_pairs={{0,8},{4,12},{8,0},{12,4},{1,9},{5,13},{9,1},{13,5},{2,10},{6,14},... | collective-permute-start | bytes 208904 | tf_op jit(solution)/shard_map/ppermute | solution.py:973
  9.6 6.4 %collective-permute-start.2 = (bf16[16,2176]{1,0:T(8,128)(2,1)}, bf16[16,2176]{1,0:T(8,128)(2,1)S(1)}, u32[]{:S(2)}, u32[]{:S(2)}) collective-permute-start(bf16[16,2176]{1,0:T(8,128)(2,1)} %get-tuple-element.201), channel_id=1, source_target_pairs={{0,12},{4,8},{8,4},{12,0},{1,13},{5,9},{9,5},{13,1},{2,14},{6,10},... | collective-permute-start | bytes 208904 | tf_op jit(solution)/shard_map/ppermute | solution.py:973
  16.2 34.6 %collective-permute-start.4 = (bf16[192,2048]{1,0:T(8,128)(2,1)}, bf16[192,2048]{1,0:T(8,128)(2,1)S(1)}, u32[]{:S(2)}, u32[]{:S(2)}) collective-permute-start(bf16[192,2048]{1,0:T(8,128)(2,1)} %shard_map.238.refs_0_), channel_id=1, source_target_pairs={{0,4},{4,0},{8,12},{12,8},{1,5},{5,1},{9,13},{13,9},{2,6},{6,2},{1... | collective-permute-start | bytes 2359304 | tf_op jit(solution)/shard_map/ppermute | solution.py:973
  17.0 33.8 %collective-permute-start.3 = (bf16[192,2048]{1,0:T(8,128)(2,1)}, bf16[192,2048]{1,0:T(8,128)(2,1)S(1)}, u32[]{:S(2)}, u32[]{:S(2)}) collective-permute-start(bf16[192,2048]{1,0:T(8,128)(2,1)} %shard_map.238.refs_0_), channel_id=1, source_target_pairs={{0,8},{4,12},{8,0},{12,4},{1,9},{5,13},{9,1},{13,5},{2,10},{6,14},... | collective-permute-start | bytes 2359304 | tf_op jit(solution)/shard_map/ppermute | solution.py:973
  50.8 25.1 %collective-permute-start.5 = (bf16[192,2048]{1,0:T(8,128)(2,1)S(1)}, bf16[192,2048]{1,0:T(8,128)(2,1)S(1)}, u32[]{:S(2)}, u32[]{:S(2)}) collective-permute-start(bf16[192,2048]{1,0:T(8,128)(2,1)S(1)} %collective-permute-done.3.refs_2_), channel_id=1, source_target_pairs={{0,4},{4,0},{8,12},{12,8},{1,5},{5,1},{9,13},{13,9},{2,6},{6,2},{1... | collective-permute-start | bytes 2359304 | tf_op jit(solution)/shard_map/ppermute | solution.py:973
  53.7 4.4 %collective-permute-start.6 = (bf16[4,384]{1,0:T(4,128)(2,1)S(1)}, bf16[4,384]{1,0:T(4,128)(2,1)S(1)}, u32[]{:S(2)}, u32[]{:S(2)}) collective-permute-start(bf16[4,384]{1,0:T(4,128)(2,1)S(1)} %pad_maximum_fusion.9), channel_id=1, source_target_pairs={{0,16},{16,0},{1,17},{17,1},{2,18},{18,2},{3,19},{19,3},{4,20},{20... | collective-permute-start | bytes 9224 | tf_op jit(solution)/shard_map/ppermute | solution.py:973
  53.7 20.3 %collective-permute-start.7 = (bf16[2,16,1536]{2,1,0:T(8,128)(2,1)}, bf16[2,16,1536]{2,1,0:T(8,128)(2,1)}, u32[]{:S(2)}, u32[]{:S(2)}) collective-permute-start(bf16[2,16,1536]{2,1,0:T(8,128)(2,1)} %get-tuple-element.221), channel_id=1, source_target_pairs={{0,4},{4,0},{8,12},{12,8},{1,5},{5,1},{9,13},{13,9},{2,6},{6,2},{1... | collective-permute-start | bytes 294920 | tf_op jit(solution)/shard_map/ppermute | solution.py:973
  53.8 20.2 %collective-permute-start.8 = (bf16[2,16,1536]{2,1,0:T(8,128)(2,1)}, bf16[2,16,1536]{2,1,0:T(8,128)(2,1)}, u32[]{:S(2)}, u32[]{:S(2)}) collective-permute-start(bf16[2,16,1536]{2,1,0:T(8,128)(2,1)} %get-tuple-element.222), channel_id=1, source_target_pairs={{0,8},{4,12},{8,0},{12,4},{1,9},{5,13},{9,1},{13,5},{2,10},{6,14},... | collective-permute-start | bytes 294920 | tf_op jit(solution)/shard_map/ppermute | solution.py:973
  56.1 19.8 %collective-permute-start.9 = (bf16[2,16,1536]{2,1,0:T(8,128)(2,1)}, bf16[2,16,1536]{2,1,0:T(8,128)(2,1)}, u32[]{:S(2)}, u32[]{:S(2)}) collective-permute-start(bf16[2,16,1536]{2,1,0:T(8,128)(2,1)} %get-tuple-element.223), channel_id=1, source_target_pairs={{0,12},{4,8},{8,4},{12,0},{1,13},{5,9},{9,5},{13,1},{2,14},{6,10},... | collective-permute-start | bytes 294920 | tf_op jit(solution)/shard_map/ppermute | solution.py:973
  77.7 5.3 %collective-permute-start.11 = (bf16[192,2048]{1,0:T(8,128)(2,1)S(1)}, bf16[192,2048]{1,0:T(8,128)(2,1)S(1)}, u32[]{:S(2)}, u32[]{:S(2)}) collective-permute-start(bf16[192,2048]{1,0:T(8,128)(2,1)S(1)} %copy-done), channel_id=1, source_target_pairs={{0,16},{16,0},{1,17},{17,1},{2,18},{18,2},{3,19},{19,3},{4,20},{20... | collective-permute-start | bytes 2359304 | tf_op jit(solution)/shard_map/ppermute | solution.py:973
  77.8 5.7 %collective-permute-start.12 = (bf16[192,2048]{1,0:T(8,128)(2,1)S(1)}, bf16[192,2048]{1,0:T(8,128)(2,1)S(1)}, u32[]{:S(2)}, u32[]{:S(2)}) collective-permute-start(bf16[192,2048]{1,0:T(8,128)(2,1)S(1)} %collective-permute-done.4.refs_1_), channel_id=1, source_target_pairs={{0,16},{16,0},{1,17},{17,1},{2,18},{18,2},{3,19},{19,3},{4,20},{20... | collective-permute-start | bytes 2359304 | tf_op jit(solution)/shard_map/ppermute | solution.py:973
  79.1 4.9 %collective-permute-start.13 = (bf16[192,2048]{1,0:T(8,128)(2,1)S(1)}, bf16[192,2048]{1,0:T(8,128)(2,1)S(1)}, u32[]{:S(2)}, u32[]{:S(2)}) collective-permute-start(bf16[192,2048]{1,0:T(8,128)(2,1)S(1)} %collective-permute-done.3.refs_2_), channel_id=1, source_target_pairs={{0,16},{16,0},{1,17},{17,1},{2,18},{18,2},{3,19},{19,3},{4,20},{20... | collective-permute-start | bytes 2359304 | tf_op jit(solution)/shard_map/ppermute | solution.py:973
  79.2 5.5 %collective-permute-start.14 = (bf16[192,2048]{1,0:T(8,128)(2,1)S(1)}, bf16[192,2048]{1,0:T(8,128)(2,1)S(1)}, u32[]{:S(2)}, u32[]{:S(2)}) collective-permute-start(bf16[192,2048]{1,0:T(8,128)(2,1)S(1)} %collective-permute-done.5.refs_3_), channel_id=1, source_target_pairs={{0,16},{16,0},{1,17},{17,1},{2,18},{18,2},{3,19},{19,3},{4,20},{20... | collective-permute-start | bytes 2359304 | tf_op jit(solution)/shard_map/ppermute | solution.py:973
  80.5 25.7 %collective-permute-start.18 = (bf16[2,64,1536]{2,1,0:T(8,128)(2,1)}, bf16[2,64,1536]{2,1,0:T(8,128)(2,1)}, u32[]{:S(2)}, u32[]{:S(2)}) collective-permute-start(bf16[2,64,1536]{2,1,0:T(8,128)(2,1)} %pad_maximum_fusion.4.refs_18_), channel_id=1, source_target_pairs={{0,3},{1,2},{2,1},{3,0},{4,7},{5,6},{6,5},{7,4},{8,11},{9,10},{10,... | collective-permute-start | bytes 1179656 | tf_op jit(solution)/shard_map/ppermute | solution.py:973
  83.0 23.2 %collective-permute-start.17 = (bf16[2,64,1536]{2,1,0:T(8,128)(2,1)}, bf16[2,64,1536]{2,1,0:T(8,128)(2,1)S(1)}, u32[]{:S(2)}, u32[]{:S(2)}) collective-permute-start(bf16[2,64,1536]{2,1,0:T(8,128)(2,1)} %pad_maximum_fusion.4.refs_18_), channel_id=1, source_target_pairs={{0,2},{1,3},{2,0},{3,1},{4,6},{5,7},{6,4},{7,5},{8,10},{9,11},{10,... | collective-permute-start | bytes 1179656 | tf_op jit(solution)/shard_map/ppermute | solution.py:973
  83.5 22.7 %collective-permute-start.16 = (bf16[2,64,1536]{2,1,0:T(8,128)(2,1)}, bf16[2,64,1536]{2,1,0:T(8,128)(2,1)S(1)}, u32[]{:S(2)}, u32[]{:S(2)}) collective-permute-start(bf16[2,64,1536]{2,1,0:T(8,128)(2,1)} %pad_maximum_fusion.4.refs_18_), channel_id=1, source_target_pairs={{0,1},{1,0},{2,3},{3,2},{4,5},{5,4},{6,7},{7,6},{8,9},{9,8},{10,11... | collective-permute-start | bytes 1179656 | tf_op jit(solution)/shard_map/ppermute | solution.py:973
  84.0 22.1 %collective-permute-start.10 = (bf16[192,768]{1,0:T(8,128)(2,1)}, bf16[192,768]{1,0:T(8,128)(2,1)}, u32[]{:S(2)}, u32[]{:S(2)}) collective-permute-start(bf16[192,768]{1,0:T(8,128)(2,1)} %get-tuple-element.230), channel_id=1, source_target_pairs={{0,8},{4,12},{8,0},{12,4},{1,9},{5,13},{9,1},{13,5},{2,10},{6,14},... | collective-permute-start | bytes 884744 | tf_op jit(solution)/shard_map/ppermute | solution.py:973
  85.8 20.3 %collective-permute-start.15 = (bf16[192,768]{1,0:T(8,128)(2,1)}, bf16[192,768]{1,0:T(8,128)(2,1)}, u32[]{:S(2)}, u32[]{:S(2)}) collective-permute-start(bf16[192,768]{1,0:T(8,128)(2,1)} %get-tuple-element.258.refs_0_), channel_id=1, source_target_pairs={{0,4},{4,0},{8,12},{12,8},{1,5},{5,1},{9,13},{13,9},{2,6},{6,2},{1... | collective-permute-start | bytes 884744 | tf_op jit(solution)/shard_map/ppermute | solution.py:973
  106.2 8.0 %collective-permute-start.19 = (bf16[64,1536]{1,0:T(8,128)(2,1)}, bf16[64,1536]{1,0:T(8,128)(2,1)S(1)}, u32[]{:S(2)}, u32[]{:S(2)}) collective-permute-start(bf16[64,1536]{1,0:T(8,128)(2,1)} %get-tuple-element.251), channel_id=1, source_target_pairs={{0,1},{1,0},{2,3},{3,2},{4,5},{5,4},{6,7},{7,6},{8,9},{9,8},{10,11... | collective-permute-start | bytes 589832 | tf_op jit(solution)/shard_map/ppermute | solution.py:973
  107.8 9.9 %collective-permute-start.20 = (bf16[64,1536]{1,0:T(8,128)(2,1)}, bf16[64,1536]{1,0:T(8,128)(2,1)S(1)}, u32[]{:S(2)}, u32[]{:S(2)}) collective-permute-start(bf16[64,1536]{1,0:T(8,128)(2,1)} %get-tuple-element.252), channel_id=1, source_target_pairs={{0,2},{1,3},{2,0},{3,1},{4,6},{5,7},{6,4},{7,5},{8,10},{9,11},{10,... | collective-permute-start | bytes 589832 | tf_op jit(solution)/shard_map/ppermute | solution.py:973
  109.3 8.4 %collective-permute-start.21 = (bf16[64,1536]{1,0:T(8,128)(2,1)}, bf16[64,1536]{1,0:T(8,128)(2,1)S(1)}, u32[]{:S(2)}, u32[]{:S(2)}) collective-permute-start(bf16[64,1536]{1,0:T(8,128)(2,1)} %get-tuple-element.253), channel_id=1, source_target_pairs={{0,3},{1,2},{2,1},{3,0},{4,7},{5,6},{6,5},{7,4},{8,11},{9,10},{10,... | collective-permute-start | bytes 589832 | tf_op jit(solution)/shard_map/ppermute | solution.py:973
  109.9 13.8 %collective-permute-start.22 = (bf16[192,768]{1,0:T(8,128)(2,1)S(1)}, bf16[192,768]{1,0:T(8,128)(2,1)S(1)}, u32[]{:S(2)}, u32[]{:S(2)}) collective-permute-start(bf16[192,768]{1,0:T(8,128)(2,1)S(1)} %copy-done.55), channel_id=1, source_target_pairs={{0,8},{4,12},{8,0},{12,4},{1,9},{5,13},{9,1},{13,5},{2,10},{6,14},... | collective-permute-start | bytes 884744 | tf_op jit(solution)/shard_map/ppermute | solution.py:973
  110.7 13.3 %collective-permute-start.23 = (bf16[192,768]{1,0:T(8,128)(2,1)}, bf16[192,768]{1,0:T(8,128)(2,1)S(1)}, u32[]{:S(2)}, u32[]{:S(2)}) collective-permute-start(bf16[192,768]{1,0:T(8,128)(2,1)} %collective-permute-done.10.refs_4_), channel_id=1, source_target_pairs={{0,4},{4,0},{8,12},{12,8},{1,5},{5,1},{9,13},{13,9},{2,6},{6,2},{1... | collective-permute-start | bytes 884744 | tf_op jit(solution)/shard_map/ppermute | solution.py:973
  118.9 80.7 %copy-start.1 = (f32[64,1536]{1,0:T(8,128)}, f32[64,1536]{1,0:T(8,128)S(1)}, u32[]{:S(2)}) copy-start(f32[64,1536]{1,0:T(8,128)S(1)} %get-tuple-element.428.refs_4_) | copy-start | bytes 1179652
  124.0 16.9 %collective-permute-start.25 = (bf16[192,768]{1,0:T(8,128)(2,1)S(1)}, bf16[192,768]{1,0:T(8,128)(2,1)S(1)}, u32[]{:S(2)}, u32[]{:S(2)}) collective-permute-start(bf16[192,768]{1,0:T(8,128)(2,1)S(1)} %collective-permute-done.22.refs_5_), channel_id=1, source_target_pairs={{0,4},{4,0},{8,12},{12,8},{1,5},{5,1},{9,13},{13,9},{2,6},{6,2},{1... | collective-permute-start | bytes 884744 | tf_op jit(solution)/shard_map/ppermute | solution.py:973
  124.2 19.0 %collective-permute-start.26 = (bf16[192,768]{1,0:T(8,128)(2,1)S(1)}, bf16[192,768]{1,0:T(8,128)(2,1)S(1)}, u32[]{:S(2)}, u32[]{:S(2)}) collective-permute-start(bf16[192,768]{1,0:T(8,128)(2,1)S(1)} %copy-done.29), channel_id=1, source_target_pairs={{0,4},{4,0},{8,12},{12,8},{1,5},{5,1},{9,13},{13,9},{2,6},{6,2},{1... | collective-permute-start | bytes 884744 | tf_op jit(solution)/shard_map/ppermute | solution.py:973
  126.1 14.9 %collective-permute-start.24 = (bf16[64,1536]{1,0:T(8,128)(2,1)S(1)}, bf16[64,1536]{1,0:T(8,128)(2,1)S(1)}, u32[]{:S(2)}, u32[]{:S(2)}) collective-permute-start(bf16[64,1536]{1,0:T(8,128)(2,1)S(1)} %multiply_convert_fusion), channel_id=1, source_target_pairs={{0,8},{4,12},{8,0},{12,4},{1,9},{5,13},{9,1},{13,5},{2,10},{6,14},... | collective-permute-start | bytes 589832 | tf_op jit(solution)/shard_map/ppermute | solution.py:973
  126.2 18.0 %collective-permute-start.28 = (bf16[192,768]{1,0:T(8,128)(2,1)S(1)}, bf16[192,768]{1,0:T(8,128)(2,1)S(1)}, u32[]{:S(2)}, u32[]{:S(2)}) collective-permute-start(bf16[192,768]{1,0:T(8,128)(2,1)S(1)} %copy-done.29), channel_id=1, source_target_pairs={{0,16},{16,0},{1,17},{17,1},{2,18},{18,2},{3,19},{19,3},{4,20},{20... | collective-permute-start | bytes 884744 | tf_op jit(solution)/shard_map/ppermute | solution.py:973
  126.2 17.5 %collective-permute-start.27 = (bf16[192,768]{1,0:T(8,128)(2,1)}, bf16[192,768]{1,0:T(8,128)(2,1)S(1)}, u32[]{:S(2)}, u32[]{:S(2)}) collective-permute-start(bf16[192,768]{1,0:T(8,128)(2,1)} %get-tuple-element.258.refs_0_), channel_id=1, source_target_pairs={{0,16},{16,0},{1,17},{17,1},{2,18},{18,2},{3,19},{19,3},{4,20},{20... | collective-permute-start | bytes 884744 | tf_op jit(solution)/shard_map/ppermute | solution.py:973
  143.1 2.2 collective-permute-start.29
  143.1 16.1 %collective-permute-start.30 = (bf16[192,768]{1,0:T(8,128)(2,1)S(1)}, bf16[192,768]{1,0:T(8,128)(2,1)S(1)}, u32[]{:S(2)}, u32[]{:S(2)}) collective-permute-start(bf16[192,768]{1,0:T(8,128)(2,1)S(1)} %collective-permute-done.26.refs_3_), channel_id=1, source_target_pairs={{0,16},{16,0},{1,17},{17,1},{2,18},{18,2},{3,19},{19,3},{4,20},{20... | collective-permute-start | bytes 884744 | tf_op jit(solution)/shard_map/ppermute | solution.py:973
  143.6 15.6 %collective-permute-start.31 = (bf16[192,768]{1,0:T(8,128)(2,1)}, bf16[192,768]{1,0:T(8,128)(2,1)S(1)}, u32[]{:S(2)}, u32[]{:S(2)}) collective-permute-start(bf16[192,768]{1,0:T(8,128)(2,1)} %collective-permute-done.10.refs_4_), channel_id=1, source_target_pairs={{0,16},{16,0},{1,17},{17,1},{2,18},{18,2},{3,19},{19,3},{4,20},{20... | collective-permute-start | bytes 884744 | tf_op jit(solution)/shard_map/ppermute | solution.py:973
  143.7 15.6 %collective-permute-start.32 = (bf16[192,768]{1,0:T(8,128)(2,1)S(1)}, bf16[192,768]{1,0:T(8,128)(2,1)S(1)}, u32[]{:S(2)}, u32[]{:S(2)}) collective-permute-start(bf16[192,768]{1,0:T(8,128)(2,1)S(1)} %collective-permute-done.22.refs_5_), channel_id=1, source_target_pairs={{0,16},{16,0},{1,17},{17,1},{2,18},{18,2},{3,19},{19,3},{4,20},{20... | collective-permute-start | bytes 884744 | tf_op jit(solution)/shard_map/ppermute | solution.py:973
  144.2 15.1 %collective-permute-start.33 = (bf16[192,768]{1,0:T(8,128)(2,1)S(1)}, bf16[192,768]{1,0:T(8,128)(2,1)S(1)}, u32[]{:S(2)}, u32[]{:S(2)}) collective-permute-start(bf16[192,768]{1,0:T(8,128)(2,1)S(1)} %collective-permute-done.23.refs_6_), channel_id=1, source_target_pairs={{0,16},{16,0},{1,17},{17,1},{2,18},{18,2},{3,19},{19,3},{4,20},{20... | collective-permute-start | bytes 884744 | tf_op jit(solution)/shard_map/ppermute | solution.py:973
  145.3 14.0 %collective-permute-start.34 = (bf16[192,768]{1,0:T(8,128)(2,1)S(1)}, bf16[192,768]{1,0:T(8,128)(2,1)S(1)}, u32[]{:S(2)}, u32[]{:S(2)}) collective-permute-start(bf16[192,768]{1,0:T(8,128)(2,1)S(1)} %collective-permute-done.25.refs_7_), channel_id=1, source_target_pairs={{0,16},{16,0},{1,17},{17,1},{2,18},{18,2},{3,19},{19,3},{4,20},{20... | collective-permute-start | bytes 884744 | tf_op jit(solution)/shard_map/ppermute | solution.py:973
  173.1 13.4 %collective-permute-start.35 = (bf16[512,3072]{1,0:T(8,128)(2,1)}, bf16[512,3072]{1,0:T(8,128)(2,1)S(1)}, u32[]{:S(2)}, u32[]{:S(2)}) collective-permute-start(bf16[512,3072]{1,0:T(8,128)(2,1)} %get-tuple-element.277), channel_id=1, source_target_pairs={{0,16},{16,0},{1,17},{17,1},{2,18},{18,2},{3,19},{19,3},{4,20},{20... | collective-permute-start | bytes 9437192 | tf_op jit(solution)/shard_map/ppermute | solution.py:973
  173.1 8.0 %collective-permute-start.36 = (bf16[64,1536]{1,0:T(8,128)(2,1)}, bf16[64,1536]{1,0:T(8,128)(2,1)S(1)}, u32[]{:S(2)}, u32[]{:S(2)}) collective-permute-start(bf16[64,1536]{1,0:T(8,128)(2,1)} %get-tuple-element.279), channel_id=1, source_target_pairs={{0,1},{1,0},{2,3},{3,2},{4,5},{5,4},{6,7},{7,6},{8,9},{9,8},{10,11... | collective-permute-start | bytes 589832 | tf_op jit(solution)/shard_map/ppermute | solution.py:973
  174.1 11.4 %collective-permute-start.37 = (bf16[64,1536]{1,0:T(8,128)(2,1)}, bf16[64,1536]{1,0:T(8,128)(2,1)S(1)}, u32[]{:S(2)}, u32[]{:S(2)}) collective-permute-start(bf16[64,1536]{1,0:T(8,128)(2,1)} %get-tuple-element.280), channel_id=1, source_target_pairs={{0,2},{1,3},{2,0},{3,1},{4,6},{5,7},{6,4},{7,5},{8,10},{9,11},{10,... | collective-permute-start | bytes 589832 | tf_op jit(solution)/shard_map/ppermute | solution.py:973
  175.2 10.2 %collective-permute-start.38 = (bf16[64,1536]{1,0:T(8,128)(2,1)}, bf16[64,1536]{1,0:T(8,128)(2,1)S(1)}, u32[]{:S(2)}, u32[]{:S(2)}) collective-permute-start(bf16[64,1536]{1,0:T(8,128)(2,1)} %get-tuple-element.281), channel_id=1, source_target_pairs={{0,3},{1,2},{2,1},{3,0},{4,7},{5,6},{6,5},{7,4},{8,11},{9,10},{10,... | collective-permute-start | bytes 589832 | tf_op jit(solution)/shard_map/ppermute | solution.py:973
  186.5 11.4 %collective-permute-start.39 = (bf16[64,1536]{1,0:T(8,128)(2,1)}, bf16[64,1536]{1,0:T(8,128)(2,1)S(1)}, u32[]{:S(2)}, u32[]{:S(2)}) collective-permute-start(bf16[64,1536]{1,0:T(8,128)(2,1)} %get-tuple-element.287), channel_id=1, source_target_pairs={{0,1},{1,0},{2,3},{3,2},{4,5},{5,4},{6,7},{7,6},{8,9},{9,8},{10,11... | collective-permute-start | bytes 589832 | tf_op jit(solution)/shard_map/ppermute | solution.py:973
  187.8 10.4 %collective-permute-start.40 = (bf16[64,1536]{1,0:T(8,128)(2,1)}, bf16[64,1536]{1,0:T(8,128)(2,1)S(1)}, u32[]{:S(2)}, u32[]{:S(2)}) collective-permute-start(bf16[64,1536]{1,0:T(8,128)(2,1)} %get-tuple-element.288), channel_id=1, source_target_pairs={{0,2},{1,3},{2,0},{3,1},{4,6},{5,7},{6,4},{7,5},{8,10},{9,11},{10,... | collective-permute-start | bytes 589832 | tf_op jit(solution)/shard_map/ppermute | solution.py:973
  188.6 9.5 %collective-permute-start.41 = (bf16[64,1536]{1,0:T(8,128)(2,1)}, bf16[64,1536]{1,0:T(8,128)(2,1)S(1)}, u32[]{:S(2)}, u32[]{:S(2)}) collective-permute-start(bf16[64,1536]{1,0:T(8,128)(2,1)} %get-tuple-element.289), channel_id=1, source_target_pairs={{0,3},{1,2},{2,1},{3,0},{4,7},{5,6},{6,5},{7,4},{8,11},{9,10},{10,... | collective-permute-start | bytes 589832 | tf_op jit(solution)/shard_map/ppermute | solution.py:973
  190.1 9.1 %collective-permute-start.42 = (bf16[64,1536]{1,0:T(8,128)(2,1)S(1)}, bf16[64,1536]{1,0:T(8,128)(2,1)S(1)}, u32[]{:S(2)}, u32[]{:S(2)}) collective-permute-start(bf16[64,1536]{1,0:T(8,128)(2,1)S(1)} %add_convert_fusion), channel_id=1, source_target_pairs={{0,8},{4,12},{8,0},{12,4},{1,9},{5,13},{9,1},{13,5},{2,10},{6,14},... | collective-permute-start | bytes 589832 | tf_op jit(solution)/shard_map/ppermute | solution.py:973
  200.4 15.1 %collective-permute-start.43 = (bf16[2,192,768]{2,1,0:T(8,128)(2,1)S(1)}, bf16[2,192,768]{2,1,0:T(8,128)(2,1)S(1)}, u32[]{:S(2)}, u32[]{:S(2)}) collective-permute-start(bf16[2,192,768]{2,1,0:T(8,128)(2,1)S(1)} %copy-done.51), channel_id=1, source_target_pairs={{0,4},{4,0},{8,12},{12,8},{1,5},{5,1},{9,13},{13,9},{2,6},{6,2},{1... | collective-permute-start | bytes 1769480 | tf_op jit(solution)/shard_map/ppermute | solution.py:973
  215.7 20.6 %collective-permute-start.44 = (bf16[2,192,768]{2,1,0:T(8,128)(2,1)S(1)}, bf16[2,192,768]{2,1,0:T(8,128)(2,1)S(1)}, u32[]{:S(2)}, u32[]{:S(2)}) collective-permute-start(bf16[2,192,768]{2,1,0:T(8,128)(2,1)S(1)} %copy-done.50), channel_id=1, source_target_pairs={{0,4},{4,0},{8,12},{12,8},{1,5},{5,1},{9,13},{13,9},{2,6},{6,2},{1... | collective-permute-start | bytes 1769480 | tf_op jit(solution)/shard_map/ppermute | solution.py:973
  216.0 21.1 %collective-permute-start.45 = (bf16[192,768]{1,0:T(8,128)(2,1)S(1)}, bf16[192,768]{1,0:T(8,128)(2,1)S(1)}, u32[]{:S(2)}, u32[]{:S(2)}) collective-permute-start(bf16[192,768]{1,0:T(8,128)(2,1)S(1)} %fusion.5), channel_id=1, source_target_pairs={{0,8},{4,12},{8,0},{12,4},{1,9},{5,13},{9,1},{13,5},{2,10},{6,14},... | collective-permute-start | bytes 884744 | tf_op jit(solution)/shard_map/ppermute | solution.py:973
  216.8 20.4 %collective-permute-start.46 = (bf16[2,64,1536]{2,1,0:T(8,128)(2,1)S(1)}, bf16[2,64,1536]{2,1,0:T(8,128)(2,1)S(1)}, u32[]{:S(2)}, u32[]{:S(2)}) collective-permute-start(bf16[2,64,1536]{2,1,0:T(8,128)(2,1)S(1)} %copy-done.54), channel_id=1, source_target_pairs={{0,1},{1,0},{2,3},{3,2},{4,5},{5,4},{6,7},{7,6},{8,9},{9,8},{10,11... | collective-permute-start | bytes 1179656 | tf_op jit(solution)/shard_map/ppermute | solution.py:973
  217.9 19.3 %collective-permute-start.47 = (bf16[2,64,1536]{2,1,0:T(8,128)(2,1)S(1)}, bf16[2,64,1536]{2,1,0:T(8,128)(2,1)S(1)}, u32[]{:S(2)}, u32[]{:S(2)}) collective-permute-start(bf16[2,64,1536]{2,1,0:T(8,128)(2,1)S(1)} %copy-done.53), channel_id=1, source_target_pairs={{0,2},{1,3},{2,0},{3,1},{4,6},{5,7},{6,4},{7,5},{8,10},{9,11},{10,... | collective-permute-start | bytes 1179656 | tf_op jit(solution)/shard_map/ppermute | solution.py:973
  218.8 18.4 %collective-permute-start.48 = (bf16[2,64,1536]{2,1,0:T(8,128)(2,1)S(1)}, bf16[2,64,1536]{2,1,0:T(8,128)(2,1)S(1)}, u32[]{:S(2)}, u32[]{:S(2)}) collective-permute-start(bf16[2,64,1536]{2,1,0:T(8,128)(2,1)S(1)} %copy-done.52), channel_id=1, source_target_pairs={{0,3},{1,2},{2,1},{3,0},{4,7},{5,6},{6,5},{7,4},{8,11},{9,10},{10,... | collective-permute-start | bytes 1179656 | tf_op jit(solution)/shard_map/ppermute | solution.py:973
  237.9 4.0 %collective-permute-start.49 = (bf16[256,3584]{1,0:T(8,128)(2,1)}, bf16[256,3584]{1,0:T(8,128)(2,1)S(1)}, u32[]{:S(2)}, u32[]{:S(2)}) collective-permute-start(bf16[256,3584]{1,0:T(8,128)(2,1)} %get-tuple-element.320), channel_id=1, source_target_pairs={{0,16},{16,0},{1,17},{17,1},{2,18},{18,2},{3,19},{19,3},{4,20},{20... | collective-permute-start | bytes 5505032 | tf_op jit(solution)/shard_map/ppermute | solution.py:973
  247.7 31.2 %collective-permute-start.50 = (bf16[2,192,1152]{2,1,0:T(8,128)(2,1)}, bf16[2,192,1152]{2,1,0:T(8,128)(2,1)}, u32[]{:S(2)}, u32[]{:S(2)}) collective-permute-start(bf16[2,192,1152]{2,1,0:T(8,128)(2,1)} %get-tuple-element.341), channel_id=1, source_target_pairs={{0,4},{4,0},{8,12},{12,8},{1,5},{5,1},{9,13},{13,9},{2,6},{6,2},{1... | collective-permute-start | bytes 2654216 | tf_op jit(solution)/shard_map/ppermute | solution.py:973
  252.0 15.7 %all-to-all-start = ((bf16[4,64,1536]{2,1,0:T(8,128)(2,1)}), bf16[4,64,1536]{2,1,0:T(8,128)(2,1)}, u32[]{:S(2)}, u32[]{:S(2)}) async-start(bf16[4,64,1536]{2,1,0:T(8,128)(2,1)} %get-tuple-element.348), calls=%async_computation | async-start | bytes 1572864 | tf_op jit(solution)/shard_map/all_to_all | solution.py:1263
  257.1 25.2 %collective-permute-start.54 = (bf16[192,768]{1,0:T(8,128)(2,1)}, bf16[192,768]{1,0:T(8,128)(2,1)S(1)}, u32[]{:S(2)}, u32[]{:S(2)}) collective-permute-start(bf16[192,768]{1,0:T(8,128)(2,1)} %fusion.6), channel_id=1, source_target_pairs={{0,8},{4,12},{8,0},{12,4},{1,9},{5,13},{9,1},{13,5},{2,10},{6,14},... | collective-permute-start | bytes 884744 | tf_op jit(solution)/shard_map/ppermute | solution.py:973
  259.4 21.4 %collective-permute-start.51 = (bf16[32,1536]{1,0:T(8,128)(2,1)}, bf16[32,1536]{1,0:T(8,128)(2,1)S(1)}, u32[]{:S(2)}, u32[]{:S(2)}) collective-permute-start(bf16[32,1536]{1,0:T(8,128)(2,1)} %get-tuple-element.354), channel_id=1, source_target_pairs={{0,4},{4,0},{8,12},{12,8},{1,5},{5,1},{9,13},{13,9},{2,6},{6,2},{1... | collective-permute-start | bytes 294920 | tf_op jit(solution)/shard_map/ppermute | solution.py:973
  259.8 21.0 %collective-permute-start.52 = (bf16[32,1536]{1,0:T(8,128)(2,1)}, bf16[32,1536]{1,0:T(8,128)(2,1)S(1)}, u32[]{:S(2)}, u32[]{:S(2)}) collective-permute-start(bf16[32,1536]{1,0:T(8,128)(2,1)} %get-tuple-element.355), channel_id=1, source_target_pairs={{0,8},{4,12},{8,0},{12,4},{1,9},{5,13},{9,1},{13,5},{2,10},{6,14},... | collective-permute-start | bytes 294920 | tf_op jit(solution)/shard_map/ppermute | solution.py:973
  262.1 20.2 %collective-permute-start.53 = (bf16[32,1536]{1,0:T(8,128)(2,1)S(1)}, bf16[32,1536]{1,0:T(8,128)(2,1)S(1)}, u32[]{:S(2)}, u32[]{:S(2)}) collective-permute-start(bf16[32,1536]{1,0:T(8,128)(2,1)S(1)} %copy-done.56), channel_id=1, source_target_pairs={{0,12},{4,8},{8,4},{12,0},{1,13},{5,9},{9,5},{13,1},{2,14},{6,10},... | collective-permute-start | bytes 294920 | tf_op jit(solution)/shard_map/ppermute | solution.py:973
  282.3 10.4 %collective-permute-start.56 = (bf16[16,1792]{1,0:T(8,128)(2,1)S(1)}, bf16[16,1792]{1,0:T(8,128)(2,1)S(1)}, u32[]{:S(2)}, u32[]{:S(2)}) collective-permute-start(bf16[16,1792]{1,0:T(8,128)(2,1)S(1)} %copy-done.59), channel_id=1, source_target_pairs={{0,4},{4,0},{8,12},{12,8},{1,5},{5,1},{9,13},{13,9},{2,6},{6,2},{1... | collective-permute-start | bytes 172040 | tf_op jit(solution)/shard_map/ppermute | solution.py:973
  282.4 10.4 %collective-permute-start.57 = (bf16[16,1792]{1,0:T(8,128)(2,1)S(1)}, bf16[16,1792]{1,0:T(8,128)(2,1)S(1)}, u32[]{:S(2)}, u32[]{:S(2)}) collective-permute-start(bf16[16,1792]{1,0:T(8,128)(2,1)S(1)} %copy-done.58), channel_id=1, source_target_pairs={{0,8},{4,12},{8,0},{12,4},{1,9},{5,13},{9,1},{13,5},{2,10},{6,14},... | collective-permute-start | bytes 172040 | tf_op jit(solution)/shard_map/ppermute | solution.py:973
  284.9 7.8 %collective-permute-start.58 = (bf16[16,1792]{1,0:T(8,128)(2,1)S(1)}, bf16[16,1792]{1,0:T(8,128)(2,1)S(1)}, u32[]{:S(2)}, u32[]{:S(2)}) collective-permute-start(bf16[16,1792]{1,0:T(8,128)(2,1)S(1)} %copy-done.57), channel_id=1, source_target_pairs={{0,12},{4,8},{8,4},{12,0},{1,13},{5,9},{9,5},{13,1},{2,14},{6,10},... | collective-permute-start | bytes 172040 | tf_op jit(solution)/shard_map/ppermute | solution.py:973
  286.7 27.6 %collective-permute-start.59 = (bf16[192,1152]{1,0:T(8,128)(2,1)S(1)}, bf16[192,1152]{1,0:T(8,128)(2,1)}, u32[]{:S(2)}, u32[]{:S(2)}) collective-permute-start(bf16[192,1152]{1,0:T(8,128)(2,1)S(1)} %fusion.3), channel_id=1, source_target_pairs={{0,8},{4,12},{8,0},{12,4},{1,9},{5,13},{9,1},{13,5},{2,10},{6,14},... | collective-permute-start | bytes 1327112 | tf_op jit(solution)/shard_map/ppermute | solution.py:973
  286.7 27.4 %collective-permute-start.55 = (bf16[2,192,896]{2,1,0:T(8,128)(2,1)}, bf16[2,192,896]{2,1,0:T(8,128)(2,1)S(1)}, u32[]{:S(2)}, u32[]{:S(2)}) collective-permute-start(bf16[2,192,896]{2,1,0:T(8,128)(2,1)} %get-tuple-element.360), channel_id=1, source_target_pairs={{0,4},{4,0},{8,12},{12,8},{1,5},{5,1},{9,13},{13,9},{2,6},{6,2},{1... | collective-permute-start | bytes 2064392 | tf_op jit(solution)/shard_map/ppermute | solution.py:973
  316.4 17.1 %collective-permute-start.60 = (f32[16,256]{1,0:T(8,128)S(1)}, f32[16,256]{1,0:T(8,128)S(1)}, u32[]{:S(2)}, u32[]{:S(2)}) collective-permute-start(f32[16,256]{1,0:T(8,128)S(1)} %copy-done.49), channel_id=1, source_target_pairs={{0,16},{16,0},{1,17},{17,1},{2,18},{18,2},{3,19},{19,3},{4,20},{20... | collective-permute-start | bytes 49160 | tf_op jit(solution)/shard_map/ppermute | solution.py:973
  316.4 18.7 %collective-permute-start.61 = (bf16[192,896]{1,0:T(8,128)(2,1)S(1)}, bf16[192,896]{1,0:T(8,128)(2,1)S(1)}, u32[]{:S(2)}, u32[]{:S(2)}) collective-permute-start(bf16[192,896]{1,0:T(8,128)(2,1)S(1)} %fusion.4), channel_id=1, source_target_pairs={{0,8},{4,12},{8,0},{12,4},{1,9},{5,13},{9,1},{13,5},{2,10},{6,14},... | collective-permute-start | bytes 1032200 | tf_op jit(solution)/shard_map/ppermute | solution.py:973
  (59 other events, 858.6 us)

commit v3 on v2

--- a/solution.py
+++ b/solution.py
@@ -817,61 +817,84 @@
     split_tokens(total, parts, places)
 
 
+def token_copies(gathered, whole, rows):
+    return [
+        (gathered[s].at[n], whole.at[pl.ds((s * 4 + n) * rows, rows)]) for s in range(2) for n in range(4)
+    ]
+
+
+def exchanged_copies(pieces, whole, places, rows):
+    return [
+        (pieces[n].at[s], whole.at[token_block(places, s, n, rows)]) for n in range(4) for s in range(2)
+    ]
+
+
+def token_block(places, s, n, rows):
+    return pl.ds(pl.multiple_of(places[8 + n] * 4 + s * 4 * rows, 64), rows)
+
+
 def feed_forward_kernel(places, *refs):
     weights, ins, grads = refs[0:16], refs[16:18], refs[18:22]
-    two_parts, out_parts, keeps, sends = refs[22:30], refs[30:34], refs[34], refs[35]
-    w_all, in_all, grad_all, total, weight_sems, in_sems, grad_sems = refs[36:43]
-    rows, units, half = two_parts[0].shape[0], w_all.shape[1] // 3, w_all.shape[0] // 2
-
-    def block(s, n):
-        return pl.ds(pl.multiple_of(places[8 + n] * 4 + s * 4 * rows, 64), rows)
-
+    two_parts, common = refs[22:30], refs[30]
+    w_all, in_all, grad_all, total, weight_sems, in_sems, grad_sems = refs[31:38]
+    rows, units = two_parts[0].shape[0], w_all.shape[1] // 3
     depth, part = weights[0].shape[0], w_all.shape[1] // 2
     w_pairs = []
     for n in range(16):
         row = pl.ds(pl.multiple_of(places[n // 2], 64), depth)
         w_pairs.append((weights[n], w_all.at[row, pl.ds(n % 2 * part, part)]))
     w_copies = started(w_pairs, weight_sems)
-    grad_copies = started(
-        [
-            (grads[n].at[s], grad_all.at[block(s, n)])
-            for n in range(4)
-            for s in range(2)
-        ],
-        grad_sems,
-    )
-    in_copies = started(
-        [(ins[s].at[n], in_all.at[pl.ds((s * 4 + n) * rows, rows)]) for s in range(2) for n in range(4)],
-        in_sems,
-    )
-    for copy in w_copies + grad_copies + in_copies:
+    grad_copies = started(exchanged_copies(grads, grad_all, places, rows), grad_sems)
+    in_copies = started(token_copies(ins, in_all, rows), in_sems)
+    for copy in w_copies + in_copies:
         copy.wait()
     both = mm(in_all[...], w_all[:, : 2 * units])
+    for copy in grad_copies:
+        copy.wait()
     d_hidden = mm(grad_all[...], w_all[:, 2 * units :])
     gate, up = both[:, :units], both[:, units:]
     sigmoid = jax.nn.sigmoid(gate)
     silu = gate * sigmoid
-    hidden = (silu * up).astype(jnp.bfloat16)
-    d_gate = (d_hidden * up * sigmoid * (1.0 + gate * (1.0 - sigmoid))).astype(jnp.bfloat16)
-    d_up = (d_hidden * silu).astype(jnp.bfloat16)
-    for target in (keeps, sends):
-        at = 2 * half
-        for value in (d_gate, d_up, hidden):
-            target[:, at : at + units] = value
-            at += units
-    d_both = keeps[:, 2 * half : 2 * half + 2 * units]
-    total[...] = mm(d_both, w_all[:, : 2 * units], ABT).astype(jnp.bfloat16)
+    d_gate = d_hidden * up * sigmoid * (1.0 + gate * (1.0 - sigmoid))
+    for n, value in enumerate((d_gate, d_hidden * silu, silu * up)):
+        common[:, n * units : (n + 1) * units] = value.astype(jnp.bfloat16)
+    total[...] = mm(common[:, : 2 * units], w_all[:, : 2 * units], ABT).astype(jnp.bfloat16)
     for s in range(2):
         for n in range(4):
-            two_parts[s * 4 + n][...] = total[block(s, n)]
-    total[...] = mm(hidden, w_all[:, 2 * units :], ABT).astype(jnp.bfloat16)
+            two_parts[s * 4 + n][...] = total[token_block(places, s, n, rows)]
+
+
+def feed_forward_rest_kernel(places, *refs):
+    weights, ins, grads, common = refs[0:8], refs[8:10], refs[10:14], refs[14]
+    out_parts, mine, other = refs[15:19], refs[19], refs[20]
+    w_all, in_all, grad_all, total, weight_sems, in_sems, grad_sems = refs[21:28]
+    rows, units = out_parts[0].shape[1], w_all.shape[1]
+    depth, half = weights[0].shape[0], w_all.shape[0] // 2
+    lanes = pl.ds(weights[0].shape[1] - units, units)
+    w_copies = started(
+        [
+            (
+                weights[n].at[:, lanes],
+                w_all.at[pl.ds(pl.multiple_of(places[n], 64), depth)],
+            )
+            for n in range(8)
+        ],
+        weight_sems,
+    )
+    grad_copies = started(exchanged_copies(grads, grad_all, places, rows), grad_sems)
+    in_copies = started(token_copies(ins, in_all, rows), in_sems)
+    for copy in in_copies + grad_copies:
+        copy.wait()
+    for target, place in ((other, 13), (mine, 12)):
+        at = pl.ds(pl.multiple_of(places[place], 128), half)
+        target[:, :half] = in_all[:, at]
+        target[:, half:] = grad_all[:, at]
+    for copy in w_copies:
+        copy.wait()
+    total[...] = mm(common[:, 2 * units :], w_all[...], ABT).astype(jnp.bfloat16)
     for s in range(2):
         for n in range(4):
-            out_parts[n][s] = total[block(s, n)]
-    for target, place in ((keeps, 12), (sends, 13)):
-        lanes = pl.ds(pl.multiple_of(places[place], 128), half)
-        target[:, :half] = in_all[:, lanes]
-        target[:, half : 2 * half] = grad_all[:, lanes]
+            out_parts[n][s] = total[token_block(places, s, n, rows)]
 
 
 def attention_backward_kernel(heads, places, *refs):
@@ -931,13 +954,15 @@
             parts[n, k * quarter : (k + 1) * quarter] = total[rows]
 
 
-def weight_grad_kernel(groups, places, mine, came, *refs):
-    outs, total = refs[:-1], refs[-1]
+def weight_grad_kernel(groups, count, places, *refs):
+    mine, came, outs, total = refs[0:count], refs[count : 2 * count], refs[2 * count : -1], refs[-1]
+    right = count - 1
     half, at = total.shape[0], 0
     for left, start, width in groups:
         lefts, rights = slice(left * half, (left + 1) * half), slice(start, start + width)
         total[:, at : at + width] = (
-            mm(mine[:, lefts], mine[:, rights], ATB) + mm(came[:, lefts], came[:, rights], ATB)
+            mm(mine[0][:, lefts], mine[right][:, rights], ATB)
+            + mm(came[0][:, lefts], came[right][:, rights], ATB)
         ).astype(jnp.bfloat16)
         at += width
     depth, at = outs[0].shape[1], 0
@@ -1163,7 +1188,7 @@
     pair = ((2, rows, features), low)
     outs = call(
         feed_forward_kernel,
-        [((rows, features), low)] * 8 + [pair] * 4 + [((tokens, features + 3 * units), low)] * 2,
+        [((rows, features), low)] * 8 + [((tokens, 3 * units), low)],
         [
             pltpu.VMEM((features, 3 * units), low),
             pltpu.VMEM((tokens, features), low),
@@ -1178,29 +1203,51 @@
         "a" * 22,
         12,
     )
-    own_parts, pair_parts, out_parts, keeps, sends = outs[:4], outs[4:8], outs[8:12], outs[12], outs[13]
+    own_parts, pair_parts, common = outs[:4], outs[4:8], outs[8]
+    rest = call(
+        feed_forward_rest_kernel,
+        [pair] * 4 + [((tokens, features), low)] * 2,
+        [
+            pltpu.VMEM((features, units), low),
+            pltpu.VMEM((tokens, features), low),
+            pltpu.VMEM((tokens, features), low),
+            pltpu.VMEM((tokens, features), low),
+            pltpu.SemaphoreType.DMA((8,)),
+            pltpu.SemaphoreType.DMA((8,)),
+            pltpu.SemaphoreType.DMA((8,)),
+        ],
+        places,
+        [*ffn_weights[1::2], h_own, h_pair, *grad_pieces, common],
+        "a" * 14 + "v",
+        4,
+    )
+    out_parts, keeps, sends = rest[:4], rest[4], rest[5]
 
     def grads_of(mine, came, groups, pieces=1):
         total = sum(group[2] for group in groups)
         return call(
-            functools.partial(weight_grad_kernel, groups),
+            functools.partial(weight_grad_kernel, groups, len(mine)),
             [((2, depth, total // pieces), low)] * (2 * pieces),
             [pltpu.VMEM((half, total), low)],
             places,
-            [mine, came],
-            "vv",
+            [*mine, *came],
+            "v" * (2 * len(mine)),
             total / 400.0,
         )
 
     pair_sum = add_up(sum_tp(pair_parts)).astype(low)
-    came, pair_sum, own_parts = step((other_core(sends), pair_sum, own_parts))
+    common_came, pair_sum, own_parts, keeps, sends, out_parts = step(
+        (other_core(common), pair_sum, own_parts, keeps, sends, out_parts)
+    )
+    came = (other_core(sends), common_came)
 
     two_other = swap(pair_sum, "ctx", 2)
-    own_sum = add_up(sum_tp(own_parts))
+    own_received = sum_tp(own_parts)
     ffn_grads = grads_of(
-        keeps, came, ((0, features, 2 * units), (1, features + 2 * units, units)), 2
-    )
-    d_two = own_sum + two_other.astype(wide)
+        (keeps, common), came, ((0, 0, 2 * units), (1, 2 * units, units)), 2
+    )
+    own_received, two_other, ffn_grads = step((own_received, two_other, tuple(ffn_grads)))
+    d_two = add_up(own_received + [two_other])
     gain_two_grad = jnp.sum(d_two * normed_two, axis=0, keepdims=True)
     d_middle = own_grad.astype(wide) + norm_back(d_two, normed_two, factor_two, gain_two)
     d_low, ffn_grads = step((d_middle.astype(low), tuple(ffn_grads)))
@@ -1253,12 +1300,12 @@
     ffn_other = ffn_other + [swap(ffn_leave, "ctx", 2)]
     query_start = features + 2 * width + 128
     near_two, far_two = grads_of(
-        keeps, came, ((0, query_start, 2 * width), (1, query_start + 2 * width, width))
+        (keeps,), (came,), ((0, query_start, 2 * width), (1, query_start + 2 * width, width))
     )
     out_messages, near_two, far_two, keeps = step((out_messages, near_two, far_two, keeps))
     two_came = swap(far_two, "ctx", 1)
     out_messages = to_owners(out_messages)
-    near_one, far_one = grads_of(keeps, came, ((0, features, 2 * width + 128),))
+    near_one, far_one = grads_of((keeps,), (came,), ((0, features, 2 * width + 128),))
     d_parts, near_one, far_one = step((d_parts, near_one, far_one))
     d_received = lax.all_to_all(d_parts, "tp", 0, 0)
     messages = call(

time: 338 us -> 332 us (0.982)
  blocking collectives: 82.5 us -> 76.1 us
  Pallas kernels: 76.7 us -> 81.7 us
    all_gather x6, blocking collectives: 82.5 us -> 76.1 us  [gathered_tp(): return lax.all_gather(block, 'tp', axis=0)]
    pallas_call x14 -> x15, Pallas kernels: 76.7 us -> 81.7 us  [call(): pl.pallas_call(kernel, out_shape=[jax.ShapeDtypeStruct(shape, kind) for s...]
    ppermute x62 -> x63, waiting for transfers between devices: 79.2 us -> 77.7 us  [swap(): return lax.ppermute(block, axis, [(i, i ^ distance) for i in range(size)])]
    ppermute x62 -> x63, starting transfers between devices: 61 us -> 62.4 us  [swap(): return lax.ppermute(block, axis, [(i, i ^ distance) for i in range(size)])]
    unnamed x122 -> x148, local copies, waits for them, and re-layouts: 6.66 us -> 7.6 us
  transfers between devices with their start and end apart: 63 -> 64, of which waited for: 25 -> 23; matrix products, arithmetic and copies ran while one was open for 5% -> 4% of each run, Pallas kernels for 17% -> 19%
where the time goes in v3:
time: 332 us; the launch traced here: 331 us
  Pallas kernels  81.7 us (25%)
  waiting for transfers between devices  80.8 us (24%)
  blocking collectives  76.1 us (23%)
  starting transfers between devices  66.9 us (20%)
  local copies, waits for them, and re-layouts  14.5 us (4%)
  other arithmetic  9.29 us (3%)
    pallas_call x15, Pallas kernels, call(): pl.pallas_call(kernel, out_shape=[jax.ShapeDtypeStruct(shape, kind) for s...  81.7 us
    ppermute x63, waiting for transfers between devices, swap(): return lax.ppermute(block, axis, [(i, i ^ distance) for i in range(size)])  77.7 us
    all_gather x6, blocking collectives, gathered_tp(): return lax.all_gather(block, 'tp', axis=0)  76.1 us
    ppermute x63, starting transfers between devices, swap(): return lax.ppermute(block, axis, [(i, i ^ distance) for i in range(size)])  62.4 us
    unnamed x148, local copies, waits for them, and re-layouts  7.6 us
  transfers between devices with their start and end apart: 64, of which 23 were waited for; matrix products, arithmetic and copies ran while one was open for 4% of the time, Pallas kernels for 19%

profile of v3, /device:TPU:0, one launch (start us, length us, event | category | flops | bytes accessed | tf_op | source)
XLA Modules:
  0.0 331.4 jit_solution(15684426108959249460)
XLA Ops:
  1.5 2.4 shard_map.237
  3.9 3.1 collective-permute-start
  7.0 2.6 collective-permute-start.1
  9.6 1.4 copy.32.beta
  11.0 2.2 shard_map.238.refs_0_
  13.2 1.5 collective-permute-done.1
  14.7 1.3 collective-permute-done.2
  17.0 1.7 collective-permute-start.3
  20.2 3.4 %shard_map.239 = (bf16[2,16,1536]{2,1,0:T(8,128)(2,1)}, bf16[2,16,1536]{2,1,0:T(8,128)(2,1)}, bf16[2,16,1536]{2,1,0:T(8,128)(2,1)}, bf16[2,16,1536]{2,1,0:T(8,12...) custom-call(s32[34]{0:T(128)} %concatenate.48.places, ...), custom_call_target="tpu_custom_call" | custom-call | flops 3000000 | bytes 30000 | tf_op jit(solution)/shard_map/pallas_call | solution.py:983
  23.8 12.8 %all-gather = bf16[256,1536]{1,0:T(8,128)(2,1)} all-gather(bf16[64,1536]{1,0:T(8,128)(2,1)S(1)} %pad_maximum_fusion.5.block), channel_id=2, replica_groups=mesh['fsdp'=2,'ctx'=4,'tp'=4] {'tp'}, dimensions={0}, use_global_device_ids=true | all-gather | bytes 983040 | tf_op jit(solution)/shard_map/all_gather | solution.py:1002
  36.5 14.2 %collective-permute-done.4.refs_1_ = bf16[192,2048]{1,0:T(8,128)(2,1)S(1)} collective-permute-done((bf16[192,2048]{1,0:T(8,128)(2,1)}, bf16[192,2048]{1,0:T(8,128)(2,1)S(1)}, u32[]{:S(2)}, u32[]{:S(2)}) %collective-permute-start.4) | collective-permute-done | bytes 786464 | tf_op jit(solution)/shard_map/ppermute | solution.py:998
  50.8 2.9 collective-permute-start.5
  53.9 2.3 collective-permute-start.8
  56.2 2.0 collective-permute-start.9
  58.9 15.0 %collective-permute-done.7 = bf16[2,16,1536]{2,1,0:T(8,128)(2,1)S(1)} collective-permute-done((bf16[2,16,1536]{2,1,0:T(8,128)(2,1)}, bf16[2,16,1536]{2,1,0:T(8,128)(2,1)S(1)}, u32[]{:S(2)}, u32[]{:S(2)}) %collective-permute-start.7) | collective-permute-done | bytes 98336 | tf_op jit(solution)/shard_map/ppermute | solution.py:998
  73.9 1.9 collective-permute-done.9
  77.2 2.5 collective-permute-start.18
  83.0 2.4 collective-permute-start.15
  86.3 9.2 %shard_map.240 = (bf16[256,1536]{1,0:T(8,128)(2,1)}, f32[256,896]{1,0:T(8,128)}, f32[3,256,256]{2,1,0:T(8,128)}, f32[3,256,256]{2,1,0:T(8,128)}) custom-call(s32[34]{0:T(128)} %concatenate.48.places, bf16[192,2048]{1,0:T(8,128)(2,1)} %shard_map.238.refs_0_, bf16[192,2048]{1,0:T(8,128)(2,1)} %copy-done.3, bf16[192,2048]{1,0:T(8,128)(2,1)} %copy-done.4, ...), custom_call_target="tpu_custom_call" | custom-call | flops 20000000 | bytes 200000 | tf_op jit(solution)/shard_map/pallas_call | solution.py:983
  95.6 7.8 %shard_map.241 = (f32[256,768]{1,0:T(8,128)}, bf16[256,384]{1,0:T(8,128)(2,1)}, f32[3,256,256]{2,1,0:T(8,128)}, f32[3,256,256]{2,1,0:T(8,128)}, bf16[64,1536]{1,...) custom-call(s32[34]{0:T(128)} %concatenate.48.places, ...), custom_call_target="tpu_custom_call" | custom-call | flops 9000000 | bytes 90000 | tf_op jit(solution)/shard_map/pallas_call | solution.py:983
  104.5 1.5 collective-permute-start.20
  108.8 2.8 collective-permute-done.19
  111.6 3.2 collective-permute-done.20
  116.1 5.1 %collective-permute-done.22.refs_5_.refs_2_ = bf16[192,768]{1,0:T(8,128)(2,1)S(1)} collective-permute-done((bf16[192,768]{1,0:T(8,128)(2,1)S(1)}, bf16[192,768]{1,0:T(8,128)(2,1)S(1)}, u32[]{:S(2)}, u32[]{:S(2)}) %collective-permute-start.22) | collective-permute-done | bytes 294944 | tf_op jit(solution)/shard_map/ppermute | solution.py:998
  121.8 1.9 collective-permute-start.26
  124.3 13.3 %all-gather.1 = bf16[256,1536]{1,0:T(8,128)(2,1)} all-gather(bf16[64,1536]{1,0:T(8,128)(2,1)S(1)} %multiply_convert_fusion), channel_id=3, replica_groups=mesh['fsdp'=2,'ctx'=4,'tp'=4] {'tp'}, dimensions={0}, use_global_device_ids=true | all-gather | bytes 983040 | tf_op jit(solution)/shard_map/all_gather | solution.py:1002
  138.5 2.2 collective-permute-done.26.refs_3_.refs_1_
  142.7 13.6 %all-gather.2 = bf16[256,1536]{1,0:T(8,128)(2,1)} all-gather(bf16[64,1536]{1,0:T(8,128)(2,1)S(1)} %collective-permute-done.24), channel_id=4, replica_groups=mesh['fsdp'=2,'ctx'=4,'tp'=4] {'tp'}, dimensions={0}, use_global_device_ids=true | all-gather | bytes 983040 | tf_op jit(solution)/shard_map/all_gather | solution.py:1002
  157.3 10.5 %shard_map.242 = (bf16[64,1536]{1,0:T(8,128)(2,1)}, bf16[64,1536]{1,0:T(8,128)(2,1)}, bf16[64,1536]{1,0:T(8,128)(2,1)}, bf16[64,1536]{1,0:T(8,128)(2,1)}, bf16[6...) custom-call(s32[34]{0:T(128)} %concatenate.48.places, ...), custom_call_target="tpu_custom_call" | custom-call | flops 12000000 | bytes 120000 | tf_op jit(solution)/shard_map/pallas_call | solution.py:983
  170.1 1.5 collective-permute-start.38
  171.6 7.5 %shard_map.243 = (bf16[2,64,1536]{2,1,0:T(8,128)(2,1)}, bf16[2,64,1536]{2,1,0:T(8,128)(2,1)}, bf16[2,64,1536]{2,1,0:T(8,128)(2,1)}, bf16[2,64,1536]{2,1,0:T(8,12...) custom-call(s32[34]{0:T(128)} %concatenate.48.places, ...), custom_call_target="tpu_custom_call" | custom-call | flops 4000000 | bytes 40000 | tf_op jit(solution)/shard_map/pallas_call | solution.py:983
  179.1 1.2 collective-permute-done.37
  180.5 1.2 collective-permute-start.39
  182.6 1.5 collective-permute-start.41
  184.1 1.3 collective-permute-start.42
  186.5 6.9 %shard_map.244 = (bf16[2,192,768]{2,1,0:T(8,128)(2,1)}, bf16[2,192,768]{2,1,0:T(8,128)(2,1)}, bf16[2,192,768]{2,1,0:T(8,128)(2,1)}, bf16[2,192,768]{2,1,0:T(8,128)(2,1)}) custom-call(s32[34]{0:T(128)} %concatenate.48.places, bf16[512,1536]{1,0:T(8,128)(2,1)} %get-tuple-element.313.refs_0_, bf16[512,1536]{1,0:T(8,128)(2,1)} %get-tuple-element.293.refs_14_.refs_1_, ...), custom_call_target="tpu_custom_call" | custom-call | flops 3840000 | bytes 38400 | tf_op jit(solution)/shard_map/pallas_call | solution.py:983
  195.9 12.3 %all-gather.3 = bf16[256,1536]{1,0:T(8,128)(2,1)} all-gather(bf16[64,1536]{1,0:T(8,128)(2,1)S(1)} %get-tuple-element.330), channel_id=5, replica_groups=mesh['fsdp'=2,'ctx'=4,'tp'=4] {'tp'}, dimensions={0}, use_global_device_ids=true | all-gather | bytes 983040 | tf_op jit(solution)/shard_map/all_gather | solution.py:1002
  208.2 2.9 collective-permute-done.44
  211.9 1.2 collective-permute-start.47
  213.9 1.5 collective-permute-start.49
  215.4 14.2 %shard_map.245 = (bf16[256,3584]{1,0:T(8,128)(2,1)}, bf16[256,3584]{1,0:T(8,128)(2,1)}, bf16[4,64,1536]{2,1,0:T(8,128)(2,1)}) custom-call(s32[34]{0:T(128)} %concatenate.48.places, bf16[192,2048]{1,0:T(8,128)(2,1)} %shard_map.238.refs_0_, bf16[192,2048]{1,0:T(8,128)(2,1)} %copy-done.3, bf16[192,2048]{1,0:T(8,128)(2,1)} %copy-done.4, ...), custom_call_target="tpu_custom_call" | custom-call | flops 14000000 | bytes 140000 | tf_op jit(solution)/shard_map/pallas_call | solution.py:983
  229.6 2.4 collective-permute-done.45
  233.3 2.3 shard_map.246
  236.4 1.3 copy-done.2
  237.7 4.6 %shard_map.247 = (bf16[2,192,1152]{2,1,0:T(8,128)(2,1)}, bf16[2,192,1152]{2,1,0:T(8,128)(2,1)}) custom-call(s32[34]{0:T(128)} %concatenate.48.places, bf16[256,3584]{1,0:T(8,128)(2,1)} %get-tuple-element.375.refs_0_, bf16[256,3584]{1,0:T(8,128)(2,1)} %copy-done.2), custom_call_target="tpu_custom_call" | custom-call | flops 2880000 | bytes 28800 | tf_op jit(solution)/shard_map/pallas_call | solution.py:983
  242.5 4.2 %shard_map.248 = (bf16[2,192,896]{2,1,0:T(8,128)(2,1)}, bf16[2,192,896]{2,1,0:T(8,128)(2,1)}) custom-call(s32[34]{0:T(128)} %concatenate.48.places, bf16[256,3584]{1,0:T(8,128)(2,1)} %get-tuple-element.375.refs_0_, bf16[256,3584]{1,0:T(8,128)(2,1)} %copy-done.2), custom_call_target="tpu_custom_call" | custom-call | flops 2240000 | bytes 22400 | tf_op jit(solution)/shard_map/pallas_call | solution.py:983
  246.7 4.5 %all-to-all-start = ((bf16[4,64,1536]{2,1,0:T(8,128)(2,1)}), bf16[4,64,1536]{2,1,0:T(8,128)(2,1)}, u32[]{:S(2)}, u32[]{:S(2)}) async-start(bf16[4,64,1536]{2,1,0:T(8,128)(2,1)} %get-tuple-element.380), calls=%async_computation | async-start | bytes 1572864 | tf_op jit(solution)/shard_map/all_to_all | solution.py:1310
  251.9 2.7 collective-permute-start.55
  255.2 1.4 collective-permute-start.53
  256.6 2.4 collective-permute-start.54
  259.0 3.1 all-to-all-done.d_parts
  262.1 2.3 shard_map.249
  264.4 9.0 %collective-permute-done.51 = bf16[2,192,1152]{2,1,0:T(8,128)(2,1)} collective-permute-done((bf16[2,192,1152]{2,1,0:T(8,128)(2,1)}, bf16[2,192,1152]{2,1,0:T(8,128)(2,1)}, u32[]{:S(2)}, u32[]{:S(2)}) %collective-permute-start.51) | collective-permute-done | bytes 884768 | tf_op jit(solution)/shard_map/ppermute | solution.py:998
  273.5 1.3 convert_add_fusion
  274.9 2.9 collective-permute-done.54
  277.8 2.0 collective-permute-start.58
  279.8 2.4 collective-permute-start.59
  282.2 2.0 collective-permute-start.56
  287.6 6.3 %collective-permute-done.58 = bf16[16,1792]{1,0:T(8,128)(2,1)S(1)} collective-permute-done((bf16[16,1792]{1,0:T(8,128)(2,1)S(1)}, bf16[16,1792]{1,0:T(8,128)(2,1)S(1)}, u32[]{:S(2)}, u32[]{:S(2)}) %collective-permute-start.58) | collective-permute-done | bytes 57376 | tf_op jit(solution)/shard_map/ppermute | solution.py:998
  294.0 11.5 %all-gather.4 = bf16[256,1792]{1,0:T(8,128)(2,1)} all-gather(bf16[64,1792]{1,0:T(8,128)(2,1)S(1)} %fusion.7), channel_id=6, replica_groups=mesh['fsdp'=2,'ctx'=4,'tp'=4] {'tp'}, dimensions={0}, use_global_device_ids=true | all-gather | bytes 1146880 | tf_op jit(solution)/shard_map/all_gather | solution.py:1002
  305.5 2.1 shard_map.250
  311.0 2.7 collective-permute-start.62
  313.7 12.7 %all-gather.5 = bf16[256,1536]{1,0:T(8,128)(2,1)} all-gather(bf16[64,1536]{1,0:T(8,128)(2,1)S(1)} %pad_maximum_fusion.7), channel_id=7, replica_groups=mesh['fsdp'=2,'ctx'=4,'tp'=4] {'tp'}, dimensions={0}, use_global_device_ids=true | all-gather | bytes 983040 | tf_op jit(solution)/shard_map/all_gather | solution.py:1002
  326.4 2.1 shard_map.251
  (311 shorter events, 41.3 us)
Async XLA Ops:
  3.9 9.3 %collective-permute-start = (bf16[16,2176]{1,0:T(8,128)(2,1)}, bf16[16,2176]{1,0:T(8,128)(2,1)S(1)}, u32[]{:S(2)}, u32[]{:S(2)}) collective-permute-start(bf16[16,2176]{1,0:T(8,128)(2,1)} %get-tuple-element.215), channel_id=1, source_target_pairs={{0,4},{4,0},{8,12},{12,8},{1,5},{5,1},{9,13},{13,9},{2,6},{6,2},{1... | collective-permute-start | bytes 208904 | tf_op jit(solution)/shard_map/ppermute | solution.py:998
  7.0 7.7 %collective-permute-start.1 = (bf16[16,2176]{1,0:T(8,128)(2,1)}, bf16[16,2176]{1,0:T(8,128)(2,1)S(1)}, u32[]{:S(2)}, u32[]{:S(2)}) collective-permute-start(bf16[16,2176]{1,0:T(8,128)(2,1)} %get-tuple-element.216), channel_id=1, source_target_pairs={{0,8},{4,12},{8,0},{12,4},{1,9},{5,13},{9,1},{13,5},{2,10},{6,14},... | collective-permute-start | bytes 208904 | tf_op jit(solution)/shard_map/ppermute | solution.py:998
  9.6 6.4 %collective-permute-start.2 = (bf16[16,2176]{1,0:T(8,128)(2,1)}, bf16[16,2176]{1,0:T(8,128)(2,1)S(1)}, u32[]{:S(2)}, u32[]{:S(2)}) collective-permute-start(bf16[16,2176]{1,0:T(8,128)(2,1)} %get-tuple-element.217), channel_id=1, source_target_pairs={{0,12},{4,8},{8,4},{12,0},{1,13},{5,9},{9,5},{13,1},{2,14},{6,10},... | collective-permute-start | bytes 208904 | tf_op jit(solution)/shard_map/ppermute | solution.py:998
  16.2 34.6 %collective-permute-start.4 = (bf16[192,2048]{1,0:T(8,128)(2,1)}, bf16[192,2048]{1,0:T(8,128)(2,1)S(1)}, u32[]{:S(2)}, u32[]{:S(2)}) collective-permute-start(bf16[192,2048]{1,0:T(8,128)(2,1)} %shard_map.238.refs_0_), channel_id=1, source_target_pairs={{0,4},{4,0},{8,12},{12,8},{1,5},{5,1},{9,13},{13,9},{2,6},{6,2},{1... | collective-permute-start | bytes 2359304 | tf_op jit(solution)/shard_map/ppermute | solution.py:998
  17.0 33.8 %collective-permute-start.3 = (bf16[192,2048]{1,0:T(8,128)(2,1)}, bf16[192,2048]{1,0:T(8,128)(2,1)S(1)}, u32[]{:S(2)}, u32[]{:S(2)}) collective-permute-start(bf16[192,2048]{1,0:T(8,128)(2,1)} %shard_map.238.refs_0_), channel_id=1, source_target_pairs={{0,8},{4,12},{8,0},{12,4},{1,9},{5,13},{9,1},{13,5},{2,10},{6,14},... | collective-permute-start | bytes 2359304 | tf_op jit(solution)/shard_map/ppermute | solution.py:998
  50.8 25.0 %collective-permute-start.5 = (bf16[192,2048]{1,0:T(8,128)(2,1)S(1)}, bf16[192,2048]{1,0:T(8,128)(2,1)S(1)}, u32[]{:S(2)}, u32[]{:S(2)}) collective-permute-start(bf16[192,2048]{1,0:T(8,128)(2,1)S(1)} %collective-permute-done.3.refs_2_), channel_id=1, source_target_pairs={{0,4},{4,0},{8,12},{12,8},{1,5},{5,1},{9,13},{13,9},{2,6},{6,2},{1... | collective-permute-start | bytes 2359304 | tf_op jit(solution)/shard_map/ppermute | solution.py:998
  53.7 4.4 %collective-permute-start.6 = (bf16[4,384]{1,0:T(4,128)(2,1)S(1)}, bf16[4,384]{1,0:T(4,128)(2,1)S(1)}, u32[]{:S(2)}, u32[]{:S(2)}) collective-permute-start(bf16[4,384]{1,0:T(4,128)(2,1)S(1)} %pad_maximum_fusion.9), channel_id=1, source_target_pairs={{0,16},{16,0},{1,17},{17,1},{2,18},{18,2},{3,19},{19,3},{4,20},{20... | collective-permute-start | bytes 9224 | tf_op jit(solution)/shard_map/ppermute | solution.py:998
  53.7 20.2 %collective-permute-start.7 = (bf16[2,16,1536]{2,1,0:T(8,128)(2,1)}, bf16[2,16,1536]{2,1,0:T(8,128)(2,1)S(1)}, u32[]{:S(2)}, u32[]{:S(2)}) collective-permute-start(bf16[2,16,1536]{2,1,0:T(8,128)(2,1)} %get-tuple-element.237), channel_id=1, source_target_pairs={{0,4},{4,0},{8,12},{12,8},{1,5},{5,1},{9,13},{13,9},{2,6},{6,2},{1... | collective-permute-start | bytes 294920 | tf_op jit(solution)/shard_map/ppermute | solution.py:998
  53.9 20.0 %collective-permute-start.8 = (bf16[2,16,1536]{2,1,0:T(8,128)(2,1)}, bf16[2,16,1536]{2,1,0:T(8,128)(2,1)S(1)}, u32[]{:S(2)}, u32[]{:S(2)}) collective-permute-start(bf16[2,16,1536]{2,1,0:T(8,128)(2,1)} %get-tuple-element.238), channel_id=1, source_target_pairs={{0,8},{4,12},{8,0},{12,4},{1,9},{5,13},{9,1},{13,5},{2,10},{6,14},... | collective-permute-start | bytes 294920 | tf_op jit(solution)/shard_map/ppermute | solution.py:998
  56.2 19.6 %collective-permute-start.9 = (bf16[2,16,1536]{2,1,0:T(8,128)(2,1)}, bf16[2,16,1536]{2,1,0:T(8,128)(2,1)S(1)}, u32[]{:S(2)}, u32[]{:S(2)}) collective-permute-start(bf16[2,16,1536]{2,1,0:T(8,128)(2,1)} %get-tuple-element.239), channel_id=1, source_target_pairs={{0,12},{4,8},{8,4},{12,0},{1,13},{5,9},{9,5},{13,1},{2,14},{6,10},... | collective-permute-start | bytes 294920 | tf_op jit(solution)/shard_map/ppermute | solution.py:998
  75.9 3.8 %collective-permute-start.11 = (bf16[192,2048]{1,0:T(8,128)(2,1)S(1)}, bf16[192,2048]{1,0:T(8,128)(2,1)S(1)}, u32[]{:S(2)}, u32[]{:S(2)}) collective-permute-start(bf16[192,2048]{1,0:T(8,128)(2,1)S(1)} %copy-done), channel_id=1, source_target_pairs={{0,16},{16,0},{1,17},{17,1},{2,18},{18,2},{3,19},{19,3},{4,20},{20... | collective-permute-start | bytes 2359304 | tf_op jit(solution)/shard_map/ppermute | solution.py:998
  76.0 4.2 %collective-permute-start.12 = (bf16[192,2048]{1,0:T(8,128)(2,1)S(1)}, bf16[192,2048]{1,0:T(8,128)(2,1)S(1)}, u32[]{:S(2)}, u32[]{:S(2)}) collective-permute-start(bf16[192,2048]{1,0:T(8,128)(2,1)S(1)} %collective-permute-done.4.refs_1_), channel_id=1, source_target_pairs={{0,16},{16,0},{1,17},{17,1},{2,18},{18,2},{3,19},{19,3},{4,20},{20... | collective-permute-start | bytes 2359304 | tf_op jit(solution)/shard_map/ppermute | solution.py:998
  76.5 4.8 %collective-permute-start.13 = (bf16[192,2048]{1,0:T(8,128)(2,1)S(1)}, bf16[192,2048]{1,0:T(8,128)(2,1)S(1)}, u32[]{:S(2)}, u32[]{:S(2)}) collective-permute-start(bf16[192,2048]{1,0:T(8,128)(2,1)S(1)} %collective-permute-done.3.refs_2_), channel_id=1, source_target_pairs={{0,16},{16,0},{1,17},{17,1},{2,18},{18,2},{3,19},{19,3},{4,20},{20... | collective-permute-start | bytes 2359304 | tf_op jit(solution)/shard_map/ppermute | solution.py:998
  76.6 5.4 %collective-permute-start.14 = (bf16[192,2048]{1,0:T(8,128)(2,1)S(1)}, bf16[192,2048]{1,0:T(8,128)(2,1)S(1)}, u32[]{:S(2)}, u32[]{:S(2)}) collective-permute-start(bf16[192,2048]{1,0:T(8,128)(2,1)S(1)} %collective-permute-done.5.refs_3_), channel_id=1, source_target_pairs={{0,16},{16,0},{1,17},{17,1},{2,18},{18,2},{3,19},{19,3},{4,20},{20... | collective-permute-start | bytes 2359304 | tf_op jit(solution)/shard_map/ppermute | solution.py:998
  77.2 26.3 %collective-permute-start.18 = (bf16[2,64,1536]{2,1,0:T(8,128)(2,1)S(1)}, bf16[2,64,1536]{2,1,0:T(8,128)(2,1)}, u32[]{:S(2)}, u32[]{:S(2)}) collective-permute-start(bf16[2,64,1536]{2,1,0:T(8,128)(2,1)S(1)} %pad_maximum_fusion.4.refs_18_.refs_10_), channel_id=1, source_target_pairs={{0,3},{1,2},{2,1},{3,0},{4,7},{5,6},{6,5},{7,4},{8,11},{9,10},{10,... | collective-permute-start | bytes 1179656 | tf_op jit(solution)/shard_map/ppermute | solution.py:998
  79.7 23.8 %collective-permute-start.17 = (bf16[2,64,1536]{2,1,0:T(8,128)(2,1)S(1)}, bf16[2,64,1536]{2,1,0:T(8,128)(2,1)S(1)}, u32[]{:S(2)}, u32[]{:S(2)}) collective-permute-start(bf16[2,64,1536]{2,1,0:T(8,128)(2,1)S(1)} %pad_maximum_fusion.4.refs_18_.refs_10_), channel_id=1, source_target_pairs={{0,2},{1,3},{2,0},{3,1},{4,6},{5,7},{6,4},{7,5},{8,10},{9,11},{10,... | collective-permute-start | bytes 1179656 | tf_op jit(solution)/shard_map/ppermute | solution.py:998
  80.2 23.3 %collective-permute-start.16 = (bf16[2,64,1536]{2,1,0:T(8,128)(2,1)S(1)}, bf16[2,64,1536]{2,1,0:T(8,128)(2,1)S(1)}, u32[]{:S(2)}, u32[]{:S(2)}) collective-permute-start(bf16[2,64,1536]{2,1,0:T(8,128)(2,1)S(1)} %pad_maximum_fusion.4.refs_18_.refs_10_), channel_id=1, source_target_pairs={{0,1},{1,0},{2,3},{3,2},{4,5},{5,4},{6,7},{7,6},{8,9},{9,8},{10,11... | collective-permute-start | bytes 1179656 | tf_op jit(solution)/shard_map/ppermute | solution.py:998
  81.3 22.1 %collective-permute-start.10 = (bf16[192,768]{1,0:T(8,128)(2,1)}, bf16[192,768]{1,0:T(8,128)(2,1)}, u32[]{:S(2)}, u32[]{:S(2)}) collective-permute-start(bf16[192,768]{1,0:T(8,128)(2,1)} %get-tuple-element.246), channel_id=1, source_target_pairs={{0,8},{4,12},{8,0},{12,4},{1,9},{5,13},{9,1},{13,5},{2,10},{6,14},... | collective-permute-start | bytes 884744 | tf_op jit(solution)/shard_map/ppermute | solution.py:998
  83.0 20.4 %collective-permute-start.15 = (bf16[192,768]{1,0:T(8,128)(2,1)}, bf16[192,768]{1,0:T(8,128)(2,1)}, u32[]{:S(2)}, u32[]{:S(2)}) collective-permute-start(bf16[192,768]{1,0:T(8,128)(2,1)} %get-tuple-element.274.refs_0_), channel_id=1, source_target_pairs={{0,4},{4,0},{8,12},{12,8},{1,5},{5,1},{9,13},{13,9},{2,6},{6,2},{1... | collective-permute-start | bytes 884744 | tf_op jit(solution)/shard_map/ppermute | solution.py:998
  103.5 8.1 %collective-permute-start.19 = (bf16[64,1536]{1,0:T(8,128)(2,1)}, bf16[64,1536]{1,0:T(8,128)(2,1)S(1)}, u32[]{:S(2)}, u32[]{:S(2)}) collective-permute-start(bf16[64,1536]{1,0:T(8,128)(2,1)} %get-tuple-element.267), channel_id=1, source_target_pairs={{0,1},{1,0},{2,3},{3,2},{4,5},{5,4},{6,7},{7,6},{8,9},{9,8},{10,11... | collective-permute-start | bytes 589832 | tf_op jit(solution)/shard_map/ppermute | solution.py:998
  104.5 10.3 %collective-permute-start.20 = (bf16[64,1536]{1,0:T(8,128)(2,1)}, bf16[64,1536]{1,0:T(8,128)(2,1)S(1)}, u32[]{:S(2)}, u32[]{:S(2)}) collective-permute-start(bf16[64,1536]{1,0:T(8,128)(2,1)} %get-tuple-element.268), channel_id=1, source_target_pairs={{0,2},{1,3},{2,0},{3,1},{4,6},{5,7},{6,4},{7,5},{8,10},{9,11},{10,... | collective-permute-start | bytes 589832 | tf_op jit(solution)/shard_map/ppermute | solution.py:998
  106.0 8.8 %collective-permute-start.21 = (bf16[64,1536]{1,0:T(8,128)(2,1)}, bf16[64,1536]{1,0:T(8,128)(2,1)S(1)}, u32[]{:S(2)}, u32[]{:S(2)}) collective-permute-start(bf16[64,1536]{1,0:T(8,128)(2,1)} %get-tuple-element.269), channel_id=1, source_target_pairs={{0,3},{1,2},{2,1},{3,0},{4,7},{5,6},{6,5},{7,4},{8,11},{9,10},{10,... | collective-permute-start | bytes 589832 | tf_op jit(solution)/shard_map/ppermute | solution.py:998
  107.1 14.1 %collective-permute-start.22 = (bf16[192,768]{1,0:T(8,128)(2,1)S(1)}, bf16[192,768]{1,0:T(8,128)(2,1)S(1)}, u32[]{:S(2)}, u32[]{:S(2)}) collective-permute-start(bf16[192,768]{1,0:T(8,128)(2,1)S(1)} %copy-done.66), channel_id=1, source_target_pairs={{0,8},{4,12},{8,0},{12,4},{1,9},{5,13},{9,1},{13,5},{2,10},{6,14},... | collective-permute-start | bytes 884744 | tf_op jit(solution)/shard_map/ppermute | solution.py:998
  107.9 13.7 %collective-permute-start.23 = (bf16[192,768]{1,0:T(8,128)(2,1)}, bf16[192,768]{1,0:T(8,128)(2,1)S(1)}, u32[]{:S(2)}, u32[]{:S(2)}) collective-permute-start(bf16[192,768]{1,0:T(8,128)(2,1)} %collective-permute-done.10.refs_4_), channel_id=1, source_target_pairs={{0,4},{4,0},{8,12},{12,8},{1,5},{5,1},{9,13},{13,9},{2,6},{6,2},{1... | collective-permute-start | bytes 884744 | tf_op jit(solution)/shard_map/ppermute | solution.py:998
  121.6 16.9 %collective-permute-start.25 = (bf16[192,768]{1,0:T(8,128)(2,1)S(1)}, bf16[192,768]{1,0:T(8,128)(2,1)S(1)}, u32[]{:S(2)}, u32[]{:S(2)}) collective-permute-start(bf16[192,768]{1,0:T(8,128)(2,1)S(1)} %collective-permute-done.22.refs_5_.refs_2_), channel_id=1, source_target_pairs={{0,4},{4,0},{8,12},{12,8},{1,5},{5,1},{9,13},{13,9},{2,6},{6,2},{1... | collective-permute-start | bytes 884744 | tf_op jit(solution)/shard_map/ppermute | solution.py:998
  121.8 19.0 %collective-permute-start.26 = (bf16[192,768]{1,0:T(8,128)(2,1)S(1)}, bf16[192,768]{1,0:T(8,128)(2,1)S(1)}, u32[]{:S(2)}, u32[]{:S(2)}) collective-permute-start(bf16[192,768]{1,0:T(8,128)(2,1)S(1)} %copy-done.16), channel_id=1, source_target_pairs={{0,4},{4,0},{8,12},{12,8},{1,5},{5,1},{9,13},{13,9},{2,6},{6,2},{1... | collective-permute-start | bytes 884744 | tf_op jit(solution)/shard_map/ppermute | solution.py:998
  123.7 14.9 %collective-permute-start.24 = (bf16[64,1536]{1,0:T(8,128)(2,1)S(1)}, bf16[64,1536]{1,0:T(8,128)(2,1)S(1)}, u32[]{:S(2)}, u32[]{:S(2)}) collective-permute-start(bf16[64,1536]{1,0:T(8,128)(2,1)S(1)} %multiply_convert_fusion), channel_id=1, source_target_pairs={{0,8},{4,12},{8,0},{12,4},{1,9},{5,13},{9,1},{13,5},{2,10},{6,14},... | collective-permute-start | bytes 589832 | tf_op jit(solution)/shard_map/ppermute | solution.py:998
  123.8 18.0 %collective-permute-start.28 = (bf16[192,768]{1,0:T(8,128)(2,1)S(1)}, bf16[192,768]{1,0:T(8,128)(2,1)S(1)}, u32[]{:S(2)}, u32[]{:S(2)}) collective-permute-start(bf16[192,768]{1,0:T(8,128)(2,1)S(1)} %copy-done.16), channel_id=1, source_target_pairs={{0,16},{16,0},{1,17},{17,1},{2,18},{18,2},{3,19},{19,3},{4,20},{20... | collective-permute-start | bytes 884744 | tf_op jit(solution)/shard_map/ppermute | solution.py:998
  123.8 17.4 %collective-permute-start.27 = (bf16[192,768]{1,0:T(8,128)(2,1)S(1)}, bf16[192,768]{1,0:T(8,128)(2,1)S(1)}, u32[]{:S(2)}, u32[]{:S(2)}) collective-permute-start(bf16[192,768]{1,0:T(8,128)(2,1)S(1)} %copy-done.47), channel_id=1, source_target_pairs={{0,16},{16,0},{1,17},{17,1},{2,18},{18,2},{3,19},{19,3},{4,20},{20... | collective-permute-start | bytes 884744 | tf_op jit(solution)/shard_map/ppermute | solution.py:998
  140.7 1.8 collective-permute-start.29
  140.7 15.5 %collective-permute-start.31 = (bf16[192,768]{1,0:T(8,128)(2,1)}, bf16[192,768]{1,0:T(8,128)(2,1)S(1)}, u32[]{:S(2)}, u32[]{:S(2)}) collective-permute-start(bf16[192,768]{1,0:T(8,128)(2,1)} %collective-permute-done.10.refs_4_), channel_id=1, source_target_pairs={{0,16},{16,0},{1,17},{17,1},{2,18},{18,2},{3,19},{19,3},{4,20},{20... | collective-permute-start | bytes 884744 | tf_op jit(solution)/shard_map/ppermute | solution.py:998
  141.2 15.0 %collective-permute-start.33 = (bf16[192,768]{1,0:T(8,128)(2,1)S(1)}, bf16[192,768]{1,0:T(8,128)(2,1)S(1)}, u32[]{:S(2)}, u32[]{:S(2)}) collective-permute-start(bf16[192,768]{1,0:T(8,128)(2,1)S(1)} %collective-permute-done.23.refs_6_), channel_id=1, source_target_pairs={{0,16},{16,0},{1,17},{17,1},{2,18},{18,2},{3,19},{19,3},{4,20},{20... | collective-permute-start | bytes 884744 | tf_op jit(solution)/shard_map/ppermute | solution.py:998
  141.3 15.0 %collective-permute-start.30 = (bf16[192,768]{1,0:T(8,128)(2,1)S(1)}, bf16[192,768]{1,0:T(8,128)(2,1)S(1)}, u32[]{:S(2)}, u32[]{:S(2)}) collective-permute-start(bf16[192,768]{1,0:T(8,128)(2,1)S(1)} %collective-permute-done.26.refs_3_.refs_1_), channel_id=1, source_target_pairs={{0,16},{16,0},{1,17},{17,1},{2,18},{18,2},{3,19},{19,3},{4,20},{20... | collective-permute-start | bytes 884744 | tf_op jit(solution)/shard_map/ppermute | solution.py:998
  141.8 14.5 %collective-permute-start.32 = (bf16[192,768]{1,0:T(8,128)(2,1)S(1)}, bf16[192,768]{1,0:T(8,128)(2,1)S(1)}, u32[]{:S(2)}, u32[]{:S(2)}) collective-permute-start(bf16[192,768]{1,0:T(8,128)(2,1)S(1)} %collective-permute-done.22.refs_5_.refs_2_), channel_id=1, source_target_pairs={{0,16},{16,0},{1,17},{17,1},{2,18},{18,2},{3,19},{19,3},{4,20},{20... | collective-permute-start | bytes 884744 | tf_op jit(solution)/shard_map/ppermute | solution.py:998
  142.5 13.8 %collective-permute-start.34 = (bf16[192,768]{1,0:T(8,128)(2,1)S(1)}, bf16[192,768]{1,0:T(8,128)(2,1)S(1)}, u32[]{:S(2)}, u32[]{:S(2)}) collective-permute-start(bf16[192,768]{1,0:T(8,128)(2,1)S(1)} %collective-permute-done.25.refs_7_.refs_3_), channel_id=1, source_target_pairs={{0,16},{16,0},{1,17},{17,1},{2,18},{18,2},{3,19},{19,3},{4,20},{20... | collective-permute-start | bytes 884744 | tf_op jit(solution)/shard_map/ppermute | solution.py:998
  167.9 12.5 %collective-permute-start.35 = (bf16[512,1536]{1,0:T(8,128)(2,1)}, bf16[512,1536]{1,0:T(8,128)(2,1)S(1)}, u32[]{:S(2)}, u32[]{:S(2)}) collective-permute-start(bf16[512,1536]{1,0:T(8,128)(2,1)} %get-tuple-element.293.refs_14_.refs_1_), channel_id=1, source_target_pairs={{0,16},{16,0},{1,17},{17,1},{2,18},{18,2},{3,19},{19,3},{4,20},{20... | collective-permute-start | bytes 4718600 | tf_op jit(solution)/shard_map/ppermute | solution.py:998
  168.0 11.1 %collective-permute-start.36 = (bf16[64,1536]{1,0:T(8,128)(2,1)}, bf16[64,1536]{1,0:T(8,128)(2,1)S(1)}, u32[]{:S(2)}, u32[]{:S(2)}) collective-permute-start(bf16[64,1536]{1,0:T(8,128)(2,1)} %get-tuple-element.295), channel_id=1, source_target_pairs={{0,1},{1,0},{2,3},{3,2},{4,5},{5,4},{6,7},{7,6},{8,9},{9,8},{10,11... | collective-permute-start | bytes 589832 | tf_op jit(solution)/shard_map/ppermute | solution.py:998
  168.9 11.4 %collective-permute-start.37 = (bf16[64,1536]{1,0:T(8,128)(2,1)}, bf16[64,1536]{1,0:T(8,128)(2,1)S(1)}, u32[]{:S(2)}, u32[]{:S(2)}) collective-permute-start(bf16[64,1536]{1,0:T(8,128)(2,1)} %get-tuple-element.296), channel_id=1, source_target_pairs={{0,2},{1,3},{2,0},{3,1},{4,6},{5,7},{6,4},{7,5},{8,10},{9,11},{10,... | collective-permute-start | bytes 589832 | tf_op jit(solution)/shard_map/ppermute | solution.py:998
  170.1 10.2 %collective-permute-start.38 = (bf16[64,1536]{1,0:T(8,128)(2,1)}, bf16[64,1536]{1,0:T(8,128)(2,1)S(1)}, u32[]{:S(2)}, u32[]{:S(2)}) collective-permute-start(bf16[64,1536]{1,0:T(8,128)(2,1)} %get-tuple-element.297), channel_id=1, source_target_pairs={{0,3},{1,2},{2,1},{3,0},{4,7},{5,6},{6,5},{7,4},{8,11},{9,10},{10,... | collective-permute-start | bytes 589832 | tf_op jit(solution)/shard_map/ppermute | solution.py:998
  180.4 4.9 %collective-permute-start.43 = (bf16[512,1536]{1,0:T(8,128)(2,1)}, bf16[512,1536]{1,0:T(8,128)(2,1)S(1)}, u32[]{:S(2)}, u32[]{:S(2)}) collective-permute-start(bf16[512,1536]{1,0:T(8,128)(2,1)} %get-tuple-element.314), channel_id=1, source_target_pairs={{0,16},{16,0},{1,17},{17,1},{2,18},{18,2},{3,19},{19,3},{4,20},{20... | collective-permute-start | bytes 4718600 | tf_op jit(solution)/shard_map/ppermute | solution.py:998
  180.5 12.9 %collective-permute-start.39 = (bf16[64,1536]{1,0:T(8,128)(2,1)S(1)}, bf16[64,1536]{1,0:T(8,128)(2,1)S(1)}, u32[]{:S(2)}, u32[]{:S(2)}) collective-permute-start(bf16[64,1536]{1,0:T(8,128)(2,1)S(1)} %copy-done.69), channel_id=1, source_target_pairs={{0,1},{1,0},{2,3},{3,2},{4,5},{5,4},{6,7},{7,6},{8,9},{9,8},{10,11... | collective-permute-start | bytes 589832 | tf_op jit(solution)/shard_map/ppermute | solution.py:998
  181.8 11.7 %collective-permute-start.40 = (bf16[64,1536]{1,0:T(8,128)(2,1)S(1)}, bf16[64,1536]{1,0:T(8,128)(2,1)S(1)}, u32[]{:S(2)}, u32[]{:S(2)}) collective-permute-start(bf16[64,1536]{1,0:T(8,128)(2,1)S(1)} %copy-done.68), channel_id=1, source_target_pairs={{0,2},{1,3},{2,0},{3,1},{4,6},{5,7},{6,4},{7,5},{8,10},{9,11},{10,... | collective-permute-start | bytes 589832 | tf_op jit(solution)/shard_map/ppermute | solution.py:998
  182.6 10.8 %collective-permute-start.41 = (bf16[64,1536]{1,0:T(8,128)(2,1)S(1)}, bf16[64,1536]{1,0:T(8,128)(2,1)S(1)}, u32[]{:S(2)}, u32[]{:S(2)}) collective-permute-start(bf16[64,1536]{1,0:T(8,128)(2,1)S(1)} %copy-done.67), channel_id=1, source_target_pairs={{0,3},{1,2},{2,1},{3,0},{4,7},{5,6},{6,5},{7,4},{8,11},{9,10},{10,... | collective-permute-start | bytes 589832 | tf_op jit(solution)/shard_map/ppermute | solution.py:998
  184.1 10.5 %collective-permute-start.42 = (bf16[64,1536]{1,0:T(8,128)(2,1)S(1)}, bf16[64,1536]{1,0:T(8,128)(2,1)S(1)}, u32[]{:S(2)}, u32[]{:S(2)}) collective-permute-start(bf16[64,1536]{1,0:T(8,128)(2,1)S(1)} %add_convert_fusion), channel_id=1, source_target_pairs={{0,8},{4,12},{8,0},{12,4},{1,9},{5,13},{9,1},{13,5},{2,10},{6,14},... | collective-permute-start | bytes 589832 | tf_op jit(solution)/shard_map/ppermute | solution.py:998
  195.9 15.2 %collective-permute-start.44 = (bf16[2,192,768]{2,1,0:T(8,128)(2,1)S(1)}, bf16[2,192,768]{2,1,0:T(8,128)(2,1)S(1)}, u32[]{:S(2)}, u32[]{:S(2)}) collective-permute-start(bf16[2,192,768]{2,1,0:T(8,128)(2,1)S(1)} %copy-done.62), channel_id=1, source_target_pairs={{0,4},{4,0},{8,12},{12,8},{1,5},{5,1},{9,13},{13,9},{2,6},{6,2},{1... | collective-permute-start | bytes 1769480 | tf_op jit(solution)/shard_map/ppermute | solution.py:998
  211.3 20.8 %collective-permute-start.45 = (bf16[2,192,768]{2,1,0:T(8,128)(2,1)S(1)}, bf16[2,192,768]{2,1,0:T(8,128)(2,1)S(1)}, u32[]{:S(2)}, u32[]{:S(2)}) collective-permute-start(bf16[2,192,768]{2,1,0:T(8,128)(2,1)S(1)} %copy-done.61), channel_id=1, source_target_pairs={{0,4},{4,0},{8,12},{12,8},{1,5},{5,1},{9,13},{13,9},{2,6},{6,2},{1... | collective-permute-start | bytes 1769480 | tf_op jit(solution)/shard_map/ppermute | solution.py:998
  211.6 20.6 %collective-permute-start.46 = (bf16[192,768]{1,0:T(8,128)(2,1)S(1)}, bf16[192,768]{1,0:T(8,128)(2,1)S(1)}, u32[]{:S(2)}, u32[]{:S(2)}) collective-permute-start(bf16[192,768]{1,0:T(8,128)(2,1)S(1)} %fusion.5), channel_id=1, source_target_pairs={{0,8},{4,12},{8,0},{12,4},{1,9},{5,13},{9,1},{13,5},{2,10},{6,14},... | collective-permute-start | bytes 884744 | tf_op jit(solution)/shard_map/ppermute | solution.py:998
  211.9 20.4 %collective-permute-start.47 = (bf16[2,64,1536]{2,1,0:T(8,128)(2,1)S(1)}, bf16[2,64,1536]{2,1,0:T(8,128)(2,1)S(1)}, u32[]{:S(2)}, u32[]{:S(2)}) collective-permute-start(bf16[2,64,1536]{2,1,0:T(8,128)(2,1)S(1)} %copy-done.65), channel_id=1, source_target_pairs={{0,1},{1,0},{2,3},{3,2},{4,5},{5,4},{6,7},{7,6},{8,9},{9,8},{10,11... | collective-permute-start | bytes 1179656 | tf_op jit(solution)/shard_map/ppermute | solution.py:998
  213.1 19.2 %collective-permute-start.48 = (bf16[2,64,1536]{2,1,0:T(8,128)(2,1)S(1)}, bf16[2,64,1536]{2,1,0:T(8,128)(2,1)S(1)}, u32[]{:S(2)}, u32[]{:S(2)}) collective-permute-start(bf16[2,64,1536]{2,1,0:T(8,128)(2,1)S(1)} %copy-done.64), channel_id=1, source_target_pairs={{0,2},{1,3},{2,0},{3,1},{4,6},{5,7},{6,4},{7,5},{8,10},{9,11},{10,... | collective-permute-start | bytes 1179656 | tf_op jit(solution)/shard_map/ppermute | solution.py:998
  213.9 18.4 %collective-permute-start.49 = (bf16[2,64,1536]{2,1,0:T(8,128)(2,1)S(1)}, bf16[2,64,1536]{2,1,0:T(8,128)(2,1)S(1)}, u32[]{:S(2)}, u32[]{:S(2)}) collective-permute-start(bf16[2,64,1536]{2,1,0:T(8,128)(2,1)S(1)} %copy-done.63), channel_id=1, source_target_pairs={{0,3},{1,2},{2,1},{3,0},{4,7},{5,6},{6,5},{7,4},{8,11},{9,10},{10,... | collective-permute-start | bytes 1179656 | tf_op jit(solution)/shard_map/ppermute | solution.py:998
  232.3 4.1 %collective-permute-start.50 = (bf16[256,3584]{1,0:T(8,128)(2,1)}, bf16[256,3584]{1,0:T(8,128)(2,1)S(1)}, u32[]{:S(2)}, u32[]{:S(2)}) collective-permute-start(bf16[256,3584]{1,0:T(8,128)(2,1)} %get-tuple-element.352), channel_id=1, source_target_pairs={{0,16},{16,0},{1,17},{17,1},{2,18},{18,2},{3,19},{19,3},{4,20},{20... | collective-permute-start | bytes 5505032 | tf_op jit(solution)/shard_map/ppermute | solution.py:998
  242.2 31.2 %collective-permute-start.51 = (bf16[2,192,1152]{2,1,0:T(8,128)(2,1)}, bf16[2,192,1152]{2,1,0:T(8,128)(2,1)}, u32[]{:S(2)}, u32[]{:S(2)}) collective-permute-start(bf16[2,192,1152]{2,1,0:T(8,128)(2,1)} %get-tuple-element.373), channel_id=1, source_target_pairs={{0,4},{4,0},{8,12},{12,8},{1,5},{5,1},{9,13},{13,9},{2,6},{6,2},{1... | collective-permute-start | bytes 2654216 | tf_op jit(solution)/shard_map/ppermute | solution.py:998
  246.7 15.4 %all-to-all-start = ((bf16[4,64,1536]{2,1,0:T(8,128)(2,1)}), bf16[4,64,1536]{2,1,0:T(8,128)(2,1)}, u32[]{:S(2)}, u32[]{:S(2)}) async-start(bf16[4,64,1536]{2,1,0:T(8,128)(2,1)} %get-tuple-element.380), calls=%async_computation | async-start | bytes 1572864 | tf_op jit(solution)/shard_map/all_to_all | solution.py:1310
  251.9 25.9 %collective-permute-start.55 = (bf16[192,768]{1,0:T(8,128)(2,1)S(1)}, bf16[192,768]{1,0:T(8,128)(2,1)S(1)}, u32[]{:S(2)}, u32[]{:S(2)}) collective-permute-start(bf16[192,768]{1,0:T(8,128)(2,1)S(1)} %fusion.6), channel_id=1, source_target_pairs={{0,8},{4,12},{8,0},{12,4},{1,9},{5,13},{9,1},{13,5},{2,10},{6,14},... | collective-permute-start | bytes 884744 | tf_op jit(solution)/shard_map/ppermute | solution.py:998
  254.6 20.3 %collective-permute-start.52 = (bf16[32,1536]{1,0:T(8,128)(2,1)}, bf16[32,1536]{1,0:T(8,128)(2,1)S(1)}, u32[]{:S(2)}, u32[]{:S(2)}) collective-permute-start(bf16[32,1536]{1,0:T(8,128)(2,1)} %get-tuple-element.386), channel_id=1, source_target_pairs={{0,4},{4,0},{8,12},{12,8},{1,5},{5,1},{9,13},{13,9},{2,6},{6,2},{1... | collective-permute-start | bytes 294920 | tf_op jit(solution)/shard_map/ppermute | solution.py:998
  255.2 19.7 %collective-permute-start.53 = (bf16[32,1536]{1,0:T(8,128)(2,1)}, bf16[32,1536]{1,0:T(8,128)(2,1)S(1)}, u32[]{:S(2)}, u32[]{:S(2)}) collective-permute-start(bf16[32,1536]{1,0:T(8,128)(2,1)} %get-tuple-element.387), channel_id=1, source_target_pairs={{0,8},{4,12},{8,0},{12,4},{1,9},{5,13},{9,1},{13,5},{2,10},{6,14},... | collective-permute-start | bytes 294920 | tf_op jit(solution)/shard_map/ppermute | solution.py:998
  256.6 21.2 %collective-permute-start.54 = (bf16[32,1536]{1,0:T(8,128)(2,1)}, bf16[32,1536]{1,0:T(8,128)(2,1)S(1)}, u32[]{:S(2)}, u32[]{:S(2)}) collective-permute-start(bf16[32,1536]{1,0:T(8,128)(2,1)} %get-tuple-element.388), channel_id=1, source_target_pairs={{0,12},{4,8},{8,4},{12,0},{1,13},{5,9},{9,5},{13,1},{2,14},{6,10},... | collective-permute-start | bytes 294920 | tf_op jit(solution)/shard_map/ppermute | solution.py:998
  277.8 9.8 %collective-permute-start.57 = (bf16[16,1792]{1,0:T(8,128)(2,1)S(1)}, bf16[16,1792]{1,0:T(8,128)(2,1)S(1)}, u32[]{:S(2)}, u32[]{:S(2)}) collective-permute-start(bf16[16,1792]{1,0:T(8,128)(2,1)S(1)} %copy-done.72), channel_id=1, source_target_pairs={{0,4},{4,0},{8,12},{12,8},{1,5},{5,1},{9,13},{13,9},{2,6},{6,2},{1... | collective-permute-start | bytes 172040 | tf_op jit(solution)/shard_map/ppermute | solution.py:998
  277.8 16.0 %collective-permute-start.58 = (bf16[16,1792]{1,0:T(8,128)(2,1)S(1)}, bf16[16,1792]{1,0:T(8,128)(2,1)S(1)}, u32[]{:S(2)}, u32[]{:S(2)}) collective-permute-start(bf16[16,1792]{1,0:T(8,128)(2,1)S(1)} %copy-done.71), channel_id=1, source_target_pairs={{0,8},{4,12},{8,0},{12,4},{1,9},{5,13},{9,1},{13,5},{2,10},{6,14},... | collective-permute-start | bytes 172040 | tf_op jit(solution)/shard_map/ppermute | solution.py:998
  279.8 14.0 %collective-permute-start.59 = (bf16[16,1792]{1,0:T(8,128)(2,1)S(1)}, bf16[16,1792]{1,0:T(8,128)(2,1)S(1)}, u32[]{:S(2)}, u32[]{:S(2)}) collective-permute-start(bf16[16,1792]{1,0:T(8,128)(2,1)S(1)} %copy-done.70), channel_id=1, source_target_pairs={{0,12},{4,8},{8,4},{12,0},{1,13},{5,9},{9,5},{13,1},{2,14},{6,10},... | collective-permute-start | bytes 172040 | tf_op jit(solution)/shard_map/ppermute | solution.py:998
  282.2 26.8 %collective-permute-start.60 = (bf16[192,1152]{1,0:T(8,128)(2,1)S(1)}, bf16[192,1152]{1,0:T(8,128)(2,1)}, u32[]{:S(2)}, u32[]{:S(2)}) collective-permute-start(bf16[192,1152]{1,0:T(8,128)(2,1)S(1)} %fusion.3), channel_id=1, source_target_pairs={{0,8},{4,12},{8,0},{12,4},{1,9},{5,13},{9,1},{13,5},{2,10},{6,14},... | collective-permute-start | bytes 1327112 | tf_op jit(solution)/shard_map/ppermute | solution.py:998
  282.2 26.6 %collective-permute-start.56 = (bf16[2,192,896]{2,1,0:T(8,128)(2,1)}, bf16[2,192,896]{2,1,0:T(8,128)(2,1)S(1)}, u32[]{:S(2)}, u32[]{:S(2)}) collective-permute-start(bf16[2,192,896]{2,1,0:T(8,128)(2,1)} %get-tuple-element.392), channel_id=1, source_target_pairs={{0,4},{4,0},{8,12},{12,8},{1,5},{5,1},{9,13},{13,9},{2,6},{6,2},{1... | collective-permute-start | bytes 2064392 | tf_op jit(solution)/shard_map/ppermute | solution.py:998
  311.0 17.5 %collective-permute-start.61 = (f32[16,256]{1,0:T(8,128)S(1)}, f32[16,256]{1,0:T(8,128)S(1)}, u32[]{:S(2)}, u32[]{:S(2)}) collective-permute-start(f32[16,256]{1,0:T(8,128)S(1)} %copy-done.59), channel_id=1, source_target_pairs={{0,16},{16,0},{1,17},{17,1},{2,18},{18,2},{3,19},{19,3},{4,20},{20... | collective-permute-start | bytes 49160 | tf_op jit(solution)/shard_map/ppermute | solution.py:998
  311.0 18.8 %collective-permute-start.62 = (bf16[192,896]{1,0:T(8,128)(2,1)S(1)}, bf16[192,896]{1,0:T(8,128)(2,1)S(1)}, u32[]{:S(2)}, u32[]{:S(2)}) collective-permute-start(bf16[192,896]{1,0:T(8,128)(2,1)S(1)} %fusion.4), channel_id=1, source_target_pairs={{0,8},{4,12},{8,0},{12,4},{1,9},{5,13},{9,1},{13,5},{2,10},{6,14},... | collective-permute-start | bytes 1032200 | tf_op jit(solution)/shard_map/ppermute | solution.py:998
  (73 other events, 1036.3 us)
